TPU v7x, 32 devices: a whole 2x2x4 slice. The times are simulated.
32 devices in a mesh: groups: 2 (over y), db: 4 (over x, core), cand: 4 (over z).
Axes of the slice: x: 2, y: 2, z: 4, core: 2. Of those that a mesh axis runs over, the one named last changes fastest.
Arguments:
- coords: float32 [3, 128, 64], P(None, ('groups', 'db', 'cand')), parts along dimension 1, may hold values from 0 to 1
- species: int32 [128, 64], P(('groups', 'db', 'cand')), parts along dimension 0, may hold values from 0 to 88
- miller: int32 [3, 4096], replicated, may hold values from -8 to 8
- offsets: int32 [4096], replicated, may hold values from 0 to 1023
- form_amps: float32 [89, 4], replicated, may hold values from 0.5 to 6
- form_decay: float32 [89, 4], replicated, may hold values from 0.2 to 20
- ref_patterns: bfloat16 [65536, 1024], P(('db', 'cand')), may hold values from -6 to 6
Outputs:
- scores: bfloat16 [128, 65536], P('groups', ('db', 'cand')), parts along dimension 0
There are 2 independent parts, one for each index of `groups`. A program takes and returns all parts, laid end to end along the dimension named above; an argument that names none is the same for every part. Nothing has to cross between parts.
All inputs are finite; a program needn't handle non-finite values.
Results may differ from a plain program's by a relative error of at most 0.0071.
Values may be sent and summed in bfloat16 or wider, within the bound.
No kernel may reach another device: no remote copies, remote signals or barrier semaphores. Data moves between devices by JAX's collectives and lax.ppermute only.
A program may use at most 64 MiB of HBM per device.

v0:
```python
import jax
import jax.numpy as jnp
from jax import lax
from jax.sharding import PartitionSpec as P

EPSILON = 1e-06
Q_SCALE = 0.0025
PEAK_WIDTH = 0.5
TWO_PI = 6.283185307179586


def form_table(indices, form_amps, form_decay):
    q_square = (
        indices[0] * indices[0] + indices[1] * indices[1] + indices[2] * indices[2]
    ) * Q_SCALE
    result = jnp.zeros((form_amps.shape[0], indices.shape[1]), jnp.float32)
    for term in range(4):
        result = result + form_amps[:, term : term + 1] * jnp.exp(
            -form_decay[:, term : term + 1] * q_square[None, :]
        )
    return result.astype(jnp.bfloat16)


def structure(atom_coords, atom_species, indices, centres, form_amps, form_decay, nbins):
    count = atom_coords.shape[1]
    atoms = atom_coords.shape[2]
    table = form_table(indices, form_amps, form_decay)
    kinds = jnp.arange(form_amps.shape[0], dtype=jnp.float32)
    onehot = (atom_species.reshape(-1)[:, None] == kinds[None, :]).astype(jnp.bfloat16)
    weights = jnp.dot(onehot, table, preferred_element_type=jnp.float32).reshape(
        count, atoms, indices.shape[1]
    )
    phases = TWO_PI * (
        atom_coords[0][:, :, None] * indices[0][None, None, :]
        + atom_coords[1][:, :, None] * indices[1][None, None, :]
        + atom_coords[2][:, :, None] * indices[2][None, None, :]
    )
    real_part = jnp.sum(weights * jnp.cos(phases), axis=1)
    imag_part = jnp.sum(weights * jnp.sin(phases), axis=1)
    intensity = (real_part * real_part + imag_part * imag_part).astype(jnp.bfloat16)
    bin_grid = jnp.arange(nbins, dtype=jnp.float32)
    distance = (bin_grid[None, :] - centres[:, None]) / PEAK_WIDTH
    profile = jnp.exp(-0.5 * distance * distance).astype(jnp.bfloat16)
    return jnp.dot(intensity, profile, preferred_element_type=jnp.float32)


def standardize(rows):
    row_mean = jnp.mean(rows, axis=1, keepdims=True)
    centered = rows - row_mean
    spread = jnp.sqrt(jnp.mean(centered * centered, axis=1, keepdims=True) + EPSILON)
    return (centered / spread).astype(jnp.bfloat16)


def per_device(coords, species, miller, offsets, form_amps, form_decay, ref_patterns):
    nbins = ref_patterns.shape[1]
    ref_z = standardize(ref_patterns.astype(jnp.float32))
    scale_back = 1.0 / jnp.sqrt(jnp.float32(nbins))
    pattern = structure(
        coords,
        species.astype(jnp.float32),
        miller.astype(jnp.float32),
        offsets.astype(jnp.float32),
        form_amps,
        form_decay,
        nbins,
    )
    cand_z = standardize(pattern)
    product = lax.dot_general(
        lax.all_gather(cand_z, ("db", "cand"), axis=0, tiled=True),
        ref_z,
        (((1,), (1,)), ((), ())),
        preferred_element_type=jnp.float32,
    )
    scores = product * scale_back
    return scores.astype(jnp.bfloat16)


def solution(mesh):
    in_specs = (
        P(None, ("groups", "db", "cand"), None),
        P(("groups", "db", "cand"), None),
        P(),
        P(),
        P(),
        P(),
        P(("db", "cand"), None),
    )
    out_specs = P("groups", ("db", "cand"))
    return jax.shard_map(
        per_device, mesh=mesh, in_specs=in_specs, out_specs=out_specs, check_vma=False
    )
```

profile of v0, /device:TPU:0, one launch (start us, length us, event | category | flops | bytes accessed | tf_op | source)
XLA Modules:
  0.0 74.7 jit_solution(15144540133896257717)
XLA Ops:
  0.0 0.7 convert_element_type.31
  0.7 0.1 eq.15
  0.8 0.8 %negate_bitcast_fusion.3 = (f32[89]{0:T(128)S(1)}, f32[89]{0:T(128)S(1)}, f32[89]{0:T(128)S(1)}, f32[89]{0:T(128)S(1)}, f32[89]{0:T(128)S(1)}, /*index=5*/f32[89]{0:T(128)S(1)}, f32[89]{0:T(128)S(1)}, f32[89]{0:T(128)S(1)}) fusion(f32[89,4]{0,1:T(4,128)} %param.12, f32[89,4]{0,1:T(4,128)} %param.11), kind=kLoop, calls=%fused_computation.44 | loop fusion | flops 356 | bytes 5696 | tf_op jit(solution)/shard_map/mul | solution.py:19
  1.6 0.7 slice_bitcast_fusion.2
  2.3 0.7 convert_element_type.35
  3.1 0.0 copy-start
  3.1 4.7 %convert_reduce_fusion = f32[4096]{0:T(1024)S(1)} fusion(bf16[4096,1024]{1,0:T(8,128)(2,1)} %param.13), kind=kLoop, calls=%fused_computation.1 | loop fusion | flops 8384512 | bytes 8404992 | tf_op jit(solution)/shard_map/reduce_sum | solution.py:48
  7.8 1.1 %copy-done = bf16[4096,1024]{1,0:T(8,128)(2,1)S(1)} copy-done((bf16[4096,1024]{1,0:T(8,128)(2,1)S(1)}, bf16[4096,1024]{1,0:T(8,128)(2,1)}, u32[]{:S(2)}) %copy-start) | copy-done | bytes 8388632
  8.8 0.0 copy-start.1
  8.8 2.8 %fusion.2 = f32[4096]{0:T(1024)S(1)} fusion(bf16[4096,1024]{1,0:T(8,128)(2,1)S(1)} %copy-done, f32[4096]{0:T(1024)S(1)} %broadcast_multiply_fusion), kind=kLoop, calls=%fused_computation.4 | loop fusion | flops 16773120 | bytes 8421376 | tf_op jit(solution)/shard_map/reduce_sum | solution.py:50
  11.6 0.0 copy-done.1
  11.7 0.1 add_multiply_fusion.1
  11.7 17.9 %multiply_reduce_fusion.1 = (f32[4,4096]{1,0:T(4,128)S(1)}, f32[4,4096]{1,0:T(4,128)S(1)}) fusion(f32[4096]{0:T(1024)S(1)} %bitcast.33, f32[4,64]{1,0:T(4,128)S(1)} %get-tuple-element.12, f32[4096]{0:T(1024)S(1)} %bitcast.34, f32[4,64]{1,0:T(4,128)S(1)} %get-tuple-element.13, f32[4096]{0:T(1024)S(1)} %bitcast.35, f32[4,64]{1,0:T(4,128)S(1)} %get-tuple-element.11, ...), kind=kOutput, calls=%fused_computation.12 | convolution fusion | flops 201496832 | bytes 203552 | tf_op jit(solution)/shard_map/dot_general | solution.py:30
  29.6 3.8 %fusion.27 = (f32[4]{0:T(128)S(1)}, f32[4,1024]{1,0:T(4,128)S(1)}) fusion(f32[4096]{0:T(1024)S(1)} %convert_element_type.35, f32[4,4096]{1,0:T(4,128)S(1)} %get-tuple-element.6, f32[4,4096]{1,0:T(4,128)S(1)} %get-tuple-element.5), kind=kOutput, calls=%fused_computation.49 | convolution fusion | flops 54595580 | bytes 163856 | tf_op jit(solution)/shard_map/dot_general | solution.py:44
  33.4 0.2 multiply_reduce_fusion.2
  33.6 0.1 fusion.24
  33.7 35.0 %all-gather = bf16[16,4,1024]{2,1,0:T(4,128)(2,1)S(1)} all-gather(bf16[1,4,1024]{2,1,0:T(4,128)(2,1)S(1)} %fusion.24), channel_id=1, replica_groups=mesh['groups'=2,'db'=4,'cand'=4] {'db','cand'}, dimensions={0}, use_global_device_ids=true | all-gather | bytes 139264 | tf_op jit(solution)/shard_map/all_gather | solution.py:69
  68.7 6.0 %fusion.10 = bf16[64,4096]{1,0:T(8,128)(2,1)} fusion(bf16[64,1024]{1,0:T(8,128)(2,1)S(1)} %reshape.37, bf16[4096,1024]{1,0:T(8,128)(2,1)} %param.13, f32[4096]{0:T(1024)S(1)} %add_sqrt_fusion, f32[4096]{0:T(1024)S(1)} %broadcast_multiply_fusion), kind=kOutput, calls=%fused_computation.10 | convolution fusion | flops 554172416 | bytes 9076736 | tf_op jit(solution)/shard_map/dot_general | solution.py:68
  (6 shorter events, 0.1 us)
Async XLA Ops:
  3.1 5.8 %copy-start = (bf16[4096,1024]{1,0:T(8,128)(2,1)S(1)}, bf16[4096,1024]{1,0:T(8,128)(2,1)}, u32[]{:S(2)}) copy-start(bf16[4096,1024]{1,0:T(8,128)(2,1)} %param.13) | copy-start | bytes 25165828
  8.8 2.8 %copy-start.1 = (s32[3,4096]{1,0:T(4,128)S(1)}, s32[3,4096]{1,0:T(4,128)}, u32[]{:S(2)}) copy-start(s32[3,4096]{1,0:T(4,128)} %param.9) | copy-start | bytes 147460
where the time goes:
time: 75 us; the launch traced here: 74.7 us
  blocking collectives  35 us (47%)
  matrix products  27.7 us (37%)
  other arithmetic  10.1 us (13%)
  local copies, waits for them, and re-layouts  1.9 us (3%)
    all_gather x1, blocking collectives, per_device(): lax.all_gather(cand_z, ('db', 'cand'), axis=0, tiled=True)  35 us
    dot_general x1, matrix products, structure(): jnp.dot(onehot, table, preferred_element_type=jnp.float32)  17.9 us
    dot_general x1, matrix products, per_device(): lax.dot_general(lax.all_gather(cand_z, ('db', 'cand'), axis=0, tiled=True...  5.99 us
    reduce_sum x1, other arithmetic, standardize(): row_mean = jnp.mean(rows, axis=1, keepdims=True)  4.7 us
    dot_general x1, matrix products, structure(): return jnp.dot(intensity, profile, preferred_element_type=jnp.float32)  3.82 us
    reduce_sum x2, other arithmetic, standardize(): jnp.mean(centered * centered, axis=1, keepdims=True) + EPSILON  2.97 us

commit v1 on v0

v1 whole, which is shorter than its diff:
```python
import functools

import jax
import jax.numpy as jnp
from jax import lax
from jax.experimental import pallas as pl
from jax.experimental.pallas import tpu as pltpu
from jax.sharding import PartitionSpec as P

EPSILON = 1e-06
Q_SCALE = 0.0025
PEAK_WIDTH = 0.5
LANES = 128
NORMS = 256
CHUNK = 512
REF_ROWS = 512

SIN_COEFS = (3.14159258, -5.1677069, 2.55003164, -0.59804645, 0.07722225)
COS_COEFS = (0.99999995, -4.93479286, 4.05841191, -1.33188016, 0.21969679)


def horner(coefs, x):
    result = coefs[-1] * x + coefs[-2]
    for coef in coefs[-3::-1]:
        result = result * x + coef
    return result


def flat_lanes(rows):
    return jnp.concatenate([rows[c : c + 1] for c in range(rows.shape[0])], axis=1)


def candidate_kernel(
    coords_ref, species_ref, miller_ref, offsets_ref, amps_ref, decay_ref, out_ref,
    places_ref, table_ref, spread_ref,
):
    f32, bf16 = jnp.float32, jnp.bfloat16
    count, atoms = species_ref.shape
    kinds = amps_ref.shape[1]
    reflections = miller_ref.shape[1]
    nbins = out_ref.shape[1]
    nblocks = nbins // LANES
    flat = count * atoms

    pieces = []
    for axis in range(3):
        value = flat_lanes(coords_ref[axis])
        for _ in range(3):
            piece = value.astype(bf16)
            value = value - piece.astype(f32)
            pieces.append(piece.astype(f32))
    places_ref[...] = jnp.concatenate(pieces, axis=0).astype(bf16).T

    norms = lax.broadcasted_iota(jnp.int32, (NORMS, kinds), 0).astype(f32) * Q_SCALE
    table = jnp.zeros((NORMS, kinds), f32)
    for term in range(amps_ref.shape[0]):
        table = table + amps_ref[term : term + 1, :] * jnp.exp(
            -decay_ref[term : term + 1, :] * norms
        )
    onehot = (
        lax.broadcasted_iota(jnp.int32, (kinds, flat), 0) == flat_lanes(species_ref[...])
    ).astype(f32).astype(bf16)
    table_ref[...] = jnp.dot(
        table.astype(bf16), onehot, preferred_element_type=f32
    ).astype(bf16).T

    spread_ref[...] = jnp.zeros_like(spread_ref)

    def step(index, carry):
        cols = pl.ds(pl.multiple_of(index * CHUNK, CHUNK), CHUNK)
        miller = miller_ref[:, cols]
        norm = jnp.sum(miller * miller, axis=0, keepdims=True)
        hkl = miller.astype(f32)
        hkl9 = jnp.concatenate(
            [hkl[axis : axis + 1] for axis in range(3) for _ in range(3)], axis=0
        ).astype(bf16)
        turns = jnp.dot(places_ref[...], hkl9, preferred_element_type=f32)
        pick = (
            lax.broadcasted_iota(jnp.int32, (NORMS, CHUNK), 0) == norm
        ).astype(f32).astype(bf16)
        weight = jnp.dot(table_ref[...], pick, preferred_element_type=f32)
        u = turns - jnp.round(turns)
        square = u * u
        half_sin = u * horner(SIN_COEFS, square)
        half_cos = horner(COS_COEFS, square)
        part = weight * half_sin
        total = jnp.sum(weight.reshape(count, atoms, CHUNK), axis=1)
        real = total - 2.0 * jnp.sum((part * half_sin).reshape(count, atoms, CHUNK), axis=1)
        imag = 2.0 * jnp.sum((part * half_cos).reshape(count, atoms, CHUNK), axis=1)
        intensity = (real * real + imag * imag).astype(bf16).astype(f32)

        offset = offsets_ref[:, cols]
        block = offset // LANES
        local = (offset - block * LANES).astype(f32)
        routed = jnp.concatenate(
            [jnp.where(block == i, intensity, 0.0) for i in range(nblocks)], axis=0
        ).astype(bf16)
        bins = lax.broadcasted_iota(jnp.int32, (2 * LANES, CHUNK), 0)
        bins = jnp.where(bins < LANES + LANES // 2, bins, bins - 2 * LANES).astype(f32)
        distance = (bins - local) * (1.0 / PEAK_WIDTH)
        profile = jnp.exp(-0.5 * distance * distance).astype(bf16)
        spread_ref[...] += lax.dot_general(
            routed, profile, (((1,), (1,)), ((), ())), preferred_element_type=f32
        )
        return carry

    lax.fori_loop(0, reflections // CHUNK, step, 0)

    lane = lax.broadcasted_iota(jnp.int32, (count, LANES), 1)
    blocks = []
    for i in range(nblocks):
        own = spread_ref[i * count : (i + 1) * count, :LANES]
        before = after = jnp.zeros_like(own)
        if i > 0:
            before = spread_ref[(i - 1) * count : i * count, LANES:]
        if i + 1 < nblocks:
            after = spread_ref[(i + 1) * count : (i + 2) * count, LANES:]
        blocks.append(own + jnp.where(lane < LANES // 2, before, after))
    pattern = jnp.concatenate(blocks, axis=1)
    centered = pattern - jnp.mean(pattern, axis=1, keepdims=True)
    variance = jnp.mean(centered * centered, axis=1, keepdims=True)
    out_ref[...] = (centered / jnp.sqrt(variance + EPSILON)).astype(bf16)


def candidate_patterns(coords, species, miller, offsets, form_amps, form_decay, nbins):
    count, atoms = species.shape
    return pl.pallas_call(
        candidate_kernel,
        out_shape=jax.ShapeDtypeStruct((count, nbins), jnp.bfloat16),
        scratch_shapes=[
            pltpu.VMEM((count * atoms, 9), jnp.bfloat16),
            pltpu.VMEM((count * atoms, NORMS), jnp.bfloat16),
            pltpu.VMEM((count * (nbins // LANES), 2 * LANES), jnp.float32),
        ],
        name="candidates",
    )(coords, species, miller, offsets[None, :], form_amps.T, form_decay.T)


def standardize_kernel(rows_ref, out_ref):
    rows = rows_ref[...].astype(jnp.float32)
    centered = rows - jnp.mean(rows, axis=1, keepdims=True)
    variance = jnp.mean(centered * centered, axis=1, keepdims=True)
    out_ref[...] = (centered * lax.rsqrt(variance + EPSILON)).astype(jnp.bfloat16)


def standardize_refs(rows):
    count, nbins = rows.shape
    spec = pl.BlockSpec((REF_ROWS, nbins), lambda i: (i, 0))
    return pl.pallas_call(
        standardize_kernel,
        out_shape=jax.ShapeDtypeStruct(rows.shape, jnp.bfloat16),
        grid=(count // REF_ROWS,),
        in_specs=[spec],
        out_specs=spec,
        cost_estimate=pl.CostEstimate(
            flops=6 * count * nbins, bytes_accessed=4 * count * nbins, transcendentals=0
        ),
        name="references",
    )(rows)


def score_kernel(masks, position_ref, cand_ref, refs_ref, out_ref, sorted_ref):
    total = cand_ref.shape[0]
    block = total // 2 ** len(masks)

    @pl.when(pl.program_id(0) == 0)
    def _():
        place = lax.broadcasted_iota(jnp.int32, (total, total), 1)
        group = place // block
        source = jnp.full_like(group, position_ref[0])
        for bit, mask in enumerate(masks):
            source = source ^ jnp.where((group >> bit) % 2 == 1, mask, 0)
        wanted = source * block + place % block
        row = lax.broadcasted_iota(jnp.int32, (total, total), 0)
        order = (row == wanted).astype(jnp.float32).astype(jnp.bfloat16)
        sorted_ref[...] = jnp.dot(
            order, cand_ref[...], preferred_element_type=jnp.float32
        ).astype(jnp.bfloat16)

    product = lax.dot_general(
        sorted_ref[...],
        refs_ref[...],
        (((1,), (1,)), ((), ())),
        preferred_element_type=jnp.float32,
    )
    scale = 1.0 / jnp.sqrt(jnp.float32(refs_ref.shape[1]))
    out_ref[...] = (product * scale).astype(jnp.bfloat16)


def score(position, masks, cand, refs):
    total, nbins = cand.shape
    count = refs.shape[0]
    return pl.pallas_call(
        functools.partial(score_kernel, masks),
        out_shape=jax.ShapeDtypeStruct((total, count), jnp.bfloat16),
        grid=(count // REF_ROWS,),
        in_specs=[
            pl.BlockSpec(memory_space=pltpu.SMEM),
            pl.BlockSpec((total, nbins), lambda i: (0, 0)),
            pl.BlockSpec((REF_ROWS, nbins), lambda i: (i, 0)),
        ],
        out_specs=pl.BlockSpec((total, REF_ROWS), lambda i: (0, i)),
        scratch_shapes=[pltpu.VMEM((total, nbins), jnp.bfloat16)],
        name="scores",
    )(position, cand, refs)


def per_device(ndb, ncand, coords, species, miller, offsets, form_amps, form_decay, ref_patterns):
    nbins = ref_patterns.shape[1]
    cand = candidate_patterns(coords, species, miller, offsets, form_amps, form_decay, nbins)
    members = ndb * ncand
    position = (lax.axis_index("db") * ncand + lax.axis_index("cand"))[None].astype(jnp.int32)
    masks = [ncand << bit for bit in range(ndb.bit_length() - 1)]
    masks += [1 << bit for bit in range(ncand.bit_length() - 1)]
    for mask in masks:
        pairs = [(i, i ^ mask) for i in range(members)]
        other = lax.ppermute(cand, ("db", "cand"), pairs)
        cand = jnp.concatenate([cand, other], axis=0)
    refs = standardize_refs(ref_patterns)
    return score(position, tuple(masks), cand, refs)


def solution(mesh):
    in_specs = (
        P(None, ("groups", "db", "cand"), None),
        P(("groups", "db", "cand"), None),
        P(),
        P(),
        P(),
        P(),
        P(("db", "cand"), None),
    )
    out_specs = P("groups", ("db", "cand"))
    body = functools.partial(per_device, mesh.shape["db"], mesh.shape["cand"])
    return jax.shard_map(
        body, mesh=mesh, in_specs=in_specs, out_specs=out_specs, check_vma=False
    )
```

time: 75 us -> 46.7 us (0.62)
  blocking collectives: 35 us -> 0 us
  Pallas kernels: 0 us -> 28.2 us
  matrix products: 27.7 us -> 0 us
  starting transfers between devices: 0 us -> 8.62 us
  other arithmetic: 10.1 us -> 2.14 us
  waiting for transfers between devices: 0 us -> 4.65 us
    all_gather x1 -> x0, blocking collectives: 35 us -> none  [per_device(): lax.all_gather(cand_z, ('db', 'cand'), axis=0, tiled=True)]
    pallas_call x0 -> x3, Pallas kernels: none -> 28.2 us  [the longest x1 10.6 us: standardize_refs(): pl.pallas_call(standardize_kernel, out_shape=jax.ShapeDtypeStruct(rows.sh...]
    dot_general x3 -> x0, matrix products: 27.7 us -> none  [the longest x1 17.9 us: structure(): jnp.dot(onehot, table, preferred_element_type=jnp.float32)]
    ppermute x0 -> x4, starting transfers between devices: none -> 8.62 us  [per_device(): other = lax.ppermute(cand, ('db', 'cand'), pairs)]
    reduce_sum x3 -> x0, other arithmetic: 7.66 us -> none  [the longest x1 4.7 us: standardize(): row_mean = jnp.mean(rows, axis=1, keepdims=True)]
    ppermute x0 -> x4, waiting for transfers between devices: none -> 4.65 us  [per_device(): other = lax.ppermute(cand, ('db', 'cand'), pairs)]
    concatenate x0 -> x1, local copies, waits for them, and re-layouts: none -> 2.46 us  [per_device(): cand = jnp.concatenate([cand, other], axis=0)]
    concatenate x0 -> x3, other arithmetic: none -> 2.14 us  [per_device(): cand = jnp.concatenate([cand, other], axis=0)]
  transfers between devices with their start and end apart: 0 -> 4, of which waited for: 0 -> 3; matrix products, arithmetic and copies ran while one was open for 0% -> 0% of each run, Pallas kernels for 0% -> 23%
where the time goes in v1:
time: 46.7 us; the launch traced here: 46.1 us
  Pallas kernels  28.2 us (60%)
  starting transfers between devices  8.62 us (18%)
  waiting for transfers between devices  4.65 us (10%)
  local copies, waits for them, and re-layouts  2.46 us (5%)
  other arithmetic  2.14 us (5%)
    pallas_call x1, Pallas kernels, standardize_refs(): pl.pallas_call(standardize_kernel, out_shape=jax.ShapeDtypeStruct(rows.sh...  10.6 us
    pallas_call x1, Pallas kernels, candidate_patterns(): pl.pallas_call(candidate_kernel, out_shape=jax.ShapeDtypeStruct((count, n...  9.15 us
    ppermute x4, starting transfers between devices, per_device(): other = lax.ppermute(cand, ('db', 'cand'), pairs)  8.62 us
    pallas_call x1, Pallas kernels, score(): pl.pallas_call(functools.partial(score_kernel, masks), out_shape=jax.Shap...  8.4 us
    ppermute x4, waiting for transfers between devices, per_device(): other = lax.ppermute(cand, ('db', 'cand'), pairs)  4.65 us
    concatenate x1, local copies, waits for them, and re-layouts, per_device(): cand = jnp.concatenate([cand, other], axis=0)  2.46 us
    concatenate x3, other arithmetic, per_device(): cand = jnp.concatenate([cand, other], axis=0)  2.14 us
  transfers between devices with their start and end apart: 4, of which 3 were waited for; matrix products, arithmetic and copies ran while one was open for 0% of the time, Pallas kernels for 23%

profile of v1, /device:TPU:0, one launch (start us, length us, event | category | flops | bytes accessed | tf_op | source)
XLA Modules:
  0.0 46.1 jit_solution(14310262749057646966)
XLA Ops:
  0.0 9.1 %candidates.1 = bf16[4,1024]{1,0:T(4,128)(2,1)} custom-call(f32[3,4,64]{2,1,0:T(4,128)} %coords_ref.1, s32[4,64]{1,0:T(4,128)} %species_ref.1, s32[3,4096]{1,0:T(4,128)} %miller_ref.1, s32[1,4096]{1,0:T(1,128)} %bitcast.4, f32[4,89]{1,0:T(4,128)} %bitcast.5, f32[4,89]{1,0:T(4,128)} %bitcast.6), custom_call_target="tpu_custom_call" | custom-call | tf_op jit(solution)/shard_map/candidates/pallas_call | solution.py:127
  9.1 0.4 collective-permute-start
  9.6 1.0 %collective-permute-done = bf16[4,1024]{1,0:T(4,128)(2,1)S(1)} collective-permute-done((bf16[4,1024]{1,0:T(4,128)(2,1)}, bf16[4,1024]{1,0:T(4,128)(2,1)S(1)}, u32[]{:S(2)}, u32[]{:S(2)}) %collective-permute-start) | collective-permute-done | bytes 8224 | tf_op jit(solution)/shard_map/ppermute | solution.py:217
  10.6 0.7 %pad_maximum_fusion.2 = bf16[8,1024]{1,0:T(8,128)(2,1)S(1)} fusion(bf16[4,1024]{1,0:T(4,128)(2,1)S(1)} %collective-permute-done, bf16[4,1024]{1,0:T(4,128)(2,1)} %candidates.1), kind=kLoop, calls=%fused_computation.2 | loop fusion | flops 32768 | bytes 32768 | tf_op jit(solution)/shard_map/concatenate | solution.py:218
  11.3 2.9 %collective-permute-start.1 = (bf16[8,1024]{1,0:T(8,128)(2,1)S(1)}, bf16[8,1024]{1,0:T(8,128)(2,1)S(1)}, u32[]{:S(2)}, u32[]{:S(2)}) collective-permute-start(bf16[8,1024]{1,0:T(8,128)(2,1)S(1)} %pad_maximum_fusion.2), channel_id=1, source_target_pairs={{0,8},{1,9},{2,10},{3,11},{4,12},{5,13},{6,14},{7,15},{8,0},{9,1},... | collective-permute-start | bytes 49160 | tf_op jit(solution)/shard_map/ppermute | solution.py:217
  14.2 1.7 %collective-permute-done.1 = bf16[8,1024]{1,0:T(8,128)(2,1)S(1)} collective-permute-done((bf16[8,1024]{1,0:T(8,128)(2,1)S(1)}, bf16[8,1024]{1,0:T(8,128)(2,1)S(1)}, u32[]{:S(2)}, u32[]{:S(2)}) %collective-permute-start.1) | collective-permute-done | bytes 16416 | tf_op jit(solution)/shard_map/ppermute | solution.py:217
  16.0 0.7 %pad_maximum_fusion.1 = bf16[16,1024]{1,0:T(8,128)(2,1)S(1)} fusion(bf16[8,1024]{1,0:T(8,128)(2,1)S(1)} %collective-permute-done.1, bf16[4,1024]{1,0:T(4,128)(2,1)S(1)} %collective-permute-done, bf16[4,1024]{1,0:T(4,128)(2,1)} %candidates.1), kind=kLoop, calls=%fused_computation.1 | loop fusion | flops 98304 | bytes 65536 | tf_op jit(solution)/shard_map/concatenate | solution.py:218
  16.7 2.2 %collective-permute-start.2 = (bf16[16,1024]{1,0:T(8,128)(2,1)S(1)}, bf16[16,1024]{1,0:T(8,128)(2,1)S(1)}, u32[]{:S(2)}, u32[]{:S(2)}) collective-permute-start(bf16[16,1024]{1,0:T(8,128)(2,1)S(1)} %pad_maximum_fusion.1), channel_id=1, source_target_pairs={{0,1},{1,0},{2,3},{3,2},{4,5},{5,4},{6,7},{7,6},{8,9},{9,8},{10,11... | collective-permute-start | bytes 98312 | tf_op jit(solution)/shard_map/ppermute | solution.py:217
  18.9 1.9 %collective-permute-done.2 = bf16[16,1024]{1,0:T(8,128)(2,1)S(1)} collective-permute-done((bf16[16,1024]{1,0:T(8,128)(2,1)S(1)}, bf16[16,1024]{1,0:T(8,128)(2,1)S(1)}, u32[]{:S(2)}, u32[]{:S(2)}) %collective-permute-start.2) | collective-permute-done | bytes 32800 | tf_op jit(solution)/shard_map/ppermute | solution.py:217
  20.7 0.7 %pad_maximum_fusion = bf16[32,1024]{1,0:T(8,128)(2,1)S(1)} fusion(bf16[16,1024]{1,0:T(8,128)(2,1)S(1)} %collective-permute-done.2, bf16[8,1024]{1,0:T(8,128)(2,1)S(1)} %collective-permute-done.1, bf16[4,1024]{1,0:T(4,128)(2,1)S(1)} %collective-permute-done, bf16[4,1024]{1,0:T(4,128)(2,1)} %candidates.1), kind=kLoop, calls=%fused_computation | loop fusion | flops 262144 | bytes 131072 | tf_op jit(solution)/shard_map/concatenate | solution.py:218
  21.5 3.1 %collective-permute-start.3 = (bf16[32,1024]{1,0:T(8,128)(2,1)S(1)}, bf16[32,1024]{1,0:T(8,128)(2,1)S(1)}, u32[]{:S(2)}, u32[]{:S(2)}) collective-permute-start(bf16[32,1024]{1,0:T(8,128)(2,1)S(1)} %pad_maximum_fusion), channel_id=1, source_target_pairs={{0,2},{1,3},{2,0},{3,1},{4,6},{5,7},{6,4},{7,5},{8,10},{9,11},{10,... | collective-permute-start | bytes 196616 | tf_op jit(solution)/shard_map/ppermute | solution.py:217
  24.6 0.0 copy-start
  24.6 10.6 %references.1.refs_ref = bf16[4096,1024]{1,0:T(8,128)(2,1)} custom-call(bf16[4096,1024]{1,0:T(8,128)(2,1)} %rows_ref.1), custom_call_target="tpu_custom_call" | custom-call | flops 25165824 | bytes 16777216 | tf_op jit(solution)/shard_map/references/pallas_call | solution.py:149
  35.2 0.0 collective-permute-done.3
  35.2 0.0 copy-done
  35.2 2.5 %concatenate.18.cand_ref = bf16[64,1024]{1,0:T(8,128)(2,1)} concatenate(bf16[4,1024]{1,0:T(4,128)(2,1)S(1)} %copy-done, bf16[4,1024]{1,0:T(4,128)(2,1)S(1)} %collective-permute-done, bf16[8,1024]{1,0:T(8,128)(2,1)S(1)} %collective-permute-done.1, bf16[16,1024]{1,0:T(8,128)(2,1)S(1)} %collective-permute-done.2, bf16[32,1024]{1,0:T(8,128)(2,1)S(1)} %collective-permute-done.3), dimensions={0} | concatenate | bytes 262144 | tf_op jit(solution)/shard_map/concatenate | solution.py:218
  37.7 8.4 %scores.1 = bf16[64,4096]{1,0:T(8,128)(2,1)} custom-call(s32[1]{0:T(128)} %bitcast.position_ref, bf16[64,1024]{1,0:T(8,128)(2,1)} %concatenate.18.cand_ref, bf16[4096,1024]{1,0:T(8,128)(2,1)} %references.1.refs_ref), custom_call_target="tpu_custom_call" | custom-call | tf_op jit(solution)/shard_map/scores/pallas_call | solution.py:193
Async XLA Ops:
  9.1 1.5 %collective-permute-start = (bf16[4,1024]{1,0:T(4,128)(2,1)}, bf16[4,1024]{1,0:T(4,128)(2,1)S(1)}, u32[]{:S(2)}, u32[]{:S(2)}) collective-permute-start(bf16[4,1024]{1,0:T(4,128)(2,1)} %candidates.1), channel_id=1, source_target_pairs={{0,4},{1,5},{2,6},{3,7},{4,0},{5,1},{6,2},{7,3},{8,12},{9,13},{10,... | collective-permute-start | bytes 24584 | tf_op jit(solution)/shard_map/ppermute | solution.py:217
  11.3 4.6 %collective-permute-start.1 = (bf16[8,1024]{1,0:T(8,128)(2,1)S(1)}, bf16[8,1024]{1,0:T(8,128)(2,1)S(1)}, u32[]{:S(2)}, u32[]{:S(2)}) collective-permute-start(bf16[8,1024]{1,0:T(8,128)(2,1)S(1)} %pad_maximum_fusion.2), channel_id=1, source_target_pairs={{0,8},{1,9},{2,10},{3,11},{4,12},{5,13},{6,14},{7,15},{8,0},{9,1},... | collective-permute-start | bytes 49160 | tf_op jit(solution)/shard_map/ppermute | solution.py:217
  16.7 4.1 %collective-permute-start.2 = (bf16[16,1024]{1,0:T(8,128)(2,1)S(1)}, bf16[16,1024]{1,0:T(8,128)(2,1)S(1)}, u32[]{:S(2)}, u32[]{:S(2)}) collective-permute-start(bf16[16,1024]{1,0:T(8,128)(2,1)S(1)} %pad_maximum_fusion.1), channel_id=1, source_target_pairs={{0,1},{1,0},{2,3},{3,2},{4,5},{5,4},{6,7},{7,6},{8,9},{9,8},{10,11... | collective-permute-start | bytes 98312 | tf_op jit(solution)/shard_map/ppermute | solution.py:217
  21.5 13.7 %collective-permute-start.3 = (bf16[32,1024]{1,0:T(8,128)(2,1)S(1)}, bf16[32,1024]{1,0:T(8,128)(2,1)S(1)}, u32[]{:S(2)}, u32[]{:S(2)}) collective-permute-start(bf16[32,1024]{1,0:T(8,128)(2,1)S(1)} %pad_maximum_fusion), channel_id=1, source_target_pairs={{0,2},{1,3},{2,0},{3,1},{4,6},{5,7},{6,4},{7,5},{8,10},{9,11},{10,... | collective-permute-start | bytes 196616 | tf_op jit(solution)/shard_map/ppermute | solution.py:217
  24.6 10.6 %copy-start = (bf16[4,1024]{1,0:T(4,128)(2,1)S(1)}, bf16[4,1024]{1,0:T(4,128)(2,1)}, u32[]{:S(2)}) copy-start(bf16[4,1024]{1,0:T(4,128)(2,1)} %candidates.1) | copy-start | bytes 24580

commit v2 on v1

v2 whole, which is shorter than its diff:
```python
import functools

import jax
import jax.numpy as jnp
from jax import lax
from jax.experimental import pallas as pl
from jax.experimental.pallas import tpu as pltpu
from jax.sharding import PartitionSpec as P

EPSILON = 1e-06
Q_SCALE = 0.0025
PEAK_WIDTH = 0.5
LANES = 128
NORMS = 256
CHUNK = 512
TILE = 128
STAT_ROWS = 1024
SCORE_ROWS = 512
VMEM_LIMIT = 24 << 20

SIN_COEFS = (3.14158208, -5.1671442, 2.54190894, -0.55465711)
COS_COEFS = (0.99999995, -4.93479286, 4.05841191, -1.33188016, 0.21969679)


def horner(coefs, x):
    result = coefs[-1] * x + coefs[-2]
    for coef in coefs[-3::-1]:
        result = result * x + coef
    return result


def flat_lanes(rows):
    return jnp.concatenate([rows[c : c + 1] for c in range(rows.shape[0])], axis=1)


def candidate_kernel(
    coords_hbm, species_hbm, miller_hbm, offsets_hbm, amps_hbm, decay_hbm, refs_hbm,
    out_ref, refs_ref,
    coords_ref, species_ref, miller_ref, offsets_ref, amps_ref, decay_ref,
    places_ref, table_ref, spread_ref, sems,
):
    sources = (coords_hbm, species_hbm, miller_hbm, offsets_hbm, amps_hbm, decay_hbm, refs_hbm)
    targets = (coords_ref, species_ref, miller_ref, offsets_ref, amps_ref, decay_ref, refs_ref)
    copies = [
        pltpu.make_async_copy(source, target, sems.at[i])
        for i, (source, target) in enumerate(zip(sources, targets))
    ]
    for copy in copies:
        copy.start()
    for copy in copies[:-1]:
        copy.wait()
    f32, bf16 = jnp.float32, jnp.bfloat16
    count, atoms = species_ref.shape
    kinds = amps_ref.shape[1]
    reflections = miller_ref.shape[1]
    nbins = out_ref.shape[1]
    nblocks = nbins // LANES
    flat = count * atoms

    pieces = []
    for axis in range(3):
        value = flat_lanes(coords_ref[axis])
        for _ in range(3):
            piece = value.astype(bf16)
            value = value - piece.astype(f32)
            pieces.append(piece.astype(f32))
    places_ref[...] = jnp.concatenate(pieces, axis=0).astype(bf16).T

    norms = lax.broadcasted_iota(jnp.int32, (NORMS, kinds), 0).astype(f32) * Q_SCALE
    table = jnp.zeros((NORMS, kinds), f32)
    for term in range(amps_ref.shape[0]):
        table = table + amps_ref[term : term + 1, :] * jnp.exp(
            -decay_ref[term : term + 1, :] * norms
        )
    onehot = (
        lax.broadcasted_iota(jnp.int32, (kinds, flat), 0) == flat_lanes(species_ref[...])
    ).astype(f32).astype(bf16)
    table_ref[...] = jnp.dot(
        table.astype(bf16), onehot, preferred_element_type=f32
    ).astype(bf16).T

    spread_ref[...] = jnp.zeros_like(spread_ref)

    def step(index, carry):
        cols = pl.ds(pl.multiple_of(index * CHUNK, CHUNK), CHUNK)
        miller = miller_ref[:, cols]
        norm = jnp.sum(miller * miller, axis=0, keepdims=True)
        hkl = miller.astype(f32)
        hkl9 = jnp.concatenate(
            [hkl[axis : axis + 1] for axis in range(3) for _ in range(3)], axis=0
        ).astype(bf16)
        turns = jnp.dot(places_ref[...], hkl9, preferred_element_type=f32)
        pick = (
            lax.broadcasted_iota(jnp.int32, (NORMS, CHUNK), 0) == norm
        ).astype(f32).astype(bf16)
        weight = jnp.dot(table_ref[...], pick, preferred_element_type=f32)
        rows = []
        for c in range(count):
            tiles = []
            for lane in range(0, CHUNK, TILE):
                at = (slice(c * atoms, (c + 1) * atoms), slice(lane, lane + TILE))
                t = turns[at]
                w = weight[at]
                u = t - jnp.round(t)
                square = u * u
                half_sin = u * horner(SIN_COEFS, square)
                half_cos = horner(COS_COEFS, square)
                part = w * half_sin
                real = jnp.sum(w - 2.0 * (part * half_sin), axis=0, keepdims=True)
                imag = 2.0 * jnp.sum(part * half_cos, axis=0, keepdims=True)
                tiles.append(real * real + imag * imag)
            rows.append(jnp.concatenate(tiles, axis=1))
        intensity = jnp.concatenate(rows, axis=0).astype(bf16).astype(f32)
        offset = offsets_ref[:, cols]
        block = offset // LANES
        routed = jnp.concatenate(
            [jnp.where(block == i, intensity, 0.0) for i in range(nblocks)], axis=0
        ).astype(bf16)
        local = (
            lax.broadcasted_iota(jnp.int32, (LANES, CHUNK), 0) == offset - block * LANES
        ).astype(f32).astype(bf16)
        spread_ref[...] += lax.dot_general(
            local, routed, (((1,), (1,)), ((), ())), preferred_element_type=f32
        )
        return carry

    lax.fori_loop(0, reflections // CHUNK, step, 0, unroll=True)

    sums = spread_ref[...].T
    pieces = []
    for _ in range(3):
        piece = sums.astype(bf16)
        sums = sums - piece.astype(f32)
        pieces.append(piece.astype(f32))
    centre = lax.broadcasted_iota(jnp.int32, (LANES, 2 * LANES), 0)
    bins = lax.broadcasted_iota(jnp.int32, (LANES, 2 * LANES), 1)
    bins = jnp.where(bins < LANES + LANES // 2, bins, bins - 2 * LANES)
    distance = (bins - centre).astype(f32) * (1.0 / PEAK_WIDTH)
    profile = jnp.exp(-0.5 * distance * distance).astype(bf16)
    peaks = jnp.dot(
        jnp.concatenate(pieces, axis=0).astype(bf16), profile, preferred_element_type=f32
    )
    rows = count * nblocks
    peaks = peaks[:rows] + peaks[rows : 2 * rows] + peaks[2 * rows :]
    lane = lax.broadcasted_iota(jnp.int32, (count, LANES), 1)
    blocks = []
    for i in range(nblocks):
        own = peaks[i * count : (i + 1) * count, :LANES]
        before = after = jnp.zeros_like(own)
        if i > 0:
            before = peaks[(i - 1) * count : i * count, LANES:]
        if i + 1 < nblocks:
            after = peaks[(i + 1) * count : (i + 2) * count, LANES:]
        blocks.append(own + jnp.where(lane < LANES // 2, before, after))
    pattern = jnp.concatenate(blocks, axis=1)
    centered = pattern - jnp.mean(pattern, axis=1, keepdims=True)
    variance = jnp.mean(centered * centered, axis=1, keepdims=True)
    out_ref[...] = (centered / jnp.sqrt(variance + EPSILON)).astype(bf16)
    copies[-1].wait()


def candidate_patterns(coords, species, miller, offsets, form_amps, form_decay, refs):
    count, atoms = species.shape
    nbins = refs.shape[1]
    args = (coords, species, miller, offsets[None, :], form_amps.T, form_decay.T)
    args = [pltpu.with_memory_space_constraint(arg, pltpu.HBM) for arg in args + (refs,)]
    return pl.pallas_call(
        candidate_kernel,
        out_shape=[
            pltpu.VMEM((count, nbins), jnp.bfloat16),
            pltpu.VMEM(refs.shape, refs.dtype),
        ],
        in_specs=[pl.BlockSpec(memory_space=pltpu.HBM)] * len(args),
        scratch_shapes=[pltpu.VMEM(arg.shape, arg.dtype) for arg in args[:-1]]
        + [
            pltpu.VMEM((count * atoms, 9), jnp.bfloat16),
            pltpu.VMEM((count * atoms, NORMS), jnp.bfloat16),
            pltpu.VMEM((LANES, count * (nbins // LANES)), jnp.float32),
            pltpu.SemaphoreType.DMA((len(args),)),
        ],
        compiler_params=pltpu.CompilerParams(vmem_limit_bytes=VMEM_LIMIT),
        name="candidates",
    )(*args)


VMEM_WHOLE = pl.BlockSpec(memory_space=pltpu.VMEM)


def statistics_kernel(first, refs_ref, after_ref, mean_ref, scale_ref, same_ref):
    f32 = jnp.float32
    nbins = refs_ref.shape[1]
    rows = mean_ref.shape[0]
    ones = jnp.ones((nbins, LANES), jnp.bfloat16)
    block = refs_ref[first : first + rows, :]
    mean = jnp.dot(block, ones, preferred_element_type=f32) * (1.0 / nbins)
    total = jnp.zeros((rows, LANES), f32)
    for lane in range(0, nbins, LANES):
        centered = block[:, lane : lane + LANES].astype(f32) - mean
        total = total + centered * centered
    variance = jnp.sum(total, axis=1, keepdims=True) * (1.0 / nbins)
    mean_ref[...] = mean[:, :1]
    scale_ref[...] = lax.rsqrt(variance + EPSILON) * (1.0 / nbins**0.5)


def statistics(refs, first, rows, after):
    nbins = refs.shape[1]
    return pl.pallas_call(
        functools.partial(statistics_kernel, first),
        out_shape=[pltpu.VMEM((rows, 1), jnp.float32)] * 2 + [pltpu.VMEM(refs.shape, refs.dtype)],
        in_specs=[VMEM_WHOLE, pl.BlockSpec(memory_space=pl.ANY)],
        out_specs=[VMEM_WHOLE] * 3,
        input_output_aliases={0: 2},
        compiler_params=pltpu.CompilerParams(vmem_limit_bytes=VMEM_LIMIT),
        cost_estimate=pl.CostEstimate(
            flops=2 * rows * nbins * LANES, bytes_accessed=2 * rows * nbins, transcendentals=rows
        ),
        name="statistics",
    )(pltpu.with_memory_space_constraint(refs, pltpu.VMEM), after)


def score_kernel(ncand, masks, npieces, *rest):
    cand_refs, (refs_ref, *rest) = rest[: len(masks) + 1], rest[len(masks) + 1 :]
    mean_refs, scale_refs = rest[:npieces], rest[npieces : 2 * npieces]
    out_ref, cand_t_ref = rest[2 * npieces :]
    f32, bf16 = jnp.float32, jnp.bfloat16
    cand = jnp.concatenate([ref[...] for ref in cand_refs], axis=0)
    total, nbins = cand.shape
    block = cand_refs[0].shape[0]
    place = lax.broadcasted_iota(jnp.int32, (total, total), 0)
    group = place // block
    position = lax.axis_index("db") * ncand + lax.axis_index("cand")
    source = jnp.full_like(group, position)
    for bit, mask in enumerate(masks):
        source = source ^ jnp.where((group >> bit) % 2 == 1, mask, 0)
    row = lax.broadcasted_iota(jnp.int32, (total, total), 1)
    order = (row == source * block + place % block).astype(f32).astype(bf16)
    cand_t_ref[...] = lax.dot_general(
        cand, order, (((0,), (0,)), ((), ())), preferred_element_type=f32
    ).astype(bf16)
    sums = jnp.dot(jnp.ones((8, nbins), bf16), cand_t_ref[...], preferred_element_type=f32)[:1]
    rows = mean_refs[0].shape[0]
    for i in range(refs_ref.shape[0] // SCORE_ROWS):
        start = i * SCORE_ROWS
        piece, at = start // rows, slice(start % rows, start % rows + SCORE_ROWS)
        product = jnp.dot(
            refs_ref[start : start + SCORE_ROWS, :], cand_t_ref[...], preferred_element_type=f32
        )
        product = (product - mean_refs[piece][at, :] * sums) * scale_refs[piece][at, :]
        out_ref[:, start : start + SCORE_ROWS] = product.T.astype(bf16)


def score(ncand, masks, cands, refs, means, scales):
    total = sum(cand.shape[0] for cand in cands)
    count, nbins = refs.shape
    return pl.pallas_call(
        functools.partial(score_kernel, ncand, masks, len(means)),
        out_shape=jax.ShapeDtypeStruct((total, count), jnp.bfloat16),
        in_specs=[VMEM_WHOLE] * (len(cands) + 1 + 2 * len(means)),
        scratch_shapes=[pltpu.VMEM((nbins, total), jnp.bfloat16)],
        compiler_params=pltpu.CompilerParams(vmem_limit_bytes=VMEM_LIMIT),
        name="scores",
    )(*cands, pltpu.with_memory_space_constraint(refs, pltpu.VMEM), *means, *scales)


def per_device(ndb, ncand, coords, species, miller, offsets, form_amps, form_decay, ref_patterns):
    count, nbins = ref_patterns.shape
    held, refs = candidate_patterns(
        coords, species, miller, offsets, form_amps, form_decay, ref_patterns
    )
    members = ndb * ncand
    masks = [ncand << bit for bit in range(ndb.bit_length() - 1)]
    masks += [1 << bit for bit in range(ncand.bit_length() - 1)]
    cands, means, scales = [held], [], []
    for stage, mask in enumerate(masks):
        pairs = [(i, i ^ mask) for i in range(members)]
        other = lax.ppermute(held, ("db", "cand"), pairs)
        first = len(means) * STAT_ROWS
        if first < count:
            mean, scale, refs = statistics(refs, first, STAT_ROWS, held)
            means.append(mean)
            scales.append(scale)
            other, mean = lax.optimization_barrier((other, mean))
        cands.append(other)
        held = jnp.concatenate([held, other], axis=0)
    for first in range(len(means) * STAT_ROWS, count, STAT_ROWS):
        mean, scale, refs = statistics(refs, first, STAT_ROWS, held)
        means.append(mean)
        scales.append(scale)
    return score(ncand, tuple(masks), cands, refs, means, scales)


def solution(mesh):
    in_specs = (
        P(None, ("groups", "db", "cand"), None),
        P(("groups", "db", "cand"), None),
        P(),
        P(),
        P(),
        P(),
        P(("db", "cand"), None),
    )
    out_specs = P("groups", ("db", "cand"))
    body = functools.partial(per_device, mesh.shape["db"], mesh.shape["cand"])
    return jax.shard_map(
        body, mesh=mesh, in_specs=in_specs, out_specs=out_specs, check_vma=False
    )
```

time: 46.7 us -> 25.6 us (0.55); the launches traced: 46.1 us -> 25.5 us
  Pallas kernels: 28.2 us -> 14.9 us
  waiting for transfers between devices: 4.65 us -> 2.11 us
  local copies, waits for them, and re-layouts: 2.46 us -> 0 us
  other arithmetic: 2.14 us -> 0.05 us
    pallas_call x3 -> x6, Pallas kernels: 28.2 us -> 14.9 us  [the longest x1 6.31 us: candidate_patterns(): pl.pallas_call(candidate_kernel, out_shape=[pltpu.VMEM((count, nbins), jn...]
    ppermute x4, waiting for transfers between devices: 4.65 us -> 2.11 us  [per_device(): other = lax.ppermute(held, ('db', 'cand'), pairs)]
    concatenate x1 -> x0, local copies, waits for them, and re-layouts: 2.46 us -> none  [per_device(): cand = jnp.concatenate([cand, other], axis=0)]
    concatenate x3, other arithmetic: 2.14 us -> 0.05 us  [per_device(): held = jnp.concatenate([held, other], axis=0)]
  transfers between devices with their start and end apart: 4 -> 4, of which waited for: 3 -> 3; matrix products, arithmetic and copies ran while one was open for 0% -> 0% of each run, Pallas kernels for 23% -> 19%
where the time goes in v2:
time: 25.6 us; the launch traced here: 25.5 us
  Pallas kernels  14.9 us (58%)
  starting transfers between devices  8.35 us (33%)
  waiting for transfers between devices  2.11 us (8%)
    ppermute x4, starting transfers between devices, per_device(): other = lax.ppermute(held, ('db', 'cand'), pairs)  8.35 us
    pallas_call x1, Pallas kernels, candidate_patterns(): pl.pallas_call(candidate_kernel, out_shape=[pltpu.VMEM((count, nbins), jn...  6.31 us
    pallas_call x4, Pallas kernels, statistics(): pl.pallas_call(functools.partial(statistics_kernel, first), out_shape=[pl...  4.97 us
    pallas_call x1, Pallas kernels, score(): pl.pallas_call(functools.partial(score_kernel, ncand, masks, len(means)),...  3.6 us
    ppermute x4, waiting for transfers between devices, per_device(): other = lax.ppermute(held, ('db', 'cand'), pairs)  2.11 us
  transfers between devices with their start and end apart: 4, of which 3 were waited for; matrix products, arithmetic and copies ran while one was open for 0% of the time, Pallas kernels for 19%

profile of v2, /device:TPU:0, one launch (start us, length us, event | category | flops | bytes accessed | tf_op | source)
XLA Modules:
  0.0 25.5 jit_solution(11378300375647157006)
XLA Ops:
  0.0 6.3 %candidates.1 = (bf16[4,1024]{1,0:T(4,128)(2,1)S(1)}, bf16[4096,1024]{1,0:T(8,128)(2,1)S(1)}) custom-call(f32[3,4,64]{2,1,0:T(4,128)} %coords_hbm.1, s32[4,64]{1,0:T(4,128)} %species_hbm.1, s32[3,4096]{1,0:T(4,128)} %miller_hbm.1, s32[1,4096]{1,0:T(1,128)} %bitcast.3, f32[4,89]{1,0:T(4,128)} %bitcast.4, f32[4,89]{1,0:T(4,128)} %bitcast.5, ...), custom_call_target="tpu_custom_call" | custom-call | tf_op jit(solution)/shard_map/candidates/pallas_call | solution.py:167
  6.3 0.5 %collective-permute-start = (bf16[4,1024]{1,0:T(4,128)(2,1)S(1)}, bf16[4,1024]{1,0:T(4,128)(2,1)S(1)}, u32[]{:S(2)}, u32[]{:S(2)}) collective-permute-start(bf16[4,1024]{1,0:T(4,128)(2,1)S(1)} %get-tuple-element.23.after_ref.rest_0_), channel_id=1, source_target_pairs={{0,4},{1,5},{2,6},{3,7},{4,0},{5,1},{6,2},{7,3},{8,12},{9,13},{10,... | collective-permute-start | bytes 24584 | tf_op jit(solution)/shard_map/ppermute | solution.py:276
  6.8 1.2 %statistics.4 = (f32[1024,1]{1,0:T(8,128)S(1)}, f32[1024,1]{1,0:T(8,128)S(1)}, bf16[4096,1024]{1,0:T(8,128)(2,1)S(1)}) custom-call(bf16[4096,1024]{1,0:T(8,128)(2,1)S(1)} %get-tuple-element.24.refs_ref, bf16[4,1024]{1,0:T(4,128)(2,1)S(1)} %get-tuple-element.23.after_ref.rest_0_), custom_call_target="tpu_custom_call", output_to_operand_aliasing={{2}: (0, {})} | custom-call | flops 268435456 | bytes 2097152 | tf_op jit(solution)/shard_map/statistics/pallas_call | solution.py:207
  8.1 0.0 collective-permute-done.rest_1_
  8.1 2.6 %collective-permute-start.1 = (bf16[8,1024]{1,0:T(8,128)(2,1)S(1)}, bf16[8,1024]{1,0:T(8,128)(2,1)S(1)}, u32[]{:S(2)}, u32[]{:S(2)}) collective-permute-start(bf16[8,1024]{1,0:T(8,128)(2,1)S(1)} %pad_maximum_fusion.2.after_ref), channel_id=1, source_target_pairs={{0,8},{1,9},{2,10},{3,11},{4,12},{5,13},{6,14},{7,15},{8,0},{9,1},... | collective-permute-start | bytes 49160 | tf_op jit(solution)/shard_map/ppermute | solution.py:276
  10.7 1.2 %statistics.5 = (f32[1024,1]{1,0:T(8,128)S(1)}, f32[1024,1]{1,0:T(8,128)S(1)}, bf16[4096,1024]{1,0:T(8,128)(2,1)S(1)}) custom-call(bf16[4096,1024]{1,0:T(8,128)(2,1)S(1)} %get-tuple-element.27.refs_ref, bf16[8,1024]{1,0:T(8,128)(2,1)S(1)} %pad_maximum_fusion.2.after_ref), custom_call_target="tpu_custom_call", output_to_operand_aliasing={{2}: (0, {})} | custom-call | flops 268435456 | bytes 2097152 | tf_op jit(solution)/shard_map/statistics/pallas_call | solution.py:207
  11.9 0.5 %collective-permute-done.1.rest_2_ = bf16[8,1024]{1,0:T(8,128)(2,1)S(1)} collective-permute-done((bf16[8,1024]{1,0:T(8,128)(2,1)S(1)}, bf16[8,1024]{1,0:T(8,128)(2,1)S(1)}, u32[]{:S(2)}, u32[]{:S(2)}) %collective-permute-start.1) | collective-permute-done | bytes 16416 | tf_op jit(solution)/shard_map/ppermute | solution.py:276
  12.4 2.2 %collective-permute-start.2 = (bf16[16,1024]{1,0:T(8,128)(2,1)S(1)}, bf16[16,1024]{1,0:T(8,128)(2,1)S(1)}, u32[]{:S(2)}, u32[]{:S(2)}) collective-permute-start(bf16[16,1024]{1,0:T(8,128)(2,1)S(1)} %pad_maximum_fusion.1.after_ref), channel_id=1, source_target_pairs={{0,1},{1,0},{2,3},{3,2},{4,5},{5,4},{6,7},{7,6},{8,9},{9,8},{10,11... | collective-permute-start | bytes 98312 | tf_op jit(solution)/shard_map/ppermute | solution.py:276
  14.6 1.2 %statistics.6 = (f32[1024,1]{1,0:T(8,128)S(1)}, f32[1024,1]{1,0:T(8,128)S(1)}, bf16[4096,1024]{1,0:T(8,128)(2,1)S(1)}) custom-call(bf16[4096,1024]{1,0:T(8,128)(2,1)S(1)} %get-tuple-element.30.refs_ref, bf16[16,1024]{1,0:T(8,128)(2,1)S(1)} %pad_maximum_fusion.1.after_ref), custom_call_target="tpu_custom_call", output_to_operand_aliasing={{2}: (0, {})} | custom-call | flops 268435456 | bytes 2097152 | tf_op jit(solution)/shard_map/statistics/pallas_call | solution.py:207
  15.8 0.6 %collective-permute-done.2.rest_3_ = bf16[16,1024]{1,0:T(8,128)(2,1)S(1)} collective-permute-done((bf16[16,1024]{1,0:T(8,128)(2,1)S(1)}, bf16[16,1024]{1,0:T(8,128)(2,1)S(1)}, u32[]{:S(2)}, u32[]{:S(2)}) %collective-permute-start.2) | collective-permute-done | bytes 32800 | tf_op jit(solution)/shard_map/ppermute | solution.py:276
  16.5 3.1 %collective-permute-start.3 = (bf16[32,1024]{1,0:T(8,128)(2,1)S(1)}, bf16[32,1024]{1,0:T(8,128)(2,1)S(1)}, u32[]{:S(2)}, u32[]{:S(2)}) collective-permute-start(bf16[32,1024]{1,0:T(8,128)(2,1)S(1)} %pad_maximum_fusion.after_ref), channel_id=1, source_target_pairs={{0,2},{1,3},{2,0},{3,1},{4,6},{5,7},{6,4},{7,5},{8,10},{9,11},{10,... | collective-permute-start | bytes 196616 | tf_op jit(solution)/shard_map/ppermute | solution.py:276
  19.6 1.2 %statistics.7 = (f32[1024,1]{1,0:T(8,128)S(1)}, f32[1024,1]{1,0:T(8,128)S(1)}, bf16[4096,1024]{1,0:T(8,128)(2,1)S(1)}) custom-call(bf16[4096,1024]{1,0:T(8,128)(2,1)S(1)} %get-tuple-element.33.refs_ref, bf16[32,1024]{1,0:T(8,128)(2,1)S(1)} %pad_maximum_fusion.after_ref), custom_call_target="tpu_custom_call", output_to_operand_aliasing={{2}: (0, {})} | custom-call | flops 268435456 | bytes 2097152 | tf_op jit(solution)/shard_map/statistics/pallas_call | solution.py:207
  20.9 1.0 %collective-permute-done.3.rest_4_ = bf16[32,1024]{1,0:T(8,128)(2,1)S(1)} collective-permute-done((bf16[32,1024]{1,0:T(8,128)(2,1)S(1)}, bf16[32,1024]{1,0:T(8,128)(2,1)S(1)}, u32[]{:S(2)}, u32[]{:S(2)}) %collective-permute-start.3) | collective-permute-done | bytes 65568 | tf_op jit(solution)/shard_map/ppermute | solution.py:276
  21.9 3.6 %scores.1 = bf16[64,4096]{1,0:T(8,128)(2,1)} custom-call(bf16[4,1024]{1,0:T(4,128)(2,1)S(1)} %get-tuple-element.23.after_ref.rest_0_, bf16[4,1024]{1,0:T(4,128)(2,1)S(1)} %collective-permute-done.rest_1_, bf16[8,1024]{1,0:T(8,128)(2,1)S(1)} %collective-permute-done.1.rest_2_, bf16[16,1024]{1,0:T(8,128)(2,1)S(1)} %collective-permute-done.2.rest_3_, ...), custom_call_target="tpu_custom_call" | custom-call | tf_op jit(solution)/shard_map/scores/pallas_call | solution.py:255
  (3 shorter events, 0.1 us)
Async XLA Ops:
  6.3 1.8 %collective-permute-start = (bf16[4,1024]{1,0:T(4,128)(2,1)S(1)}, bf16[4,1024]{1,0:T(4,128)(2,1)S(1)}, u32[]{:S(2)}, u32[]{:S(2)}) collective-permute-start(bf16[4,1024]{1,0:T(4,128)(2,1)S(1)} %get-tuple-element.23.after_ref.rest_0_), channel_id=1, source_target_pairs={{0,4},{1,5},{2,6},{3,7},{4,0},{5,1},{6,2},{7,3},{8,12},{9,13},{10,... | collective-permute-start | bytes 24584 | tf_op jit(solution)/shard_map/ppermute | solution.py:276
  8.1 4.3 %collective-permute-start.1 = (bf16[8,1024]{1,0:T(8,128)(2,1)S(1)}, bf16[8,1024]{1,0:T(8,128)(2,1)S(1)}, u32[]{:S(2)}, u32[]{:S(2)}) collective-permute-start(bf16[8,1024]{1,0:T(8,128)(2,1)S(1)} %pad_maximum_fusion.2.after_ref), channel_id=1, source_target_pairs={{0,8},{1,9},{2,10},{3,11},{4,12},{5,13},{6,14},{7,15},{8,0},{9,1},... | collective-permute-start | bytes 49160 | tf_op jit(solution)/shard_map/ppermute | solution.py:276
  12.4 4.1 %collective-permute-start.2 = (bf16[16,1024]{1,0:T(8,128)(2,1)S(1)}, bf16[16,1024]{1,0:T(8,128)(2,1)S(1)}, u32[]{:S(2)}, u32[]{:S(2)}) collective-permute-start(bf16[16,1024]{1,0:T(8,128)(2,1)S(1)} %pad_maximum_fusion.1.after_ref), channel_id=1, source_target_pairs={{0,1},{1,0},{2,3},{3,2},{4,5},{5,4},{6,7},{7,6},{8,9},{9,8},{10,11... | collective-permute-start | bytes 98312 | tf_op jit(solution)/shard_map/ppermute | solution.py:276
  16.5 5.3 %collective-permute-start.3 = (bf16[32,1024]{1,0:T(8,128)(2,1)S(1)}, bf16[32,1024]{1,0:T(8,128)(2,1)S(1)}, u32[]{:S(2)}, u32[]{:S(2)}) collective-permute-start(bf16[32,1024]{1,0:T(8,128)(2,1)S(1)} %pad_maximum_fusion.after_ref), channel_id=1, source_target_pairs={{0,2},{1,3},{2,0},{3,1},{4,6},{5,7},{6,4},{7,5},{8,10},{9,11},{10,... | collective-permute-start | bytes 196616 | tf_op jit(solution)/shard_map/ppermute | solution.py:276

commit v3 on v2

--- a/solution.py
+++ b/solution.py
@@ -14,8 +14,8 @@
 NORMS = 256
 CHUNK = 512
 TILE = 128
-STAT_ROWS = 1024
 SCORE_ROWS = 512
+STAT_UNIT = 256
 VMEM_LIMIT = 24 << 20
 
 SIN_COEFS = (3.14158208, -5.1671442, 2.54190894, -0.55465711)
@@ -238,15 +238,14 @@
         cand, order, (((0,), (0,)), ((), ())), preferred_element_type=f32
     ).astype(bf16)
     sums = jnp.dot(jnp.ones((8, nbins), bf16), cand_t_ref[...], preferred_element_type=f32)[:1]
-    rows = mean_refs[0].shape[0]
-    for i in range(refs_ref.shape[0] // SCORE_ROWS):
-        start = i * SCORE_ROWS
-        piece, at = start // rows, slice(start % rows, start % rows + SCORE_ROWS)
-        product = jnp.dot(
-            refs_ref[start : start + SCORE_ROWS, :], cand_t_ref[...], preferred_element_type=f32
-        )
-        product = (product - mean_refs[piece][at, :] * sums) * scale_refs[piece][at, :]
-        out_ref[:, start : start + SCORE_ROWS] = product.T.astype(bf16)
+    means, scales = (
+        jnp.concatenate([ref[...] for ref in refs], axis=0) for refs in (mean_refs, scale_refs)
+    )
+    for start in range(0, refs_ref.shape[0], SCORE_ROWS):
+        rows = slice(start, start + SCORE_ROWS)
+        product = jnp.dot(refs_ref[rows, :], cand_t_ref[...], preferred_element_type=f32)
+        product = (product - means[rows] * sums) * scales[rows]
+        out_ref[:, rows] = product.T.astype(bf16)
 
 
 def score(ncand, masks, cands, refs, means, scales):
@@ -268,22 +267,26 @@
         coords, species, miller, offsets, form_amps, form_decay, ref_patterns
     )
     members = ndb * ncand
-    masks = [ncand << bit for bit in range(ndb.bit_length() - 1)]
-    masks += [1 << bit for bit in range(ncand.bit_length() - 1)]
+    core = ncand
+    masks = [core | ncand << bit for bit in range(1, ndb.bit_length() - 1)]
+    masks += [core | 1 << bit for bit in range(ncand.bit_length() - 1)]
+    masks.append(core)
+    share = -(-count * 5 // 16 // STAT_UNIT) * STAT_UNIT
     cands, means, scales = [held], [], []
-    for stage, mask in enumerate(masks):
-        pairs = [(i, i ^ mask) for i in range(members)]
-        other = lax.ppermute(held, ("db", "cand"), pairs)
-        first = len(means) * STAT_ROWS
-        if first < count:
-            mean, scale, refs = statistics(refs, first, STAT_ROWS, held)
+    first = 0
+    for mask in masks:
+        other = lax.ppermute(held, ("db", "cand"), [(i, i ^ mask) for i in range(members)])
+        rows = min(share, count - first)
+        if rows > 0:
+            mean, scale, refs = statistics(refs, first, rows, held)
             means.append(mean)
             scales.append(scale)
+            first += rows
             other, mean = lax.optimization_barrier((other, mean))
         cands.append(other)
         held = jnp.concatenate([held, other], axis=0)
-    for first in range(len(means) * STAT_ROWS, count, STAT_ROWS):
-        mean, scale, refs = statistics(refs, first, STAT_ROWS, held)
+    if first < count:
+        mean, scale, refs = statistics(refs, first, count - first, held)
         means.append(mean)
         scales.append(scale)
     return score(ncand, tuple(masks), cands, refs, means, scales)

time: 25.6 us -> 23.5 us (0.918)
  waiting for transfers between devices: 2.11 us -> 0.52 us
  starting transfers between devices: 8.35 us -> 7.65 us
    ppermute x4, waiting for transfers between devices: 2.11 us -> 0.52 us  [per_device(): lax.ppermute(held, ('db', 'cand'), [(i, i ^ mask) for i in range(members)])]
    ppermute x4, starting transfers between devices: 8.35 us -> 7.65 us  [per_device(): lax.ppermute(held, ('db', 'cand'), [(i, i ^ mask) for i in range(members)])]
  transfers between devices with their start and end apart: 4 -> 4, of which waited for: 3 -> 2; matrix products, arithmetic and copies ran while one was open for 0% -> 0% of each run, Pallas kernels for 19% -> 22%
where the time goes in v3:
time: 23.5 us; the launch traced here: 23.2 us
  Pallas kernels  14.9 us (63%)
  starting transfers between devices  7.65 us (33%)
  waiting for transfers between devices  0.52 us (2%)
    ppermute x4, starting transfers between devices, per_device(): lax.ppermute(held, ('db', 'cand'), [(i, i ^ mask) for i in range(members)])  7.65 us
    pallas_call x1, Pallas kernels, candidate_patterns(): pl.pallas_call(candidate_kernel, out_shape=[pltpu.VMEM((count, nbins), jn...  6.31 us
    pallas_call x4, Pallas kernels, statistics(): pl.pallas_call(functools.partial(statistics_kernel, first), out_shape=[pl...  5.01 us
    pallas_call x1, Pallas kernels, score(): pl.pallas_call(functools.partial(score_kernel, ncand, masks, len(means)),...  3.61 us
    ppermute x4, waiting for transfers between devices, per_device(): lax.ppermute(held, ('db', 'cand'), [(i, i ^ mask) for i in range(members)])  0.52 us
  transfers between devices with their start and end apart: 4, of which 2 were waited for; matrix products, arithmetic and copies ran while one was open for 0% of the time, Pallas kernels for 22%

profile of v3, /device:TPU:0, one launch (start us, length us, event | category | flops | bytes accessed | tf_op | source)
XLA Modules:
  0.0 23.2 jit_solution(14693232171734785738)
XLA Ops:
  0.0 6.3 %candidates.1 = (bf16[4,1024]{1,0:T(4,128)(2,1)S(1)}, bf16[4096,1024]{1,0:T(8,128)(2,1)S(1)}) custom-call(f32[3,4,64]{2,1,0:T(4,128)} %coords_hbm.1, s32[4,64]{1,0:T(4,128)} %species_hbm.1, s32[3,4096]{1,0:T(4,128)} %miller_hbm.1, s32[1,4096]{1,0:T(1,128)} %bitcast.3, f32[4,89]{1,0:T(4,128)} %bitcast.4, f32[4,89]{1,0:T(4,128)} %bitcast.5, ...), custom_call_target="tpu_custom_call" | custom-call | tf_op jit(solution)/shard_map/candidates/pallas_call | solution.py:167
  6.3 2.4 %collective-permute-start = (bf16[4,1024]{1,0:T(4,128)(2,1)S(1)}, bf16[4,1024]{1,0:T(4,128)(2,1)S(1)}, u32[]{:S(2)}, u32[]{:S(2)}) collective-permute-start(bf16[4,1024]{1,0:T(4,128)(2,1)S(1)} %get-tuple-element.23.after_ref.rest_0_), channel_id=1, source_target_pairs={{0,12},{1,13},{2,14},{3,15},{4,8},{5,9},{6,10},{7,11},{8,4},{9,5},... | collective-permute-start | bytes 24584 | tf_op jit(solution)/shard_map/ppermute | solution.py:278
  8.8 1.5 %statistics.4 = (f32[1280,1]{1,0:T(8,128)S(1)}, f32[1280,1]{1,0:T(8,128)S(1)}, bf16[4096,1024]{1,0:T(8,128)(2,1)S(1)}) custom-call(bf16[4096,1024]{1,0:T(8,128)(2,1)S(1)} %get-tuple-element.24.refs_ref, bf16[4,1024]{1,0:T(4,128)(2,1)S(1)} %get-tuple-element.23.after_ref.rest_0_), custom_call_target="tpu_custom_call", output_to_operand_aliasing={{2}: (0, {})} | custom-call | flops 335544320 | bytes 2621440 | tf_op jit(solution)/shard_map/statistics/pallas_call | solution.py:207
  10.3 0.0 collective-permute-done.rest_1_
  10.3 2.0 %collective-permute-start.1 = (bf16[8,1024]{1,0:T(8,128)(2,1)S(1)}, bf16[8,1024]{1,0:T(8,128)(2,1)S(1)}, u32[]{:S(2)}, u32[]{:S(2)}) collective-permute-start(bf16[8,1024]{1,0:T(8,128)(2,1)S(1)} %pad_maximum_fusion.2.after_ref), channel_id=1, source_target_pairs={{0,5},{1,4},{2,7},{3,6},{4,1},{5,0},{6,3},{7,2},{8,13},{9,12},{10,... | collective-permute-start | bytes 49160 | tf_op jit(solution)/shard_map/ppermute | solution.py:278
  12.3 1.5 %statistics.5 = (f32[1280,1]{1,0:T(8,128)S(1)}, f32[1280,1]{1,0:T(8,128)S(1)}, bf16[4096,1024]{1,0:T(8,128)(2,1)S(1)}) custom-call(bf16[4096,1024]{1,0:T(8,128)(2,1)S(1)} %get-tuple-element.27.refs_ref, bf16[8,1024]{1,0:T(8,128)(2,1)S(1)} %pad_maximum_fusion.2.after_ref), custom_call_target="tpu_custom_call", output_to_operand_aliasing={{2}: (0, {})} | custom-call | flops 335544320 | bytes 2621440 | tf_op jit(solution)/shard_map/statistics/pallas_call | solution.py:207
  13.9 0.0 collective-permute-done.1.rest_2_
  13.9 2.7 %collective-permute-start.2 = (bf16[16,1024]{1,0:T(8,128)(2,1)S(1)}, bf16[16,1024]{1,0:T(8,128)(2,1)S(1)}, u32[]{:S(2)}, u32[]{:S(2)}) collective-permute-start(bf16[16,1024]{1,0:T(8,128)(2,1)S(1)} %pad_maximum_fusion.1.after_ref), channel_id=1, source_target_pairs={{0,6},{1,7},{2,4},{3,5},{4,2},{5,3},{6,0},{7,1},{8,14},{9,15},{10,... | collective-permute-start | bytes 98312 | tf_op jit(solution)/shard_map/ppermute | solution.py:278
  16.6 1.5 %statistics.6 = (f32[1280,1]{1,0:T(8,128)S(1)}, f32[1280,1]{1,0:T(8,128)S(1)}, bf16[4096,1024]{1,0:T(8,128)(2,1)S(1)}) custom-call(bf16[4096,1024]{1,0:T(8,128)(2,1)S(1)} %get-tuple-element.30.refs_ref, bf16[16,1024]{1,0:T(8,128)(2,1)S(1)} %pad_maximum_fusion.1.after_ref), custom_call_target="tpu_custom_call", output_to_operand_aliasing={{2}: (0, {})} | custom-call | flops 335544320 | bytes 2621440 | tf_op jit(solution)/shard_map/statistics/pallas_call | solution.py:207
  18.1 0.1 collective-permute-done.2.rest_3_
  18.2 0.5 %collective-permute-start.3 = (bf16[32,1024]{1,0:T(8,128)(2,1)S(1)}, bf16[32,1024]{1,0:T(8,128)(2,1)S(1)}, u32[]{:S(2)}, u32[]{:S(2)}) collective-permute-start(bf16[32,1024]{1,0:T(8,128)(2,1)S(1)} %pad_maximum_fusion.after_ref), channel_id=1, source_target_pairs={{0,4},{1,5},{2,6},{3,7},{4,0},{5,1},{6,2},{7,3},{8,12},{9,13},{10,... | collective-permute-start | bytes 196616 | tf_op jit(solution)/shard_map/ppermute | solution.py:278
  18.7 0.5 %statistics.7 = (f32[256,1]{1,0:T(8,128)S(1)}, f32[256,1]{1,0:T(8,128)S(1)}, bf16[4096,1024]{1,0:T(8,128)(2,1)S(1)}) custom-call(bf16[4096,1024]{1,0:T(8,128)(2,1)S(1)} %get-tuple-element.33.refs_ref, bf16[32,1024]{1,0:T(8,128)(2,1)S(1)} %pad_maximum_fusion.after_ref), custom_call_target="tpu_custom_call", output_to_operand_aliasing={{2}: (0, {})} | custom-call | flops 67108864 | bytes 524288 | tf_op jit(solution)/shard_map/statistics/pallas_call | solution.py:207
  19.2 0.4 %collective-permute-done.3.rest_4_ = bf16[32,1024]{1,0:T(8,128)(2,1)S(1)} collective-permute-done((bf16[32,1024]{1,0:T(8,128)(2,1)S(1)}, bf16[32,1024]{1,0:T(8,128)(2,1)S(1)}, u32[]{:S(2)}, u32[]{:S(2)}) %collective-permute-start.3) | collective-permute-done | bytes 65568 | tf_op jit(solution)/shard_map/ppermute | solution.py:278
  19.6 3.6 %scores.1 = bf16[64,4096]{1,0:T(8,128)(2,1)} custom-call(bf16[4,1024]{1,0:T(4,128)(2,1)S(1)} %get-tuple-element.23.after_ref.rest_0_, bf16[4,1024]{1,0:T(4,128)(2,1)S(1)} %collective-permute-done.rest_1_, bf16[8,1024]{1,0:T(8,128)(2,1)S(1)} %collective-permute-done.1.rest_2_, bf16[16,1024]{1,0:T(8,128)(2,1)S(1)} %collective-permute-done.2.rest_3_, ...), custom_call_target="tpu_custom_call" | custom-call | tf_op jit(solution)/shard_map/scores/pallas_call | solution.py:254
  (3 shorter events, 0.1 us)
Async XLA Ops:
  6.3 4.0 %collective-permute-start = (bf16[4,1024]{1,0:T(4,128)(2,1)S(1)}, bf16[4,1024]{1,0:T(4,128)(2,1)S(1)}, u32[]{:S(2)}, u32[]{:S(2)}) collective-permute-start(bf16[4,1024]{1,0:T(4,128)(2,1)S(1)} %get-tuple-element.23.after_ref.rest_0_), channel_id=1, source_target_pairs={{0,12},{1,13},{2,14},{3,15},{4,8},{5,9},{6,10},{7,11},{8,4},{9,5},... | collective-permute-start | bytes 24584 | tf_op jit(solution)/shard_map/ppermute | solution.py:278
  10.3 3.5 %collective-permute-start.1 = (bf16[8,1024]{1,0:T(8,128)(2,1)S(1)}, bf16[8,1024]{1,0:T(8,128)(2,1)S(1)}, u32[]{:S(2)}, u32[]{:S(2)}) collective-permute-start(bf16[8,1024]{1,0:T(8,128)(2,1)S(1)} %pad_maximum_fusion.2.after_ref), channel_id=1, source_target_pairs={{0,5},{1,4},{2,7},{3,6},{4,1},{5,0},{6,3},{7,2},{8,13},{9,12},{10,... | collective-permute-start | bytes 49160 | tf_op jit(solution)/shard_map/ppermute | solution.py:278
  13.9 4.3 %collective-permute-start.2 = (bf16[16,1024]{1,0:T(8,128)(2,1)S(1)}, bf16[16,1024]{1,0:T(8,128)(2,1)S(1)}, u32[]{:S(2)}, u32[]{:S(2)}) collective-permute-start(bf16[16,1024]{1,0:T(8,128)(2,1)S(1)} %pad_maximum_fusion.1.after_ref), channel_id=1, source_target_pairs={{0,6},{1,7},{2,4},{3,5},{4,2},{5,3},{6,0},{7,1},{8,14},{9,15},{10,... | collective-permute-start | bytes 98312 | tf_op jit(solution)/shard_map/ppermute | solution.py:278
  18.2 1.4 %collective-permute-start.3 = (bf16[32,1024]{1,0:T(8,128)(2,1)S(1)}, bf16[32,1024]{1,0:T(8,128)(2,1)S(1)}, u32[]{:S(2)}, u32[]{:S(2)}) collective-permute-start(bf16[32,1024]{1,0:T(8,128)(2,1)S(1)} %pad_maximum_fusion.after_ref), channel_id=1, source_target_pairs={{0,4},{1,5},{2,6},{3,7},{4,0},{5,1},{6,2},{7,3},{8,12},{9,13},{10,... | collective-permute-start | bytes 196616 | tf_op jit(solution)/shard_map/ppermute | solution.py:278

commit v4 on v3

--- a/solution.py
+++ b/solution.py
@@ -11,14 +11,14 @@
 Q_SCALE = 0.0025
 PEAK_WIDTH = 0.5
 LANES = 128
-NORMS = 256
-CHUNK = 512
-TILE = 128
+SIDE = 9
+NORMS = 208
+CHUNK = 4096
 SCORE_ROWS = 512
 STAT_UNIT = 256
 VMEM_LIMIT = 24 << 20
 
-SIN_COEFS = (3.14158208, -5.1671442, 2.54190894, -0.55465711)
+SIN_COEFS = (3.14159258, -5.1677069, 2.55003164, -0.59804645, 0.07722225)
 COS_COEFS = (0.99999995, -4.93479286, 4.05841191, -1.33188016, 0.21969679)
 
 
@@ -37,7 +37,7 @@
     coords_hbm, species_hbm, miller_hbm, offsets_hbm, amps_hbm, decay_hbm, refs_hbm,
     out_ref, refs_ref,
     coords_ref, species_ref, miller_ref, offsets_ref, amps_ref, decay_ref,
-    places_ref, table_ref, spread_ref, sems,
+    grid_ref, spread_ref, sems,
 ):
     sources = (coords_hbm, species_hbm, miller_hbm, offsets_hbm, amps_hbm, decay_hbm, refs_hbm)
     targets = (coords_ref, species_ref, miller_ref, offsets_ref, amps_ref, decay_ref, refs_ref)
@@ -64,7 +64,24 @@
             piece = value.astype(bf16)
             value = value - piece.astype(f32)
             pieces.append(piece.astype(f32))
-    places_ref[...] = jnp.concatenate(pieces, axis=0).astype(bf16).T
+    places = jnp.concatenate(pieces, axis=0).astype(bf16).T
+
+    axis = lax.broadcasted_iota(jnp.int32, (9, 3 * LANES), 0) // 3
+    column = lax.broadcasted_iota(jnp.int32, (9, 3 * LANES), 1)
+    tile = column // LANES
+    point = column - tile * LANES
+    index1 = point // SIDE
+    index2 = point - index1 * SIDE
+    index2 = jnp.where(tile == 0, index2, -index2)
+    yz = jnp.where(axis == 1, index1, jnp.where(axis == 2, index2, 0))
+    indices = jnp.where(tile == 2, jnp.where(axis == 0, point, 0), yz)
+    turns = jnp.dot(places, indices.astype(f32).astype(bf16), preferred_element_type=f32)
+    u = turns - jnp.round(turns)
+    square = u * u
+    half_sin = u * horner(SIN_COEFS, square)
+    half_cos = horner(COS_COEFS, square)
+    cosine = 1.0 - 2.0 * (half_sin * half_sin)
+    sine = 2.0 * (half_sin * half_cos)
 
     norms = lax.broadcasted_iota(jnp.int32, (NORMS, kinds), 0).astype(f32) * Q_SCALE
     table = jnp.zeros((NORMS, kinds), f32)
@@ -75,42 +92,58 @@
     onehot = (
         lax.broadcasted_iota(jnp.int32, (kinds, flat), 0) == flat_lanes(species_ref[...])
     ).astype(f32).astype(bf16)
-    table_ref[...] = jnp.dot(
+    atom_table = jnp.dot(
         table.astype(bf16), onehot, preferred_element_type=f32
     ).astype(bf16).T
+    point = lax.broadcasted_iota(jnp.int32, (NORMS, LANES), 1)
+    index1 = point // SIDE
+    index2 = point - index1 * SIDE
+    rest = lax.broadcasted_iota(jnp.int32, (NORMS, LANES), 0) - index1 * index1 - index2 * index2
+    pick = jnp.concatenate(
+        [(rest == h0 * h0).astype(f32).astype(bf16) for h0 in range(SIDE)], axis=1
+    )
+    weight = jnp.dot(atom_table, pick, preferred_element_type=f32)
+
+    for c in range(count):
+        atom = slice(c * atoms, (c + 1) * atoms)
+        for h0 in range(SIDE):
+            w = weight[atom, h0 * LANES : (h0 + 1) * LANES]
+            w_cos = w * cosine[atom, 2 * LANES + h0 : 2 * LANES + h0 + 1]
+            w_sin = w * sine[atom, 2 * LANES + h0 : 2 * LANES + h0 + 1]
+            for minus in range(2):
+                cos12 = cosine[atom, minus * LANES : (minus + 1) * LANES]
+                sin12 = sine[atom, minus * LANES : (minus + 1) * LANES]
+                cc = jnp.sum(w_cos * cos12, axis=0, keepdims=True)
+                ss = jnp.sum(w_sin * sin12, axis=0, keepdims=True)
+                cs = jnp.sum(w_cos * sin12, axis=0, keepdims=True)
+                sc = jnp.sum(w_sin * cos12, axis=0, keepdims=True)
+                row = (minus * SIDE + h0) * count + c
+                real, imag = cc - ss, cs + sc
+                grid_ref[row : row + 1, :] = real * real + imag * imag
+                real, imag = cc + ss, cs - sc
+                row = row + 2 * SIDE * count
+                grid_ref[row : row + 1, :] = real * real + imag * imag
+    grid = grid_ref[...].astype(bf16)
+    group = lax.broadcasted_iota(jnp.int32, (4 * SIDE * count, CHUNK), 0) // count
 
     spread_ref[...] = jnp.zeros_like(spread_ref)
 
     def step(index, carry):
         cols = pl.ds(pl.multiple_of(index * CHUNK, CHUNK), CHUNK)
         miller = miller_ref[:, cols]
-        norm = jnp.sum(miller * miller, axis=0, keepdims=True)
-        hkl = miller.astype(f32)
-        hkl9 = jnp.concatenate(
-            [hkl[axis : axis + 1] for axis in range(3) for _ in range(3)], axis=0
-        ).astype(bf16)
-        turns = jnp.dot(places_ref[...], hkl9, preferred_element_type=f32)
-        pick = (
-            lax.broadcasted_iota(jnp.int32, (NORMS, CHUNK), 0) == norm
+        miller = jnp.where(miller[1:2] < 0, -miller, miller)
+        size = jnp.abs(miller)
+        signs = jnp.where(miller < 0, 1, 0)
+        place = size[1:2] * SIDE + size[2:3]
+        chosen = (2 * signs[0:1] + signs[2:3]) * SIDE + size[0:1]
+        at_place = (
+            lax.broadcasted_iota(jnp.int32, (LANES, CHUNK), 0) == place
         ).astype(f32).astype(bf16)
-        weight = jnp.dot(table_ref[...], pick, preferred_element_type=f32)
-        rows = []
-        for c in range(count):
-            tiles = []
-            for lane in range(0, CHUNK, TILE):
-                at = (slice(c * atoms, (c + 1) * atoms), slice(lane, lane + TILE))
-                t = turns[at]
-                w = weight[at]
-                u = t - jnp.round(t)
-                square = u * u
-                half_sin = u * horner(SIN_COEFS, square)
-                half_cos = horner(COS_COEFS, square)
-                part = w * half_sin
-                real = jnp.sum(w - 2.0 * (part * half_sin), axis=0, keepdims=True)
-                imag = 2.0 * jnp.sum(part * half_cos, axis=0, keepdims=True)
-                tiles.append(real * real + imag * imag)
-            rows.append(jnp.concatenate(tiles, axis=1))
-        intensity = jnp.concatenate(rows, axis=0).astype(bf16).astype(f32)
+        values = jnp.dot(grid, at_place, preferred_element_type=f32)
+        values = jnp.where(group == chosen, values, 0.0)
+        values = jnp.sum(values.reshape(-1, 8, CHUNK), axis=0)
+        intensity = jnp.sum(values.reshape(8 // count, count, CHUNK), axis=0)
+
         offset = offsets_ref[:, cols]
         block = offset // LANES
         routed = jnp.concatenate(
@@ -173,8 +206,7 @@
         in_specs=[pl.BlockSpec(memory_space=pltpu.HBM)] * len(args),
         scratch_shapes=[pltpu.VMEM(arg.shape, arg.dtype) for arg in args[:-1]]
         + [
-            pltpu.VMEM((count * atoms, 9), jnp.bfloat16),
-            pltpu.VMEM((count * atoms, NORMS), jnp.bfloat16),
+            pltpu.VMEM((4 * SIDE * count, LANES), jnp.float32),
             pltpu.VMEM((LANES, count * (nbins // LANES)), jnp.float32),
             pltpu.SemaphoreType.DMA((len(args),)),
         ],

time: 23.5 us -> 21.7 us (0.923)
  Pallas kernels: 14.9 us -> 13.1 us
    pallas_call x1, Pallas kernels: 6.31 us -> 4.52 us  [candidate_patterns(): pl.pallas_call(candidate_kernel, out_shape=[pltpu.VMEM((count, nbins), jn...]
  transfers between devices with their start and end apart: 4 -> 4, of which waited for: 2 -> 2; matrix products, arithmetic and copies ran while one was open for 0% -> 0% of each run, Pallas kernels for 22% -> 23%
where the time goes in v4:
time: 21.7 us; the launch traced here: 21.4 us
  Pallas kernels  13.1 us (60%)
  starting transfers between devices  7.63 us (35%)
  waiting for transfers between devices  0.53 us (2%)
    ppermute x4, starting transfers between devices, per_device(): lax.ppermute(held, ('db', 'cand'), [(i, i ^ mask) for i in range(members)])  7.63 us
    pallas_call x4, Pallas kernels, statistics(): pl.pallas_call(functools.partial(statistics_kernel, first), out_shape=[pl...  5.01 us
    pallas_call x1, Pallas kernels, candidate_patterns(): pl.pallas_call(candidate_kernel, out_shape=[pltpu.VMEM((count, nbins), jn...  4.52 us
    pallas_call x1, Pallas kernels, score(): pl.pallas_call(functools.partial(score_kernel, ncand, masks, len(means)),...  3.61 us
    ppermute x4, waiting for transfers between devices, per_device(): lax.ppermute(held, ('db', 'cand'), [(i, i ^ mask) for i in range(members)])  0.53 us
  transfers between devices with their start and end apart: 4, of which 2 were waited for; matrix products, arithmetic and copies ran while one was open for 0% of the time, Pallas kernels for 23%

profile of v4, /device:TPU:0, one launch (start us, length us, event | category | flops | bytes accessed | tf_op | source)
XLA Modules:
  0.0 21.4 jit_solution(7656090324882988088)
XLA Ops:
  0.0 4.5 %candidates.1 = (bf16[4,1024]{1,0:T(4,128)(2,1)S(1)}, bf16[4096,1024]{1,0:T(8,128)(2,1)S(1)}) custom-call(f32[3,4,64]{2,1,0:T(4,128)} %coords_hbm.1, s32[4,64]{1,0:T(4,128)} %species_hbm.1, s32[3,4096]{1,0:T(4,128)} %miller_hbm.1, s32[1,4096]{1,0:T(1,128)} %bitcast.3, f32[4,89]{1,0:T(4,128)} %bitcast.4, f32[4,89]{1,0:T(4,128)} %bitcast.5, ...), custom_call_target="tpu_custom_call" | custom-call | tf_op jit(solution)/shard_map/candidates/pallas_call | solution.py:200
  4.5 2.4 %collective-permute-start = (bf16[4,1024]{1,0:T(4,128)(2,1)S(1)}, bf16[4,1024]{1,0:T(4,128)(2,1)S(1)}, u32[]{:S(2)}, u32[]{:S(2)}) collective-permute-start(bf16[4,1024]{1,0:T(4,128)(2,1)S(1)} %get-tuple-element.23.after_ref.rest_0_), channel_id=1, source_target_pairs={{0,12},{1,13},{2,14},{3,15},{4,8},{5,9},{6,10},{7,11},{8,4},{9,5},... | collective-permute-start | bytes 24584 | tf_op jit(solution)/shard_map/ppermute | solution.py:310
  7.0 1.5 %statistics.4 = (f32[1280,1]{1,0:T(8,128)S(1)}, f32[1280,1]{1,0:T(8,128)S(1)}, bf16[4096,1024]{1,0:T(8,128)(2,1)S(1)}) custom-call(bf16[4096,1024]{1,0:T(8,128)(2,1)S(1)} %get-tuple-element.24.refs_ref, bf16[4,1024]{1,0:T(4,128)(2,1)S(1)} %get-tuple-element.23.after_ref.rest_0_), custom_call_target="tpu_custom_call", output_to_operand_aliasing={{2}: (0, {})} | custom-call | flops 335544320 | bytes 2621440 | tf_op jit(solution)/shard_map/statistics/pallas_call | solution.py:239
  8.5 0.0 collective-permute-done.rest_1_
  8.5 2.0 %collective-permute-start.1 = (bf16[8,1024]{1,0:T(8,128)(2,1)S(1)}, bf16[8,1024]{1,0:T(8,128)(2,1)S(1)}, u32[]{:S(2)}, u32[]{:S(2)}) collective-permute-start(bf16[8,1024]{1,0:T(8,128)(2,1)S(1)} %pad_maximum_fusion.2.after_ref), channel_id=1, source_target_pairs={{0,5},{1,4},{2,7},{3,6},{4,1},{5,0},{6,3},{7,2},{8,13},{9,12},{10,... | collective-permute-start | bytes 49160 | tf_op jit(solution)/shard_map/ppermute | solution.py:310
  10.5 1.5 %statistics.5 = (f32[1280,1]{1,0:T(8,128)S(1)}, f32[1280,1]{1,0:T(8,128)S(1)}, bf16[4096,1024]{1,0:T(8,128)(2,1)S(1)}) custom-call(bf16[4096,1024]{1,0:T(8,128)(2,1)S(1)} %get-tuple-element.27.refs_ref, bf16[8,1024]{1,0:T(8,128)(2,1)S(1)} %pad_maximum_fusion.2.after_ref), custom_call_target="tpu_custom_call", output_to_operand_aliasing={{2}: (0, {})} | custom-call | flops 335544320 | bytes 2621440 | tf_op jit(solution)/shard_map/statistics/pallas_call | solution.py:239
  12.1 0.0 collective-permute-done.1.rest_2_
  12.1 2.7 %collective-permute-start.2 = (bf16[16,1024]{1,0:T(8,128)(2,1)S(1)}, bf16[16,1024]{1,0:T(8,128)(2,1)S(1)}, u32[]{:S(2)}, u32[]{:S(2)}) collective-permute-start(bf16[16,1024]{1,0:T(8,128)(2,1)S(1)} %pad_maximum_fusion.1.after_ref), channel_id=1, source_target_pairs={{0,6},{1,7},{2,4},{3,5},{4,2},{5,3},{6,0},{7,1},{8,14},{9,15},{10,... | collective-permute-start | bytes 98312 | tf_op jit(solution)/shard_map/ppermute | solution.py:310
  14.8 1.5 %statistics.6 = (f32[1280,1]{1,0:T(8,128)S(1)}, f32[1280,1]{1,0:T(8,128)S(1)}, bf16[4096,1024]{1,0:T(8,128)(2,1)S(1)}) custom-call(bf16[4096,1024]{1,0:T(8,128)(2,1)S(1)} %get-tuple-element.30.refs_ref, bf16[16,1024]{1,0:T(8,128)(2,1)S(1)} %pad_maximum_fusion.1.after_ref), custom_call_target="tpu_custom_call", output_to_operand_aliasing={{2}: (0, {})} | custom-call | flops 335544320 | bytes 2621440 | tf_op jit(solution)/shard_map/statistics/pallas_call | solution.py:239
  16.3 0.1 collective-permute-done.2.rest_3_
  16.4 0.5 %collective-permute-start.3 = (bf16[32,1024]{1,0:T(8,128)(2,1)S(1)}, bf16[32,1024]{1,0:T(8,128)(2,1)S(1)}, u32[]{:S(2)}, u32[]{:S(2)}) collective-permute-start(bf16[32,1024]{1,0:T(8,128)(2,1)S(1)} %pad_maximum_fusion.after_ref), channel_id=1, source_target_pairs={{0,4},{1,5},{2,6},{3,7},{4,0},{5,1},{6,2},{7,3},{8,12},{9,13},{10,... | collective-permute-start | bytes 196616 | tf_op jit(solution)/shard_map/ppermute | solution.py:310
  16.9 0.5 %statistics.7 = (f32[256,1]{1,0:T(8,128)S(1)}, f32[256,1]{1,0:T(8,128)S(1)}, bf16[4096,1024]{1,0:T(8,128)(2,1)S(1)}) custom-call(bf16[4096,1024]{1,0:T(8,128)(2,1)S(1)} %get-tuple-element.33.refs_ref, bf16[32,1024]{1,0:T(8,128)(2,1)S(1)} %pad_maximum_fusion.after_ref), custom_call_target="tpu_custom_call", output_to_operand_aliasing={{2}: (0, {})} | custom-call | flops 67108864 | bytes 524288 | tf_op jit(solution)/shard_map/statistics/pallas_call | solution.py:239
  17.4 0.4 %collective-permute-done.3.rest_4_ = bf16[32,1024]{1,0:T(8,128)(2,1)S(1)} collective-permute-done((bf16[32,1024]{1,0:T(8,128)(2,1)S(1)}, bf16[32,1024]{1,0:T(8,128)(2,1)S(1)}, u32[]{:S(2)}, u32[]{:S(2)}) %collective-permute-start.3) | collective-permute-done | bytes 65568 | tf_op jit(solution)/shard_map/ppermute | solution.py:310
  17.8 3.6 %scores.1 = bf16[64,4096]{1,0:T(8,128)(2,1)} custom-call(bf16[4,1024]{1,0:T(4,128)(2,1)S(1)} %get-tuple-element.23.after_ref.rest_0_, bf16[4,1024]{1,0:T(4,128)(2,1)S(1)} %collective-permute-done.rest_1_, bf16[8,1024]{1,0:T(8,128)(2,1)S(1)} %collective-permute-done.1.rest_2_, bf16[16,1024]{1,0:T(8,128)(2,1)S(1)} %collective-permute-done.2.rest_3_, ...), custom_call_target="tpu_custom_call" | custom-call | tf_op jit(solution)/shard_map/scores/pallas_call | solution.py:286
  (3 shorter events, 0.1 us)
Async XLA Ops:
  4.5 4.0 %collective-permute-start = (bf16[4,1024]{1,0:T(4,128)(2,1)S(1)}, bf16[4,1024]{1,0:T(4,128)(2,1)S(1)}, u32[]{:S(2)}, u32[]{:S(2)}) collective-permute-start(bf16[4,1024]{1,0:T(4,128)(2,1)S(1)} %get-tuple-element.23.after_ref.rest_0_), channel_id=1, source_target_pairs={{0,12},{1,13},{2,14},{3,15},{4,8},{5,9},{6,10},{7,11},{8,4},{9,5},... | collective-permute-start | bytes 24584 | tf_op jit(solution)/shard_map/ppermute | solution.py:310
  8.5 3.5 %collective-permute-start.1 = (bf16[8,1024]{1,0:T(8,128)(2,1)S(1)}, bf16[8,1024]{1,0:T(8,128)(2,1)S(1)}, u32[]{:S(2)}, u32[]{:S(2)}) collective-permute-start(bf16[8,1024]{1,0:T(8,128)(2,1)S(1)} %pad_maximum_fusion.2.after_ref), channel_id=1, source_target_pairs={{0,5},{1,4},{2,7},{3,6},{4,1},{5,0},{6,3},{7,2},{8,13},{9,12},{10,... | collective-permute-start | bytes 49160 | tf_op jit(solution)/shard_map/ppermute | solution.py:310
  12.1 4.3 %collective-permute-start.2 = (bf16[16,1024]{1,0:T(8,128)(2,1)S(1)}, bf16[16,1024]{1,0:T(8,128)(2,1)S(1)}, u32[]{:S(2)}, u32[]{:S(2)}) collective-permute-start(bf16[16,1024]{1,0:T(8,128)(2,1)S(1)} %pad_maximum_fusion.1.after_ref), channel_id=1, source_target_pairs={{0,6},{1,7},{2,4},{3,5},{4,2},{5,3},{6,0},{7,1},{8,14},{9,15},{10,... | collective-permute-start | bytes 98312 | tf_op jit(solution)/shard_map/ppermute | solution.py:310
  16.4 1.4 %collective-permute-start.3 = (bf16[32,1024]{1,0:T(8,128)(2,1)S(1)}, bf16[32,1024]{1,0:T(8,128)(2,1)S(1)}, u32[]{:S(2)}, u32[]{:S(2)}) collective-permute-start(bf16[32,1024]{1,0:T(8,128)(2,1)S(1)} %pad_maximum_fusion.after_ref), channel_id=1, source_target_pairs={{0,4},{1,5},{2,6},{3,7},{4,0},{5,1},{6,2},{7,3},{8,12},{9,13},{10,... | collective-permute-start | bytes 196616 | tf_op jit(solution)/shard_map/ppermute | solution.py:310

commit v5 on v4

--- a/solution.py
+++ b/solution.py
@@ -16,6 +16,7 @@
 CHUNK = 4096
 SCORE_ROWS = 512
 STAT_UNIT = 256
+STAT_STEP = 256
 VMEM_LIMIT = 24 << 20
 
 SIN_COEFS = (3.14159258, -5.1677069, 2.55003164, -0.59804645, 0.07722225)
@@ -47,8 +48,6 @@
     ]
     for copy in copies:
         copy.start()
-    for copy in copies[:-1]:
-        copy.wait()
     f32, bf16 = jnp.float32, jnp.bfloat16
     count, atoms = species_ref.shape
     kinds = amps_ref.shape[1]
@@ -57,14 +56,6 @@
     nblocks = nbins // LANES
     flat = count * atoms
 
-    pieces = []
-    for axis in range(3):
-        value = flat_lanes(coords_ref[axis])
-        for _ in range(3):
-            piece = value.astype(bf16)
-            value = value - piece.astype(f32)
-            pieces.append(piece.astype(f32))
-    places = jnp.concatenate(pieces, axis=0).astype(bf16).T
 
     axis = lax.broadcasted_iota(jnp.int32, (9, 3 * LANES), 0) // 3
     column = lax.broadcasted_iota(jnp.int32, (9, 3 * LANES), 1)
@@ -75,7 +66,34 @@
     index2 = jnp.where(tile == 0, index2, -index2)
     yz = jnp.where(axis == 1, index1, jnp.where(axis == 2, index2, 0))
     indices = jnp.where(tile == 2, jnp.where(axis == 0, point, 0), yz)
-    turns = jnp.dot(places, indices.astype(f32).astype(bf16), preferred_element_type=f32)
+    indices = indices.astype(f32).astype(bf16)
+
+    point = lax.broadcasted_iota(jnp.int32, (NORMS, LANES), 1)
+    index1 = point // SIDE
+    index2 = point - index1 * SIDE
+    rest = lax.broadcasted_iota(jnp.int32, (NORMS, LANES), 0) - index1 * index1 - index2 * index2
+    pick = jnp.concatenate(
+        [(rest == h0 * h0).astype(f32).astype(bf16) for h0 in range(SIDE)], axis=1
+    )
+
+    centre = lax.broadcasted_iota(jnp.int32, (LANES, 2 * LANES), 0)
+    bins = lax.broadcasted_iota(jnp.int32, (LANES, 2 * LANES), 1)
+    bins = jnp.where(bins < LANES + LANES // 2, bins, bins - 2 * LANES)
+    distance = (bins - centre).astype(f32) * (1.0 / PEAK_WIDTH)
+    profile = jnp.exp(-0.5 * distance * distance).astype(bf16)
+
+    for copy in copies[:2] + copies[4:6]:
+        copy.wait()
+    pieces = []
+    for axis in range(3):
+        value = flat_lanes(coords_ref[axis])
+        for _ in range(3):
+            piece = value.astype(bf16)
+            value = value - piece.astype(f32)
+            pieces.append(piece.astype(f32))
+    places = jnp.concatenate(pieces, axis=0).astype(bf16).T
+
+    turns = jnp.dot(places, indices, preferred_element_type=f32)
     u = turns - jnp.round(turns)
     square = u * u
     half_sin = u * horner(SIN_COEFS, square)
@@ -95,15 +113,9 @@
     atom_table = jnp.dot(
         table.astype(bf16), onehot, preferred_element_type=f32
     ).astype(bf16).T
-    point = lax.broadcasted_iota(jnp.int32, (NORMS, LANES), 1)
-    index1 = point // SIDE
-    index2 = point - index1 * SIDE
-    rest = lax.broadcasted_iota(jnp.int32, (NORMS, LANES), 0) - index1 * index1 - index2 * index2
-    pick = jnp.concatenate(
-        [(rest == h0 * h0).astype(f32).astype(bf16) for h0 in range(SIDE)], axis=1
-    )
     weight = jnp.dot(atom_table, pick, preferred_element_type=f32)
 
+    points = 2 * SIDE * count
     for c in range(count):
         atom = slice(c * atoms, (c + 1) * atoms)
         for h0 in range(SIDE):
@@ -113,19 +125,21 @@
             for minus in range(2):
                 cos12 = cosine[atom, minus * LANES : (minus + 1) * LANES]
                 sin12 = sine[atom, minus * LANES : (minus + 1) * LANES]
-                cc = jnp.sum(w_cos * cos12, axis=0, keepdims=True)
-                ss = jnp.sum(w_sin * sin12, axis=0, keepdims=True)
-                cs = jnp.sum(w_cos * sin12, axis=0, keepdims=True)
-                sc = jnp.sum(w_sin * cos12, axis=0, keepdims=True)
-                row = (minus * SIDE + h0) * count + c
-                real, imag = cc - ss, cs + sc
-                grid_ref[row : row + 1, :] = real * real + imag * imag
-                real, imag = cc + ss, cs - sc
-                row = row + 2 * SIDE * count
-                grid_ref[row : row + 1, :] = real * real + imag * imag
-    grid = grid_ref[...].astype(bf16)
+                terms = (w_cos * cos12, w_sin * sin12, w_cos * sin12, w_sin * cos12)
+                for i, term in enumerate(terms):
+                    row = (i * points + (minus * SIDE + h0) * count + c) * 8
+                    grid_ref[row : row + 8, :] = jnp.sum(term.reshape(-1, 8, LANES), axis=0)
+    cc, ss, cs, sc = (
+        sum(grid_ref[pl.ds(i * points * 8 + j, points, stride=8), :] for j in range(8))
+        for i in range(4)
+    )
+    plus = (cc - ss) * (cc - ss) + (cs + sc) * (cs + sc)
+    minus = (cc + ss) * (cc + ss) + (cs - sc) * (cs - sc)
+    grid = jnp.concatenate([plus, minus], axis=0).astype(bf16)
     group = lax.broadcasted_iota(jnp.int32, (4 * SIDE * count, CHUNK), 0) // count
 
+    for copy in copies[2:4]:
+        copy.wait()
     spread_ref[...] = jnp.zeros_like(spread_ref)
 
     def step(index, carry):
@@ -165,11 +179,6 @@
         piece = sums.astype(bf16)
         sums = sums - piece.astype(f32)
         pieces.append(piece.astype(f32))
-    centre = lax.broadcasted_iota(jnp.int32, (LANES, 2 * LANES), 0)
-    bins = lax.broadcasted_iota(jnp.int32, (LANES, 2 * LANES), 1)
-    bins = jnp.where(bins < LANES + LANES // 2, bins, bins - 2 * LANES)
-    distance = (bins - centre).astype(f32) * (1.0 / PEAK_WIDTH)
-    profile = jnp.exp(-0.5 * distance * distance).astype(bf16)
     peaks = jnp.dot(
         jnp.concatenate(pieces, axis=0).astype(bf16), profile, preferred_element_type=f32
     )
@@ -206,7 +215,7 @@
         in_specs=[pl.BlockSpec(memory_space=pltpu.HBM)] * len(args),
         scratch_shapes=[pltpu.VMEM(arg.shape, arg.dtype) for arg in args[:-1]]
         + [
-            pltpu.VMEM((4 * SIDE * count, LANES), jnp.float32),
+            pltpu.VMEM((8 * 8 * SIDE * count, LANES), jnp.float32),
             pltpu.VMEM((LANES, count * (nbins // LANES)), jnp.float32),
             pltpu.SemaphoreType.DMA((len(args),)),
         ],
@@ -222,16 +231,18 @@
     f32 = jnp.float32
     nbins = refs_ref.shape[1]
     rows = mean_ref.shape[0]
-    ones = jnp.ones((nbins, LANES), jnp.bfloat16)
-    block = refs_ref[first : first + rows, :]
-    mean = jnp.dot(block, ones, preferred_element_type=f32) * (1.0 / nbins)
-    total = jnp.zeros((rows, LANES), f32)
-    for lane in range(0, nbins, LANES):
-        centered = block[:, lane : lane + LANES].astype(f32) - mean
-        total = total + centered * centered
-    variance = jnp.sum(total, axis=1, keepdims=True) * (1.0 / nbins)
-    mean_ref[...] = mean[:, :1]
-    scale_ref[...] = lax.rsqrt(variance + EPSILON) * (1.0 / nbins**0.5)
+    for at in range(first, first + rows, STAT_STEP):
+        tiles = [
+            refs_ref[at : at + STAT_STEP, lane : lane + LANES].astype(f32)
+            for lane in range(0, nbins, LANES)
+        ]
+        mean = jnp.sum(sum(tiles[1:], tiles[0]), axis=1, keepdims=True) * (1.0 / nbins)
+        total = jnp.zeros((STAT_STEP, LANES), f32)
+        for tile in tiles:
+            total = total + (tile - mean) * (tile - mean)
+        variance = jnp.sum(total, axis=1, keepdims=True) * (1.0 / nbins)
+        mean_ref[at - first : at - first + STAT_STEP, :] = mean
+        scale_ref[at - first : at - first + STAT_STEP, :] = lax.rsqrt(variance + EPSILON) * (1.0 / nbins**0.5)
 
 
 def statistics(refs, first, rows, after):
@@ -253,7 +264,7 @@
 def score_kernel(ncand, masks, npieces, *rest):
     cand_refs, (refs_ref, *rest) = rest[: len(masks) + 1], rest[len(masks) + 1 :]
     mean_refs, scale_refs = rest[:npieces], rest[npieces : 2 * npieces]
-    out_ref, cand_t_ref = rest[2 * npieces :]
+    out_ref, cand_t_ref, held_ref, sems = rest[2 * npieces :]
     f32, bf16 = jnp.float32, jnp.bfloat16
     cand = jnp.concatenate([ref[...] for ref in cand_refs], axis=0)
     total, nbins = cand.shape
@@ -273,11 +284,17 @@
     means, scales = (
         jnp.concatenate([ref[...] for ref in refs], axis=0) for refs in (mean_refs, scale_refs)
     )
-    for start in range(0, refs_ref.shape[0], SCORE_ROWS):
+    copies = []
+    for i, start in enumerate(range(0, refs_ref.shape[0], SCORE_ROWS)):
         rows = slice(start, start + SCORE_ROWS)
         product = jnp.dot(refs_ref[rows, :], cand_t_ref[...], preferred_element_type=f32)
         product = (product - means[rows] * sums) * scales[rows]
-        out_ref[:, rows] = product.T.astype(bf16)
+        held_ref[:, rows] = product.T.astype(bf16)
+        copy = pltpu.make_async_copy(held_ref.at[:, rows], out_ref.at[:, rows], sems.at[i])
+        copy.start()
+        copies.append(copy)
+    for copy in copies:
+        copy.wait()
 
 
 def score(ncand, masks, cands, refs, means, scales):
@@ -287,7 +304,12 @@
         functools.partial(score_kernel, ncand, masks, len(means)),
         out_shape=jax.ShapeDtypeStruct((total, count), jnp.bfloat16),
         in_specs=[VMEM_WHOLE] * (len(cands) + 1 + 2 * len(means)),
-        scratch_shapes=[pltpu.VMEM((nbins, total), jnp.bfloat16)],
+        out_specs=pl.BlockSpec(memory_space=pltpu.HBM),
+        scratch_shapes=[
+            pltpu.VMEM((nbins, total), jnp.bfloat16),
+            pltpu.VMEM((total, count), jnp.bfloat16),
+            pltpu.SemaphoreType.DMA((count // SCORE_ROWS,)),
+        ],
         compiler_params=pltpu.CompilerParams(vmem_limit_bytes=VMEM_LIMIT),
         name="scores",
     )(*cands, pltpu.with_memory_space_constraint(refs, pltpu.VMEM), *means, *scales)

time: 21.7 us -> 21.2 us (0.977)
  Pallas kernels: 13.1 us -> 11.7 us
  waiting for transfers between devices: 0.53 us -> 1.25 us
  starting transfers between devices: 7.63 us -> 7.89 us
    pallas_call x4, Pallas kernels: 5.01 us -> 4.04 us  [statistics(): pl.pallas_call(functools.partial(statistics_kernel, first), out_shape=[pl...]
    ppermute x4, waiting for transfers between devices: 0.53 us -> 1.25 us  [per_device(): lax.ppermute(held, ('db', 'cand'), [(i, i ^ mask) for i in range(members)])]
    pallas_call x1, Pallas kernels: 4.52 us -> 4.12 us  [candidate_patterns(): pl.pallas_call(candidate_kernel, out_shape=[pltpu.VMEM((count, nbins), jn...]
    ppermute x4, starting transfers between devices: 7.63 us -> 7.89 us  [per_device(): lax.ppermute(held, ('db', 'cand'), [(i, i ^ mask) for i in range(members)])]
  transfers between devices with their start and end apart: 4 -> 4, of which waited for: 2 -> 4; matrix products, arithmetic and copies ran while one was open for 0% -> 0% of each run, Pallas kernels for 23% -> 19%
where the time goes in v5:
time: 21.2 us; the launch traced here: 20.9 us
  Pallas kernels  11.7 us (55%)
  starting transfers between devices  7.89 us (37%)
  waiting for transfers between devices  1.25 us (6%)
    ppermute x4, starting transfers between devices, per_device(): lax.ppermute(held, ('db', 'cand'), [(i, i ^ mask) for i in range(members)])  7.89 us
    pallas_call x1, Pallas kernels, candidate_patterns(): pl.pallas_call(candidate_kernel, out_shape=[pltpu.VMEM((count, nbins), jn...  4.12 us
    pallas_call x4, Pallas kernels, statistics(): pl.pallas_call(functools.partial(statistics_kernel, first), out_shape=[pl...  4.04 us
    pallas_call x1, Pallas kernels, score(): pl.pallas_call(functools.partial(score_kernel, ncand, masks, len(means)),...  3.52 us
    ppermute x4, waiting for transfers between devices, per_device(): lax.ppermute(held, ('db', 'cand'), [(i, i ^ mask) for i in range(members)])  1.25 us
  transfers between devices with their start and end apart: 4, of which 4 were waited for; matrix products, arithmetic and copies ran while one was open for 0% of the time, Pallas kernels for 19%

profile of v5, /device:TPU:0, one launch (start us, length us, event | category | flops | bytes accessed | tf_op | source)
XLA Modules:
  0.0 20.9 jit_solution(12591227822008013196)
XLA Ops:
  0.0 4.1 %candidates.1 = (bf16[4,1024]{1,0:T(4,128)(2,1)S(1)}, bf16[4096,1024]{1,0:T(8,128)(2,1)S(1)}) custom-call(f32[3,4,64]{2,1,0:T(4,128)} %coords_hbm.1, s32[4,64]{1,0:T(4,128)} %species_hbm.1, s32[3,4096]{1,0:T(4,128)} %miller_hbm.1, s32[1,4096]{1,0:T(1,128)} %bitcast.3, f32[4,89]{1,0:T(4,128)} %bitcast.4, f32[4,89]{1,0:T(4,128)} %bitcast.5, ...), custom_call_target="tpu_custom_call" | custom-call | tf_op jit(solution)/shard_map/candidates/pallas_call | solution.py:209
  4.1 2.4 %collective-permute-start = (bf16[4,1024]{1,0:T(4,128)(2,1)S(1)}, bf16[4,1024]{1,0:T(4,128)(2,1)S(1)}, u32[]{:S(2)}, u32[]{:S(2)}) collective-permute-start(bf16[4,1024]{1,0:T(4,128)(2,1)S(1)} %get-tuple-element.23.after_ref.rest_0_), channel_id=1, source_target_pairs={{0,12},{1,13},{2,14},{3,15},{4,8},{5,9},{6,10},{7,11},{8,4},{9,5},... | collective-permute-start | bytes 24584 | tf_op jit(solution)/shard_map/ppermute | solution.py:332
  6.6 1.2 %statistics.4 = (f32[1280,1]{1,0:T(8,128)S(1)}, f32[1280,1]{1,0:T(8,128)S(1)}, bf16[4096,1024]{1,0:T(8,128)(2,1)S(1)}) custom-call(bf16[4096,1024]{1,0:T(8,128)(2,1)S(1)} %get-tuple-element.24.refs_ref, bf16[4,1024]{1,0:T(4,128)(2,1)S(1)} %get-tuple-element.23.after_ref.rest_0_), custom_call_target="tpu_custom_call", output_to_operand_aliasing={{2}: (0, {})} | custom-call | flops 335544320 | bytes 2621440 | tf_op jit(solution)/shard_map/statistics/pallas_call | solution.py:250
  7.8 0.1 collective-permute-done.rest_1_
  8.0 2.2 %collective-permute-start.1 = (bf16[8,1024]{1,0:T(8,128)(2,1)S(1)}, bf16[8,1024]{1,0:T(8,128)(2,1)S(1)}, u32[]{:S(2)}, u32[]{:S(2)}) collective-permute-start(bf16[8,1024]{1,0:T(8,128)(2,1)S(1)} %pad_maximum_fusion.2.after_ref), channel_id=1, source_target_pairs={{0,5},{1,4},{2,7},{3,6},{4,1},{5,0},{6,3},{7,2},{8,13},{9,12},{10,... | collective-permute-start | bytes 49160 | tf_op jit(solution)/shard_map/ppermute | solution.py:332
  10.1 1.2 %statistics.5 = (f32[1280,1]{1,0:T(8,128)S(1)}, f32[1280,1]{1,0:T(8,128)S(1)}, bf16[4096,1024]{1,0:T(8,128)(2,1)S(1)}) custom-call(bf16[4096,1024]{1,0:T(8,128)(2,1)S(1)} %get-tuple-element.27.refs_ref, bf16[8,1024]{1,0:T(8,128)(2,1)S(1)} %pad_maximum_fusion.2.after_ref), custom_call_target="tpu_custom_call", output_to_operand_aliasing={{2}: (0, {})} | custom-call | flops 335544320 | bytes 2621440 | tf_op jit(solution)/shard_map/statistics/pallas_call | solution.py:250
  11.4 0.2 collective-permute-done.1.rest_2_
  11.6 2.8 %collective-permute-start.2 = (bf16[16,1024]{1,0:T(8,128)(2,1)S(1)}, bf16[16,1024]{1,0:T(8,128)(2,1)S(1)}, u32[]{:S(2)}, u32[]{:S(2)}) collective-permute-start(bf16[16,1024]{1,0:T(8,128)(2,1)S(1)} %pad_maximum_fusion.1.after_ref), channel_id=1, source_target_pairs={{0,6},{1,7},{2,4},{3,5},{4,2},{5,3},{6,0},{7,1},{8,14},{9,15},{10,... | collective-permute-start | bytes 98312 | tf_op jit(solution)/shard_map/ppermute | solution.py:332
  14.4 1.2 %statistics.6 = (f32[1280,1]{1,0:T(8,128)S(1)}, f32[1280,1]{1,0:T(8,128)S(1)}, bf16[4096,1024]{1,0:T(8,128)(2,1)S(1)}) custom-call(bf16[4096,1024]{1,0:T(8,128)(2,1)S(1)} %get-tuple-element.30.refs_ref, bf16[16,1024]{1,0:T(8,128)(2,1)S(1)} %pad_maximum_fusion.1.after_ref), custom_call_target="tpu_custom_call", output_to_operand_aliasing={{2}: (0, {})} | custom-call | flops 335544320 | bytes 2621440 | tf_op jit(solution)/shard_map/statistics/pallas_call | solution.py:250
  15.7 0.3 %collective-permute-done.2.rest_3_ = bf16[16,1024]{1,0:T(8,128)(2,1)S(1)} collective-permute-done((bf16[16,1024]{1,0:T(8,128)(2,1)S(1)}, bf16[16,1024]{1,0:T(8,128)(2,1)S(1)}, u32[]{:S(2)}, u32[]{:S(2)}) %collective-permute-start.2) | collective-permute-done | bytes 32800 | tf_op jit(solution)/shard_map/ppermute | solution.py:332
  16.0 0.5 %collective-permute-start.3 = (bf16[32,1024]{1,0:T(8,128)(2,1)S(1)}, bf16[32,1024]{1,0:T(8,128)(2,1)S(1)}, u32[]{:S(2)}, u32[]{:S(2)}) collective-permute-start(bf16[32,1024]{1,0:T(8,128)(2,1)S(1)} %pad_maximum_fusion.after_ref), channel_id=1, source_target_pairs={{0,4},{1,5},{2,6},{3,7},{4,0},{5,1},{6,2},{7,3},{8,12},{9,13},{10,... | collective-permute-start | bytes 196616 | tf_op jit(solution)/shard_map/ppermute | solution.py:332
  16.5 0.3 %statistics.7 = (f32[256,1]{1,0:T(8,128)S(1)}, f32[256,1]{1,0:T(8,128)S(1)}, bf16[4096,1024]{1,0:T(8,128)(2,1)S(1)}) custom-call(bf16[4096,1024]{1,0:T(8,128)(2,1)S(1)} %get-tuple-element.33.refs_ref, bf16[32,1024]{1,0:T(8,128)(2,1)S(1)} %pad_maximum_fusion.after_ref), custom_call_target="tpu_custom_call", output_to_operand_aliasing={{2}: (0, {})} | custom-call | flops 67108864 | bytes 524288 | tf_op jit(solution)/shard_map/statistics/pallas_call | solution.py:250
  16.8 0.6 %collective-permute-done.3.rest_4_ = bf16[32,1024]{1,0:T(8,128)(2,1)S(1)} collective-permute-done((bf16[32,1024]{1,0:T(8,128)(2,1)S(1)}, bf16[32,1024]{1,0:T(8,128)(2,1)S(1)}, u32[]{:S(2)}, u32[]{:S(2)}) %collective-permute-start.3) | collective-permute-done | bytes 65568 | tf_op jit(solution)/shard_map/ppermute | solution.py:332
  17.4 3.5 %scores.1 = bf16[64,4096]{1,0:T(8,128)(2,1)} custom-call(bf16[4,1024]{1,0:T(4,128)(2,1)S(1)} %get-tuple-element.23.after_ref.rest_0_, bf16[4,1024]{1,0:T(4,128)(2,1)S(1)} %collective-permute-done.rest_1_, bf16[8,1024]{1,0:T(8,128)(2,1)S(1)} %collective-permute-done.1.rest_2_, bf16[16,1024]{1,0:T(8,128)(2,1)S(1)} %collective-permute-done.2.rest_3_, ...), custom_call_target="tpu_custom_call" | custom-call | tf_op jit(solution)/shard_map/scores/pallas_call | solution.py:303
  (3 shorter events, 0.1 us)
Async XLA Ops:
  4.1 3.8 %collective-permute-start = (bf16[4,1024]{1,0:T(4,128)(2,1)S(1)}, bf16[4,1024]{1,0:T(4,128)(2,1)S(1)}, u32[]{:S(2)}, u32[]{:S(2)}) collective-permute-start(bf16[4,1024]{1,0:T(4,128)(2,1)S(1)} %get-tuple-element.23.after_ref.rest_0_), channel_id=1, source_target_pairs={{0,12},{1,13},{2,14},{3,15},{4,8},{5,9},{6,10},{7,11},{8,4},{9,5},... | collective-permute-start | bytes 24584 | tf_op jit(solution)/shard_map/ppermute | solution.py:332
  8.0 3.6 %collective-permute-start.1 = (bf16[8,1024]{1,0:T(8,128)(2,1)S(1)}, bf16[8,1024]{1,0:T(8,128)(2,1)S(1)}, u32[]{:S(2)}, u32[]{:S(2)}) collective-permute-start(bf16[8,1024]{1,0:T(8,128)(2,1)S(1)} %pad_maximum_fusion.2.after_ref), channel_id=1, source_target_pairs={{0,5},{1,4},{2,7},{3,6},{4,1},{5,0},{6,3},{7,2},{8,13},{9,12},{10,... | collective-permute-start | bytes 49160 | tf_op jit(solution)/shard_map/ppermute | solution.py:332
  11.6 4.4 %collective-permute-start.2 = (bf16[16,1024]{1,0:T(8,128)(2,1)S(1)}, bf16[16,1024]{1,0:T(8,128)(2,1)S(1)}, u32[]{:S(2)}, u32[]{:S(2)}) collective-permute-start(bf16[16,1024]{1,0:T(8,128)(2,1)S(1)} %pad_maximum_fusion.1.after_ref), channel_id=1, source_target_pairs={{0,6},{1,7},{2,4},{3,5},{4,2},{5,3},{6,0},{7,1},{8,14},{9,15},{10,... | collective-permute-start | bytes 98312 | tf_op jit(solution)/shard_map/ppermute | solution.py:332
  16.0 1.4 %collective-permute-start.3 = (bf16[32,1024]{1,0:T(8,128)(2,1)S(1)}, bf16[32,1024]{1,0:T(8,128)(2,1)S(1)}, u32[]{:S(2)}, u32[]{:S(2)}) collective-permute-start(bf16[32,1024]{1,0:T(8,128)(2,1)S(1)} %pad_maximum_fusion.after_ref), channel_id=1, source_target_pairs={{0,4},{1,5},{2,6},{3,7},{4,0},{5,1},{6,2},{7,3},{8,12},{9,13},{10,... | collective-permute-start | bytes 196616 | tf_op jit(solution)/shard_map/ppermute | solution.py:332

commit v6 on v5

--- a/solution.py
+++ b/solution.py
@@ -12,6 +12,7 @@
 PEAK_WIDTH = 0.5
 LANES = 128
 SIDE = 9
+POINTS = 96
 NORMS = 208
 CHUNK = 4096
 SCORE_ROWS = 512
@@ -151,17 +152,25 @@
         place = size[1:2] * SIDE + size[2:3]
         chosen = (2 * signs[0:1] + signs[2:3]) * SIDE + size[0:1]
         at_place = (
-            lax.broadcasted_iota(jnp.int32, (LANES, CHUNK), 0) == place
+            lax.broadcasted_iota(jnp.int32, (POINTS, CHUNK), 0) == place
         ).astype(f32).astype(bf16)
-        values = jnp.dot(grid, at_place, preferred_element_type=f32)
+        values = jnp.dot(grid[:, :POINTS], at_place, preferred_element_type=f32)
         values = jnp.where(group == chosen, values, 0.0)
-        values = jnp.sum(values.reshape(-1, 8, CHUNK), axis=0)
-        intensity = jnp.sum(values.reshape(8 // count, count, CHUNK), axis=0)
+        intensity = jnp.sum(values.reshape(-1, 8, CHUNK), axis=0)
+        shift = count
+        while shift < 8:
+            intensity = intensity + pltpu.roll(intensity, shift, axis=0)
+            shift *= 2
 
         offset = offsets_ref[:, cols]
         block = offset // LANES
+        fold = lax.broadcasted_iota(jnp.int32, (8, CHUNK), 0) // count
         routed = jnp.concatenate(
-            [jnp.where(block == i, intensity, 0.0) for i in range(nblocks)], axis=0
+            [
+                jnp.where(block == i + fold, intensity, 0.0)
+                for i in range(0, nblocks, 8 // count)
+            ],
+            axis=0,
         ).astype(bf16)
         local = (
             lax.broadcasted_iota(jnp.int32, (LANES, CHUNK), 0) == offset - block * LANES
@@ -322,8 +331,8 @@
     )
     members = ndb * ncand
     core = ncand
-    masks = [core | ncand << bit for bit in range(1, ndb.bit_length() - 1)]
-    masks += [core | 1 << bit for bit in range(ncand.bit_length() - 1)]
+    masks = [core | 1 << bit for bit in reversed(range(ncand.bit_length() - 1))]
+    masks += [core | ncand << bit for bit in range(1, ndb.bit_length() - 1)]
     masks.append(core)
     share = -(-count * 5 // 16 // STAT_UNIT) * STAT_UNIT
     cands, means, scales = [held], [], []

time: 21.2 us -> 20.9 us (0.986)
  no operation moved by 1% of the time
where the time goes in v6:
time: 20.9 us; the launch traced here: 20.8 us
  Pallas kernels  11.6 us (56%)
  starting transfers between devices  7.74 us (37%)
  waiting for transfers between devices  1.36 us (7%)
    ppermute x4, starting transfers between devices, per_device(): lax.ppermute(held, ('db', 'cand'), [(i, i ^ mask) for i in range(members)])  7.74 us
    pallas_call x4, Pallas kernels, statistics(): pl.pallas_call(functools.partial(statistics_kernel, first), out_shape=[pl...  4.04 us
    pallas_call x1, Pallas kernels, candidate_patterns(): pl.pallas_call(candidate_kernel, out_shape=[pltpu.VMEM((count, nbins), jn...  4.01 us
    pallas_call x1, Pallas kernels, score(): pl.pallas_call(functools.partial(score_kernel, ncand, masks, len(means)),...  3.52 us
    ppermute x4, waiting for transfers between devices, per_device(): lax.ppermute(held, ('db', 'cand'), [(i, i ^ mask) for i in range(members)])  1.36 us
  transfers between devices with their start and end apart: 4, of which 4 were waited for; matrix products, arithmetic and copies ran while one was open for 0% of the time, Pallas kernels for 19%

profile of v6, /device:TPU:0, one launch (start us, length us, event | category | flops | bytes accessed | tf_op | source)
XLA Modules:
  0.0 20.8 jit_solution(2826172739271486681)
XLA Ops:
  0.0 4.0 %candidates.1 = (bf16[4,1024]{1,0:T(4,128)(2,1)S(1)}, bf16[4096,1024]{1,0:T(8,128)(2,1)S(1)}) custom-call(f32[3,4,64]{2,1,0:T(4,128)} %coords_hbm.1, s32[4,64]{1,0:T(4,128)} %species_hbm.1, s32[3,4096]{1,0:T(4,128)} %miller_hbm.1, s32[1,4096]{1,0:T(1,128)} %bitcast.3, f32[4,89]{1,0:T(4,128)} %bitcast.4, f32[4,89]{1,0:T(4,128)} %bitcast.5, ...), custom_call_target="tpu_custom_call" | custom-call | tf_op jit(solution)/shard_map/candidates/pallas_call | solution.py:218
  4.0 3.5 %collective-permute-start = (bf16[4,1024]{1,0:T(4,128)(2,1)S(1)}, bf16[4,1024]{1,0:T(4,128)(2,1)S(1)}, u32[]{:S(2)}, u32[]{:S(2)}) collective-permute-start(bf16[4,1024]{1,0:T(4,128)(2,1)S(1)} %get-tuple-element.23.after_ref.rest_0_), channel_id=1, source_target_pairs={{0,6},{1,7},{2,4},{3,5},{4,2},{5,3},{6,0},{7,1},{8,14},{9,15},{10,... | collective-permute-start | bytes 24584 | tf_op jit(solution)/shard_map/ppermute | solution.py:341
  7.6 1.2 %statistics.4 = (f32[1280,1]{1,0:T(8,128)S(1)}, f32[1280,1]{1,0:T(8,128)S(1)}, bf16[4096,1024]{1,0:T(8,128)(2,1)S(1)}) custom-call(bf16[4096,1024]{1,0:T(8,128)(2,1)S(1)} %get-tuple-element.24.refs_ref, bf16[4,1024]{1,0:T(4,128)(2,1)S(1)} %get-tuple-element.23.after_ref.rest_0_), custom_call_target="tpu_custom_call", output_to_operand_aliasing={{2}: (0, {})} | custom-call | flops 335544320 | bytes 2621440 | tf_op jit(solution)/shard_map/statistics/pallas_call | solution.py:259
  8.8 0.1 collective-permute-done.rest_1_
  8.9 1.9 %collective-permute-start.1 = (bf16[8,1024]{1,0:T(8,128)(2,1)S(1)}, bf16[8,1024]{1,0:T(8,128)(2,1)S(1)}, u32[]{:S(2)}, u32[]{:S(2)}) collective-permute-start(bf16[8,1024]{1,0:T(8,128)(2,1)S(1)} %pad_maximum_fusion.2.after_ref), channel_id=1, source_target_pairs={{0,5},{1,4},{2,7},{3,6},{4,1},{5,0},{6,3},{7,2},{8,13},{9,12},{10,... | collective-permute-start | bytes 49160 | tf_op jit(solution)/shard_map/ppermute | solution.py:341
  10.9 1.2 %statistics.5 = (f32[1280,1]{1,0:T(8,128)S(1)}, f32[1280,1]{1,0:T(8,128)S(1)}, bf16[4096,1024]{1,0:T(8,128)(2,1)S(1)}) custom-call(bf16[4096,1024]{1,0:T(8,128)(2,1)S(1)} %get-tuple-element.27.refs_ref, bf16[8,1024]{1,0:T(8,128)(2,1)S(1)} %pad_maximum_fusion.2.after_ref), custom_call_target="tpu_custom_call", output_to_operand_aliasing={{2}: (0, {})} | custom-call | flops 335544320 | bytes 2621440 | tf_op jit(solution)/shard_map/statistics/pallas_call | solution.py:259
  12.1 0.2 collective-permute-done.1.rest_2_
  12.4 1.7 %collective-permute-start.2 = (bf16[16,1024]{1,0:T(8,128)(2,1)S(1)}, bf16[16,1024]{1,0:T(8,128)(2,1)S(1)}, u32[]{:S(2)}, u32[]{:S(2)}) collective-permute-start(bf16[16,1024]{1,0:T(8,128)(2,1)S(1)} %pad_maximum_fusion.1.after_ref), channel_id=1, source_target_pairs={{0,12},{1,13},{2,14},{3,15},{4,8},{5,9},{6,10},{7,11},{8,4},{9,5},... | collective-permute-start | bytes 98312 | tf_op jit(solution)/shard_map/ppermute | solution.py:341
  14.1 1.2 %statistics.6 = (f32[1280,1]{1,0:T(8,128)S(1)}, f32[1280,1]{1,0:T(8,128)S(1)}, bf16[4096,1024]{1,0:T(8,128)(2,1)S(1)}) custom-call(bf16[4096,1024]{1,0:T(8,128)(2,1)S(1)} %get-tuple-element.30.refs_ref, bf16[16,1024]{1,0:T(8,128)(2,1)S(1)} %pad_maximum_fusion.1.after_ref), custom_call_target="tpu_custom_call", output_to_operand_aliasing={{2}: (0, {})} | custom-call | flops 335544320 | bytes 2621440 | tf_op jit(solution)/shard_map/statistics/pallas_call | solution.py:259
  15.3 0.5 %collective-permute-done.2.rest_3_ = bf16[16,1024]{1,0:T(8,128)(2,1)S(1)} collective-permute-done((bf16[16,1024]{1,0:T(8,128)(2,1)S(1)}, bf16[16,1024]{1,0:T(8,128)(2,1)S(1)}, u32[]{:S(2)}, u32[]{:S(2)}) %collective-permute-start.2) | collective-permute-done | bytes 32800 | tf_op jit(solution)/shard_map/ppermute | solution.py:341
  15.8 0.6 %collective-permute-start.3 = (bf16[32,1024]{1,0:T(8,128)(2,1)S(1)}, bf16[32,1024]{1,0:T(8,128)(2,1)S(1)}, u32[]{:S(2)}, u32[]{:S(2)}) collective-permute-start(bf16[32,1024]{1,0:T(8,128)(2,1)S(1)} %pad_maximum_fusion.after_ref), channel_id=1, source_target_pairs={{0,4},{1,5},{2,6},{3,7},{4,0},{5,1},{6,2},{7,3},{8,12},{9,13},{10,... | collective-permute-start | bytes 196616 | tf_op jit(solution)/shard_map/ppermute | solution.py:341
  16.3 0.3 %statistics.7 = (f32[256,1]{1,0:T(8,128)S(1)}, f32[256,1]{1,0:T(8,128)S(1)}, bf16[4096,1024]{1,0:T(8,128)(2,1)S(1)}) custom-call(bf16[4096,1024]{1,0:T(8,128)(2,1)S(1)} %get-tuple-element.33.refs_ref, bf16[32,1024]{1,0:T(8,128)(2,1)S(1)} %pad_maximum_fusion.after_ref), custom_call_target="tpu_custom_call", output_to_operand_aliasing={{2}: (0, {})} | custom-call | flops 67108864 | bytes 524288 | tf_op jit(solution)/shard_map/statistics/pallas_call | solution.py:259
  16.6 0.6 %collective-permute-done.3.rest_4_ = bf16[32,1024]{1,0:T(8,128)(2,1)S(1)} collective-permute-done((bf16[32,1024]{1,0:T(8,128)(2,1)S(1)}, bf16[32,1024]{1,0:T(8,128)(2,1)S(1)}, u32[]{:S(2)}, u32[]{:S(2)}) %collective-permute-start.3) | collective-permute-done | bytes 65568 | tf_op jit(solution)/shard_map/ppermute | solution.py:341
  17.2 3.5 %scores.1 = bf16[64,4096]{1,0:T(8,128)(2,1)} custom-call(bf16[4,1024]{1,0:T(4,128)(2,1)S(1)} %get-tuple-element.23.after_ref.rest_0_, bf16[4,1024]{1,0:T(4,128)(2,1)S(1)} %collective-permute-done.rest_1_, bf16[8,1024]{1,0:T(8,128)(2,1)S(1)} %collective-permute-done.1.rest_2_, bf16[16,1024]{1,0:T(8,128)(2,1)S(1)} %collective-permute-done.2.rest_3_, ...), custom_call_target="tpu_custom_call" | custom-call | tf_op jit(solution)/shard_map/scores/pallas_call | solution.py:312
  (3 shorter events, 0.1 us)
Async XLA Ops:
  4.0 4.9 %collective-permute-start = (bf16[4,1024]{1,0:T(4,128)(2,1)S(1)}, bf16[4,1024]{1,0:T(4,128)(2,1)S(1)}, u32[]{:S(2)}, u32[]{:S(2)}) collective-permute-start(bf16[4,1024]{1,0:T(4,128)(2,1)S(1)} %get-tuple-element.23.after_ref.rest_0_), channel_id=1, source_target_pairs={{0,6},{1,7},{2,4},{3,5},{4,2},{5,3},{6,0},{7,1},{8,14},{9,15},{10,... | collective-permute-start | bytes 24584 | tf_op jit(solution)/shard_map/ppermute | solution.py:341
  8.9 3.4 %collective-permute-start.1 = (bf16[8,1024]{1,0:T(8,128)(2,1)S(1)}, bf16[8,1024]{1,0:T(8,128)(2,1)S(1)}, u32[]{:S(2)}, u32[]{:S(2)}) collective-permute-start(bf16[8,1024]{1,0:T(8,128)(2,1)S(1)} %pad_maximum_fusion.2.after_ref), channel_id=1, source_target_pairs={{0,5},{1,4},{2,7},{3,6},{4,1},{5,0},{6,3},{7,2},{8,13},{9,12},{10,... | collective-permute-start | bytes 49160 | tf_op jit(solution)/shard_map/ppermute | solution.py:341
  12.4 3.4 %collective-permute-start.2 = (bf16[16,1024]{1,0:T(8,128)(2,1)S(1)}, bf16[16,1024]{1,0:T(8,128)(2,1)S(1)}, u32[]{:S(2)}, u32[]{:S(2)}) collective-permute-start(bf16[16,1024]{1,0:T(8,128)(2,1)S(1)} %pad_maximum_fusion.1.after_ref), channel_id=1, source_target_pairs={{0,12},{1,13},{2,14},{3,15},{4,8},{5,9},{6,10},{7,11},{8,4},{9,5},... | collective-permute-start | bytes 98312 | tf_op jit(solution)/shard_map/ppermute | solution.py:341
  15.8 1.5 %collective-permute-start.3 = (bf16[32,1024]{1,0:T(8,128)(2,1)S(1)}, bf16[32,1024]{1,0:T(8,128)(2,1)S(1)}, u32[]{:S(2)}, u32[]{:S(2)}) collective-permute-start(bf16[32,1024]{1,0:T(8,128)(2,1)S(1)} %pad_maximum_fusion.after_ref), channel_id=1, source_target_pairs={{0,4},{1,5},{2,6},{3,7},{4,0},{5,1},{6,2},{7,3},{8,12},{9,13},{10,... | collective-permute-start | bytes 196616 | tf_op jit(solution)/shard_map/ppermute | solution.py:341

commit v7 on v6

--- a/solution.py
+++ b/solution.py
@@ -270,58 +270,55 @@
     )(pltpu.with_memory_space_constraint(refs, pltpu.VMEM), after)
 
 
-def score_kernel(ncand, masks, npieces, *rest):
-    cand_refs, (refs_ref, *rest) = rest[: len(masks) + 1], rest[len(masks) + 1 :]
+def score_kernel(ncand, masks, npieces, held_ref, other_ref, refs_ref, *rest):
     mean_refs, scale_refs = rest[:npieces], rest[npieces : 2 * npieces]
-    out_ref, cand_t_ref, held_ref, sems = rest[2 * npieces :]
+    out_ref, scores_ref, sems = rest[2 * npieces :]
     f32, bf16 = jnp.float32, jnp.bfloat16
-    cand = jnp.concatenate([ref[...] for ref in cand_refs], axis=0)
+    cand = jnp.concatenate([held_ref[...], other_ref[...]], axis=0)
     total, nbins = cand.shape
-    block = cand_refs[0].shape[0]
-    place = lax.broadcasted_iota(jnp.int32, (total, total), 0)
+    block = total >> len(masks)
+    last = (((1,), (1,)), ((), ()))
+    place = lax.broadcasted_iota(jnp.int32, (total, total), 1)
     group = place // block
     position = lax.axis_index("db") * ncand + lax.axis_index("cand")
     source = jnp.full_like(group, position)
     for bit, mask in enumerate(masks):
         source = source ^ jnp.where((group >> bit) % 2 == 1, mask, 0)
-    row = lax.broadcasted_iota(jnp.int32, (total, total), 1)
+    row = lax.broadcasted_iota(jnp.int32, (total, total), 0)
     order = (row == source * block + place % block).astype(f32).astype(bf16)
-    cand_t_ref[...] = lax.dot_general(
-        cand, order, (((0,), (0,)), ((), ())), preferred_element_type=f32
-    ).astype(bf16)
-    sums = jnp.dot(jnp.ones((8, nbins), bf16), cand_t_ref[...], preferred_element_type=f32)[:1]
+    cand = jnp.dot(order, cand, preferred_element_type=f32).astype(bf16)
+    sums = lax.dot_general(jnp.ones((8, nbins), bf16), cand, last, preferred_element_type=f32)[:1]
     means, scales = (
         jnp.concatenate([ref[...] for ref in refs], axis=0) for refs in (mean_refs, scale_refs)
     )
     copies = []
     for i, start in enumerate(range(0, refs_ref.shape[0], SCORE_ROWS)):
         rows = slice(start, start + SCORE_ROWS)
-        product = jnp.dot(refs_ref[rows, :], cand_t_ref[...], preferred_element_type=f32)
+        product = lax.dot_general(refs_ref[rows, :], cand, last, preferred_element_type=f32)
         product = (product - means[rows] * sums) * scales[rows]
-        held_ref[:, rows] = product.T.astype(bf16)
-        copy = pltpu.make_async_copy(held_ref.at[:, rows], out_ref.at[:, rows], sems.at[i])
+        scores_ref[:, rows] = product.T.astype(bf16)
+        copy = pltpu.make_async_copy(scores_ref.at[:, rows], out_ref.at[:, rows], sems.at[i])
         copy.start()
         copies.append(copy)
     for copy in copies:
         copy.wait()
 
 
-def score(ncand, masks, cands, refs, means, scales):
-    total = sum(cand.shape[0] for cand in cands)
-    count, nbins = refs.shape
+def score(ncand, masks, held, other, refs, means, scales):
+    total = held.shape[0] + other.shape[0]
+    count = refs.shape[0]
     return pl.pallas_call(
         functools.partial(score_kernel, ncand, masks, len(means)),
         out_shape=jax.ShapeDtypeStruct((total, count), jnp.bfloat16),
-        in_specs=[VMEM_WHOLE] * (len(cands) + 1 + 2 * len(means)),
+        in_specs=[VMEM_WHOLE] * (3 + 2 * len(means)),
         out_specs=pl.BlockSpec(memory_space=pltpu.HBM),
         scratch_shapes=[
-            pltpu.VMEM((nbins, total), jnp.bfloat16),
             pltpu.VMEM((total, count), jnp.bfloat16),
             pltpu.SemaphoreType.DMA((count // SCORE_ROWS,)),
         ],
         compiler_params=pltpu.CompilerParams(vmem_limit_bytes=VMEM_LIMIT),
         name="scores",
-    )(*cands, pltpu.with_memory_space_constraint(refs, pltpu.VMEM), *means, *scales)
+    )(held, other, pltpu.with_memory_space_constraint(refs, pltpu.VMEM), *means, *scales)
 
 
 def per_device(ndb, ncand, coords, species, miller, offsets, form_amps, form_decay, ref_patterns):
@@ -335,7 +332,7 @@
     masks += [core | ncand << bit for bit in range(1, ndb.bit_length() - 1)]
     masks.append(core)
     share = -(-count * 5 // 16 // STAT_UNIT) * STAT_UNIT
-    cands, means, scales = [held], [], []
+    means, scales = [], []
     first = 0
     for mask in masks:
         other = lax.ppermute(held, ("db", "cand"), [(i, i ^ mask) for i in range(members)])
@@ -346,13 +343,13 @@
             scales.append(scale)
             first += rows
             other, mean = lax.optimization_barrier((other, mean))
-        cands.append(other)
-        held = jnp.concatenate([held, other], axis=0)
+        if mask != core:
+            held = jnp.concatenate([held, other], axis=0)
     if first < count:
         mean, scale, refs = statistics(refs, first, count - first, held)
         means.append(mean)
         scales.append(scale)
-    return score(ncand, tuple(masks), cands, refs, means, scales)
+    return score(ncand, tuple(masks), held, other, refs, means, scales)
 
 
 def solution(mesh):

time: 20.9 us -> 20.7 us (level)
  Pallas kernels: 11.6 us -> 11.3 us
    pallas_call x1, Pallas kernels: 3.52 us -> 3.3 us  [score(): pl.pallas_call(functools.partial(score_kernel, ncand, masks, len(means)),...]
  transfers between devices with their start and end apart: 4 -> 4, of which waited for: 4 -> 4; matrix products, arithmetic and copies ran while one was open for 0% -> 0% of each run, Pallas kernels for 19% -> 20%
where the time goes in v7:
time: 20.7 us; the launch traced here: 20.5 us
  Pallas kernels  11.3 us (55%)
  starting transfers between devices  7.74 us (37%)
  waiting for transfers between devices  1.36 us (7%)
    ppermute x4, starting transfers between devices, per_device(): lax.ppermute(held, ('db', 'cand'), [(i, i ^ mask) for i in range(members)])  7.74 us
    pallas_call x4, Pallas kernels, statistics(): pl.pallas_call(functools.partial(statistics_kernel, first), out_shape=[pl...  4.04 us
    pallas_call x1, Pallas kernels, candidate_patterns(): pl.pallas_call(candidate_kernel, out_shape=[pltpu.VMEM((count, nbins), jn...  4.01 us
    pallas_call x1, Pallas kernels, score(): pl.pallas_call(functools.partial(score_kernel, ncand, masks, len(means)),...  3.3 us
    ppermute x4, waiting for transfers between devices, per_device(): lax.ppermute(held, ('db', 'cand'), [(i, i ^ mask) for i in range(members)])  1.36 us
  transfers between devices with their start and end apart: 4, of which 4 were waited for; matrix products, arithmetic and copies ran while one was open for 0% of the time, Pallas kernels for 20%

profile of v7, /device:TPU:0, one launch (start us, length us, event | category | flops | bytes accessed | tf_op | source)
XLA Modules:
  0.0 20.5 jit_solution(18365801374743377256)
XLA Ops:
  0.0 4.0 %candidates.1 = (bf16[4,1024]{1,0:T(4,128)(2,1)S(1)}, bf16[4096,1024]{1,0:T(8,128)(2,1)S(1)}) custom-call(f32[3,4,64]{2,1,0:T(4,128)} %coords_hbm.1, s32[4,64]{1,0:T(4,128)} %species_hbm.1, s32[3,4096]{1,0:T(4,128)} %miller_hbm.1, s32[1,4096]{1,0:T(1,128)} %bitcast.3, f32[4,89]{1,0:T(4,128)} %bitcast.4, f32[4,89]{1,0:T(4,128)} %bitcast.5, ...), custom_call_target="tpu_custom_call" | custom-call | tf_op jit(solution)/shard_map/candidates/pallas_call | solution.py:218
  4.0 3.5 %collective-permute-start = (bf16[4,1024]{1,0:T(4,128)(2,1)S(1)}, bf16[4,1024]{1,0:T(4,128)(2,1)S(1)}, u32[]{:S(2)}, u32[]{:S(2)}) collective-permute-start(bf16[4,1024]{1,0:T(4,128)(2,1)S(1)} %get-tuple-element.23.after_ref), channel_id=1, source_target_pairs={{0,6},{1,7},{2,4},{3,5},{4,2},{5,3},{6,0},{7,1},{8,14},{9,15},{10,... | collective-permute-start | bytes 24584 | tf_op jit(solution)/shard_map/ppermute | solution.py:338
  7.6 1.2 %statistics.4 = (f32[1280,1]{1,0:T(8,128)S(1)}, f32[1280,1]{1,0:T(8,128)S(1)}, bf16[4096,1024]{1,0:T(8,128)(2,1)S(1)}) custom-call(bf16[4096,1024]{1,0:T(8,128)(2,1)S(1)} %get-tuple-element.24.refs_ref, bf16[4,1024]{1,0:T(4,128)(2,1)S(1)} %get-tuple-element.23.after_ref), custom_call_target="tpu_custom_call", output_to_operand_aliasing={{2}: (0, {})} | custom-call | flops 335544320 | bytes 2621440 | tf_op jit(solution)/shard_map/statistics/pallas_call | solution.py:259
  8.8 0.1 collective-permute-done
  8.9 1.9 %collective-permute-start.1 = (bf16[8,1024]{1,0:T(8,128)(2,1)S(1)}, bf16[8,1024]{1,0:T(8,128)(2,1)S(1)}, u32[]{:S(2)}, u32[]{:S(2)}) collective-permute-start(bf16[8,1024]{1,0:T(8,128)(2,1)S(1)} %pad_maximum_fusion.2.after_ref), channel_id=1, source_target_pairs={{0,5},{1,4},{2,7},{3,6},{4,1},{5,0},{6,3},{7,2},{8,13},{9,12},{10,... | collective-permute-start | bytes 49160 | tf_op jit(solution)/shard_map/ppermute | solution.py:338
  10.9 1.2 %statistics.5 = (f32[1280,1]{1,0:T(8,128)S(1)}, f32[1280,1]{1,0:T(8,128)S(1)}, bf16[4096,1024]{1,0:T(8,128)(2,1)S(1)}) custom-call(bf16[4096,1024]{1,0:T(8,128)(2,1)S(1)} %get-tuple-element.27.refs_ref, bf16[8,1024]{1,0:T(8,128)(2,1)S(1)} %pad_maximum_fusion.2.after_ref), custom_call_target="tpu_custom_call", output_to_operand_aliasing={{2}: (0, {})} | custom-call | flops 335544320 | bytes 2621440 | tf_op jit(solution)/shard_map/statistics/pallas_call | solution.py:259
  12.1 0.2 collective-permute-done.1
  12.4 1.7 %collective-permute-start.2 = (bf16[16,1024]{1,0:T(8,128)(2,1)S(1)}, bf16[16,1024]{1,0:T(8,128)(2,1)S(1)}, u32[]{:S(2)}, u32[]{:S(2)}) collective-permute-start(bf16[16,1024]{1,0:T(8,128)(2,1)S(1)} %pad_maximum_fusion.1.after_ref), channel_id=1, source_target_pairs={{0,12},{1,13},{2,14},{3,15},{4,8},{5,9},{6,10},{7,11},{8,4},{9,5},... | collective-permute-start | bytes 98312 | tf_op jit(solution)/shard_map/ppermute | solution.py:338
  14.1 1.2 %statistics.6 = (f32[1280,1]{1,0:T(8,128)S(1)}, f32[1280,1]{1,0:T(8,128)S(1)}, bf16[4096,1024]{1,0:T(8,128)(2,1)S(1)}) custom-call(bf16[4096,1024]{1,0:T(8,128)(2,1)S(1)} %get-tuple-element.30.refs_ref, bf16[16,1024]{1,0:T(8,128)(2,1)S(1)} %pad_maximum_fusion.1.after_ref), custom_call_target="tpu_custom_call", output_to_operand_aliasing={{2}: (0, {})} | custom-call | flops 335544320 | bytes 2621440 | tf_op jit(solution)/shard_map/statistics/pallas_call | solution.py:259
  15.3 0.5 %collective-permute-done.2 = bf16[16,1024]{1,0:T(8,128)(2,1)S(1)} collective-permute-done((bf16[16,1024]{1,0:T(8,128)(2,1)S(1)}, bf16[16,1024]{1,0:T(8,128)(2,1)S(1)}, u32[]{:S(2)}, u32[]{:S(2)}) %collective-permute-start.2) | collective-permute-done | bytes 32800 | tf_op jit(solution)/shard_map/ppermute | solution.py:338
  15.8 0.6 %collective-permute-start.3 = (bf16[32,1024]{1,0:T(8,128)(2,1)S(1)}, bf16[32,1024]{1,0:T(8,128)(2,1)S(1)}, u32[]{:S(2)}, u32[]{:S(2)}) collective-permute-start(bf16[32,1024]{1,0:T(8,128)(2,1)S(1)} %pad_maximum_fusion.after_ref.held_ref), channel_id=1, source_target_pairs={{0,4},{1,5},{2,6},{3,7},{4,0},{5,1},{6,2},{7,3},{8,12},{9,13},{10,... | collective-permute-start | bytes 196616 | tf_op jit(solution)/shard_map/ppermute | solution.py:338
  16.3 0.3 %statistics.7 = (f32[256,1]{1,0:T(8,128)S(1)}, f32[256,1]{1,0:T(8,128)S(1)}, bf16[4096,1024]{1,0:T(8,128)(2,1)S(1)}) custom-call(bf16[4096,1024]{1,0:T(8,128)(2,1)S(1)} %get-tuple-element.33.refs_ref, bf16[32,1024]{1,0:T(8,128)(2,1)S(1)} %pad_maximum_fusion.after_ref.held_ref), custom_call_target="tpu_custom_call", output_to_operand_aliasing={{2}: (0, {})} | custom-call | flops 67108864 | bytes 524288 | tf_op jit(solution)/shard_map/statistics/pallas_call | solution.py:259
  16.6 0.6 %collective-permute-done.3.other_ref = bf16[32,1024]{1,0:T(8,128)(2,1)S(1)} collective-permute-done((bf16[32,1024]{1,0:T(8,128)(2,1)S(1)}, bf16[32,1024]{1,0:T(8,128)(2,1)S(1)}, u32[]{:S(2)}, u32[]{:S(2)}) %collective-permute-start.3) | collective-permute-done | bytes 65568 | tf_op jit(solution)/shard_map/ppermute | solution.py:338
  17.2 3.3 %scores.1 = bf16[64,4096]{1,0:T(8,128)(2,1)} custom-call(bf16[32,1024]{1,0:T(8,128)(2,1)S(1)} %pad_maximum_fusion.after_ref.held_ref, bf16[32,1024]{1,0:T(8,128)(2,1)S(1)} %collective-permute-done.3.other_ref, bf16[4096,1024]{1,0:T(8,128)(2,1)S(1)} %get-tuple-element.36.refs_ref, f32[1280,1]{1,0:T(8,128)S(1)} %get-tuple-element.25.rest_0_, ...), custom_call_target="tpu_custom_call" | custom-call | tf_op jit(solution)/shard_map/scores/pallas_call | solution.py:310
  (3 shorter events, 0.1 us)
Async XLA Ops:
  4.0 4.9 %collective-permute-start = (bf16[4,1024]{1,0:T(4,128)(2,1)S(1)}, bf16[4,1024]{1,0:T(4,128)(2,1)S(1)}, u32[]{:S(2)}, u32[]{:S(2)}) collective-permute-start(bf16[4,1024]{1,0:T(4,128)(2,1)S(1)} %get-tuple-element.23.after_ref), channel_id=1, source_target_pairs={{0,6},{1,7},{2,4},{3,5},{4,2},{5,3},{6,0},{7,1},{8,14},{9,15},{10,... | collective-permute-start | bytes 24584 | tf_op jit(solution)/shard_map/ppermute | solution.py:338
  8.9 3.4 %collective-permute-start.1 = (bf16[8,1024]{1,0:T(8,128)(2,1)S(1)}, bf16[8,1024]{1,0:T(8,128)(2,1)S(1)}, u32[]{:S(2)}, u32[]{:S(2)}) collective-permute-start(bf16[8,1024]{1,0:T(8,128)(2,1)S(1)} %pad_maximum_fusion.2.after_ref), channel_id=1, source_target_pairs={{0,5},{1,4},{2,7},{3,6},{4,1},{5,0},{6,3},{7,2},{8,13},{9,12},{10,... | collective-permute-start | bytes 49160 | tf_op jit(solution)/shard_map/ppermute | solution.py:338
  12.4 3.4 %collective-permute-start.2 = (bf16[16,1024]{1,0:T(8,128)(2,1)S(1)}, bf16[16,1024]{1,0:T(8,128)(2,1)S(1)}, u32[]{:S(2)}, u32[]{:S(2)}) collective-permute-start(bf16[16,1024]{1,0:T(8,128)(2,1)S(1)} %pad_maximum_fusion.1.after_ref), channel_id=1, source_target_pairs={{0,12},{1,13},{2,14},{3,15},{4,8},{5,9},{6,10},{7,11},{8,4},{9,5},... | collective-permute-start | bytes 98312 | tf_op jit(solution)/shard_map/ppermute | solution.py:338
  15.8 1.5 %collective-permute-start.3 = (bf16[32,1024]{1,0:T(8,128)(2,1)S(1)}, bf16[32,1024]{1,0:T(8,128)(2,1)S(1)}, u32[]{:S(2)}, u32[]{:S(2)}) collective-permute-start(bf16[32,1024]{1,0:T(8,128)(2,1)S(1)} %pad_maximum_fusion.after_ref.held_ref), channel_id=1, source_target_pairs={{0,4},{1,5},{2,6},{3,7},{4,0},{5,1},{6,2},{7,3},{8,12},{9,13},{10,... | collective-permute-start | bytes 196616 | tf_op jit(solution)/shard_map/ppermute | solution.py:338

commit v8 on v7

--- a/solution.py
+++ b/solution.py
@@ -41,8 +41,8 @@
     coords_ref, species_ref, miller_ref, offsets_ref, amps_ref, decay_ref,
     grid_ref, spread_ref, sems,
 ):
-    sources = (coords_hbm, species_hbm, miller_hbm, offsets_hbm, amps_hbm, decay_hbm, refs_hbm)
-    targets = (coords_ref, species_ref, miller_ref, offsets_ref, amps_ref, decay_ref, refs_ref)
+    sources = (coords_hbm, species_hbm, amps_hbm, decay_hbm, miller_hbm, offsets_hbm, refs_hbm)
+    targets = (coords_ref, species_ref, amps_ref, decay_ref, miller_ref, offsets_ref, refs_ref)
     copies = [
         pltpu.make_async_copy(source, target, sems.at[i])
         for i, (source, target) in enumerate(zip(sources, targets))
@@ -57,7 +57,6 @@
     nblocks = nbins // LANES
     flat = count * atoms
 
-
     axis = lax.broadcasted_iota(jnp.int32, (9, 3 * LANES), 0) // 3
     column = lax.broadcasted_iota(jnp.int32, (9, 3 * LANES), 1)
     tile = column // LANES
@@ -82,8 +81,7 @@
     bins = jnp.where(bins < LANES + LANES // 2, bins, bins - 2 * LANES)
     distance = (bins - centre).astype(f32) * (1.0 / PEAK_WIDTH)
     profile = jnp.exp(-0.5 * distance * distance).astype(bf16)
-
-    for copy in copies[:2] + copies[4:6]:
+    for copy in copies[:4]:
         copy.wait()
     pieces = []
     for axis in range(3):
@@ -139,7 +137,7 @@
     grid = jnp.concatenate([plus, minus], axis=0).astype(bf16)
     group = lax.broadcasted_iota(jnp.int32, (4 * SIDE * count, CHUNK), 0) // count
 
-    for copy in copies[2:4]:
+    for copy in copies[4:6]:
         copy.wait()
     spread_ref[...] = jnp.zeros_like(spread_ref)
 
@@ -185,14 +183,13 @@
     sums = spread_ref[...].T
     pieces = []
     for _ in range(3):
-        piece = sums.astype(bf16)
-        sums = sums - piece.astype(f32)
-        pieces.append(piece.astype(f32))
+        pieces.append(sums.astype(bf16))
+        sums = sums - pieces[-1].astype(f32)
     peaks = jnp.dot(
-        jnp.concatenate(pieces, axis=0).astype(bf16), profile, preferred_element_type=f32
-    )
-    rows = count * nblocks
-    peaks = peaks[:rows] + peaks[rows : 2 * rows] + peaks[2 * rows :]
+        jnp.concatenate(pieces, axis=1),
+        jnp.concatenate([profile] * 3, axis=0),
+        preferred_element_type=f32,
+    )
     lane = lax.broadcasted_iota(jnp.int32, (count, LANES), 1)
     blocks = []
     for i in range(nblocks):
@@ -224,7 +221,7 @@
         in_specs=[pl.BlockSpec(memory_space=pltpu.HBM)] * len(args),
         scratch_shapes=[pltpu.VMEM(arg.shape, arg.dtype) for arg in args[:-1]]
         + [
-            pltpu.VMEM((8 * 8 * SIDE * count, LANES), jnp.float32),
+            pltpu.VMEM((8 * 8 * SIDE * count + 8, LANES), jnp.float32),
             pltpu.VMEM((LANES, count * (nbins // LANES)), jnp.float32),
             pltpu.SemaphoreType.DMA((len(args),)),
         ],

time: 20.7 us -> 20.7 us (level)
  no operation moved by 1% of the time
where the time goes in v8:
time: 20.7 us; the launch traced here: 20.5 us
  Pallas kernels  11.3 us (55%)
  starting transfers between devices  7.74 us (37%)
  waiting for transfers between devices  1.35 us (7%)
    ppermute x4, starting transfers between devices, per_device(): lax.ppermute(held, ('db', 'cand'), [(i, i ^ mask) for i in range(members)])  7.74 us
    pallas_call x4, Pallas kernels, statistics(): pl.pallas_call(functools.partial(statistics_kernel, first), out_shape=[pl...  4.04 us
    pallas_call x1, Pallas kernels, candidate_patterns(): pl.pallas_call(candidate_kernel, out_shape=[pltpu.VMEM((count, nbins), jn...  3.98 us
    pallas_call x1, Pallas kernels, score(): pl.pallas_call(functools.partial(score_kernel, ncand, masks, len(means)),...  3.3 us
    ppermute x4, waiting for transfers between devices, per_device(): lax.ppermute(held, ('db', 'cand'), [(i, i ^ mask) for i in range(members)])  1.35 us
  transfers between devices with their start and end apart: 4, of which 4 were waited for; matrix products, arithmetic and copies ran while one was open for 0% of the time, Pallas kernels for 20%

profile of v8, /device:TPU:0, one launch (start us, length us, event | category | flops | bytes accessed | tf_op | source)
XLA Modules:
  0.0 20.5 jit_solution(12004405426910265717)
XLA Ops:
  0.0 4.0 %candidates.1 = (bf16[4,1024]{1,0:T(4,128)(2,1)S(1)}, bf16[4096,1024]{1,0:T(8,128)(2,1)S(1)}) custom-call(f32[3,4,64]{2,1,0:T(4,128)} %coords_hbm.1, s32[4,64]{1,0:T(4,128)} %species_hbm.1, s32[3,4096]{1,0:T(4,128)} %miller_hbm.1, s32[1,4096]{1,0:T(1,128)} %bitcast.3, f32[4,89]{1,0:T(4,128)} %bitcast.4, f32[4,89]{1,0:T(4,128)} %bitcast.5, ...), custom_call_target="tpu_custom_call" | custom-call | tf_op jit(solution)/shard_map/candidates/pallas_call | solution.py:215
  4.0 3.5 %collective-permute-start = (bf16[4,1024]{1,0:T(4,128)(2,1)S(1)}, bf16[4,1024]{1,0:T(4,128)(2,1)S(1)}, u32[]{:S(2)}, u32[]{:S(2)}) collective-permute-start(bf16[4,1024]{1,0:T(4,128)(2,1)S(1)} %get-tuple-element.23.after_ref), channel_id=1, source_target_pairs={{0,6},{1,7},{2,4},{3,5},{4,2},{5,3},{6,0},{7,1},{8,14},{9,15},{10,... | collective-permute-start | bytes 24584 | tf_op jit(solution)/shard_map/ppermute | solution.py:335
  7.5 1.2 %statistics.4 = (f32[1280,1]{1,0:T(8,128)S(1)}, f32[1280,1]{1,0:T(8,128)S(1)}, bf16[4096,1024]{1,0:T(8,128)(2,1)S(1)}) custom-call(bf16[4096,1024]{1,0:T(8,128)(2,1)S(1)} %get-tuple-element.24.refs_ref, bf16[4,1024]{1,0:T(4,128)(2,1)S(1)} %get-tuple-element.23.after_ref), custom_call_target="tpu_custom_call", output_to_operand_aliasing={{2}: (0, {})} | custom-call | flops 335544320 | bytes 2621440 | tf_op jit(solution)/shard_map/statistics/pallas_call | solution.py:256
  8.8 0.1 collective-permute-done
  8.9 1.9 %collective-permute-start.1 = (bf16[8,1024]{1,0:T(8,128)(2,1)S(1)}, bf16[8,1024]{1,0:T(8,128)(2,1)S(1)}, u32[]{:S(2)}, u32[]{:S(2)}) collective-permute-start(bf16[8,1024]{1,0:T(8,128)(2,1)S(1)} %pad_maximum_fusion.2.after_ref), channel_id=1, source_target_pairs={{0,5},{1,4},{2,7},{3,6},{4,1},{5,0},{6,3},{7,2},{8,13},{9,12},{10,... | collective-permute-start | bytes 49160 | tf_op jit(solution)/shard_map/ppermute | solution.py:335
  10.8 1.2 %statistics.5 = (f32[1280,1]{1,0:T(8,128)S(1)}, f32[1280,1]{1,0:T(8,128)S(1)}, bf16[4096,1024]{1,0:T(8,128)(2,1)S(1)}) custom-call(bf16[4096,1024]{1,0:T(8,128)(2,1)S(1)} %get-tuple-element.27.refs_ref, bf16[8,1024]{1,0:T(8,128)(2,1)S(1)} %pad_maximum_fusion.2.after_ref), custom_call_target="tpu_custom_call", output_to_operand_aliasing={{2}: (0, {})} | custom-call | flops 335544320 | bytes 2621440 | tf_op jit(solution)/shard_map/statistics/pallas_call | solution.py:256
  12.1 0.2 collective-permute-done.1
  12.3 1.7 %collective-permute-start.2 = (bf16[16,1024]{1,0:T(8,128)(2,1)S(1)}, bf16[16,1024]{1,0:T(8,128)(2,1)S(1)}, u32[]{:S(2)}, u32[]{:S(2)}) collective-permute-start(bf16[16,1024]{1,0:T(8,128)(2,1)S(1)} %pad_maximum_fusion.1.after_ref), channel_id=1, source_target_pairs={{0,12},{1,13},{2,14},{3,15},{4,8},{5,9},{6,10},{7,11},{8,4},{9,5},... | collective-permute-start | bytes 98312 | tf_op jit(solution)/shard_map/ppermute | solution.py:335
  14.0 1.2 %statistics.6 = (f32[1280,1]{1,0:T(8,128)S(1)}, f32[1280,1]{1,0:T(8,128)S(1)}, bf16[4096,1024]{1,0:T(8,128)(2,1)S(1)}) custom-call(bf16[4096,1024]{1,0:T(8,128)(2,1)S(1)} %get-tuple-element.30.refs_ref, bf16[16,1024]{1,0:T(8,128)(2,1)S(1)} %pad_maximum_fusion.1.after_ref), custom_call_target="tpu_custom_call", output_to_operand_aliasing={{2}: (0, {})} | custom-call | flops 335544320 | bytes 2621440 | tf_op jit(solution)/shard_map/statistics/pallas_call | solution.py:256
  15.3 0.4 %collective-permute-done.2 = bf16[16,1024]{1,0:T(8,128)(2,1)S(1)} collective-permute-done((bf16[16,1024]{1,0:T(8,128)(2,1)S(1)}, bf16[16,1024]{1,0:T(8,128)(2,1)S(1)}, u32[]{:S(2)}, u32[]{:S(2)}) %collective-permute-start.2) | collective-permute-done | bytes 32800 | tf_op jit(solution)/shard_map/ppermute | solution.py:335
  15.7 0.6 %collective-permute-start.3 = (bf16[32,1024]{1,0:T(8,128)(2,1)S(1)}, bf16[32,1024]{1,0:T(8,128)(2,1)S(1)}, u32[]{:S(2)}, u32[]{:S(2)}) collective-permute-start(bf16[32,1024]{1,0:T(8,128)(2,1)S(1)} %pad_maximum_fusion.after_ref.held_ref), channel_id=1, source_target_pairs={{0,4},{1,5},{2,6},{3,7},{4,0},{5,1},{6,2},{7,3},{8,12},{9,13},{10,... | collective-permute-start | bytes 196616 | tf_op jit(solution)/shard_map/ppermute | solution.py:335
  16.3 0.3 %statistics.7 = (f32[256,1]{1,0:T(8,128)S(1)}, f32[256,1]{1,0:T(8,128)S(1)}, bf16[4096,1024]{1,0:T(8,128)(2,1)S(1)}) custom-call(bf16[4096,1024]{1,0:T(8,128)(2,1)S(1)} %get-tuple-element.33.refs_ref, bf16[32,1024]{1,0:T(8,128)(2,1)S(1)} %pad_maximum_fusion.after_ref.held_ref), custom_call_target="tpu_custom_call", output_to_operand_aliasing={{2}: (0, {})} | custom-call | flops 67108864 | bytes 524288 | tf_op jit(solution)/shard_map/statistics/pallas_call | solution.py:256
  16.6 0.6 %collective-permute-done.3.other_ref = bf16[32,1024]{1,0:T(8,128)(2,1)S(1)} collective-permute-done((bf16[32,1024]{1,0:T(8,128)(2,1)S(1)}, bf16[32,1024]{1,0:T(8,128)(2,1)S(1)}, u32[]{:S(2)}, u32[]{:S(2)}) %collective-permute-start.3) | collective-permute-done | bytes 65568 | tf_op jit(solution)/shard_map/ppermute | solution.py:335
  17.2 3.3 %scores.1 = bf16[64,4096]{1,0:T(8,128)(2,1)} custom-call(bf16[32,1024]{1,0:T(8,128)(2,1)S(1)} %pad_maximum_fusion.after_ref.held_ref, bf16[32,1024]{1,0:T(8,128)(2,1)S(1)} %collective-permute-done.3.other_ref, bf16[4096,1024]{1,0:T(8,128)(2,1)S(1)} %get-tuple-element.36.refs_ref, f32[1280,1]{1,0:T(8,128)S(1)} %get-tuple-element.25.rest_0_, ...), custom_call_target="tpu_custom_call" | custom-call | tf_op jit(solution)/shard_map/scores/pallas_call | solution.py:307
  (3 shorter events, 0.1 us)
Async XLA Ops:
  4.0 4.9 %collective-permute-start = (bf16[4,1024]{1,0:T(4,128)(2,1)S(1)}, bf16[4,1024]{1,0:T(4,128)(2,1)S(1)}, u32[]{:S(2)}, u32[]{:S(2)}) collective-permute-start(bf16[4,1024]{1,0:T(4,128)(2,1)S(1)} %get-tuple-element.23.after_ref), channel_id=1, source_target_pairs={{0,6},{1,7},{2,4},{3,5},{4,2},{5,3},{6,0},{7,1},{8,14},{9,15},{10,... | collective-permute-start | bytes 24584 | tf_op jit(solution)/shard_map/ppermute | solution.py:335
  8.9 3.4 %collective-permute-start.1 = (bf16[8,1024]{1,0:T(8,128)(2,1)S(1)}, bf16[8,1024]{1,0:T(8,128)(2,1)S(1)}, u32[]{:S(2)}, u32[]{:S(2)}) collective-permute-start(bf16[8,1024]{1,0:T(8,128)(2,1)S(1)} %pad_maximum_fusion.2.after_ref), channel_id=1, source_target_pairs={{0,5},{1,4},{2,7},{3,6},{4,1},{5,0},{6,3},{7,2},{8,13},{9,12},{10,... | collective-permute-start | bytes 49160 | tf_op jit(solution)/shard_map/ppermute | solution.py:335
  12.3 3.4 %collective-permute-start.2 = (bf16[16,1024]{1,0:T(8,128)(2,1)S(1)}, bf16[16,1024]{1,0:T(8,128)(2,1)S(1)}, u32[]{:S(2)}, u32[]{:S(2)}) collective-permute-start(bf16[16,1024]{1,0:T(8,128)(2,1)S(1)} %pad_maximum_fusion.1.after_ref), channel_id=1, source_target_pairs={{0,12},{1,13},{2,14},{3,15},{4,8},{5,9},{6,10},{7,11},{8,4},{9,5},... | collective-permute-start | bytes 98312 | tf_op jit(solution)/shard_map/ppermute | solution.py:335
  15.7 1.5 %collective-permute-start.3 = (bf16[32,1024]{1,0:T(8,128)(2,1)S(1)}, bf16[32,1024]{1,0:T(8,128)(2,1)S(1)}, u32[]{:S(2)}, u32[]{:S(2)}) collective-permute-start(bf16[32,1024]{1,0:T(8,128)(2,1)S(1)} %pad_maximum_fusion.after_ref.held_ref), channel_id=1, source_target_pairs={{0,4},{1,5},{2,6},{3,7},{4,0},{5,1},{6,2},{7,3},{8,12},{9,13},{10,... | collective-permute-start | bytes 196616 | tf_op jit(solution)/shard_map/ppermute | solution.py:335

commit v9 on v8

--- a/solution.py
+++ b/solution.py
@@ -135,7 +135,6 @@
     plus = (cc - ss) * (cc - ss) + (cs + sc) * (cs + sc)
     minus = (cc + ss) * (cc + ss) + (cs - sc) * (cs - sc)
     grid = jnp.concatenate([plus, minus], axis=0).astype(bf16)
-    group = lax.broadcasted_iota(jnp.int32, (4 * SIDE * count, CHUNK), 0) // count
 
     for copy in copies[4:6]:
         copy.wait()
@@ -153,8 +152,12 @@
             lax.broadcasted_iota(jnp.int32, (POINTS, CHUNK), 0) == place
         ).astype(f32).astype(bf16)
         values = jnp.dot(grid[:, :POINTS], at_place, preferred_element_type=f32)
-        values = jnp.where(group == chosen, values, 0.0)
-        intensity = jnp.sum(values.reshape(-1, 8, CHUNK), axis=0)
+        fold = lax.broadcasted_iota(jnp.int32, (8, CHUNK), 0) // count
+        wanted = chosen - fold
+        intensity = jnp.zeros((8, CHUNK), f32)
+        for first in range(0, 4 * SIDE, 8 // count):
+            rows = slice(first * count, first * count + 8)
+            intensity = jnp.where(wanted == first, values[rows], intensity)
         shift = count
         while shift < 8:
             intensity = intensity + pltpu.roll(intensity, shift, axis=0)

time: 20.7 us -> 20.6 us (level)
  no operation moved by 1% of the time
where the time goes in v9:
time: 20.6 us; the launch traced here: 20.4 us
  Pallas kernels  11.2 us (54%)
  starting transfers between devices  7.74 us (38%)
  waiting for transfers between devices  1.35 us (7%)
    ppermute x4, starting transfers between devices, per_device(): lax.ppermute(held, ('db', 'cand'), [(i, i ^ mask) for i in range(members)])  7.74 us
    pallas_call x4, Pallas kernels, statistics(): pl.pallas_call(functools.partial(statistics_kernel, first), out_shape=[pl...  4.04 us
    pallas_call x1, Pallas kernels, candidate_patterns(): pl.pallas_call(candidate_kernel, out_shape=[pltpu.VMEM((count, nbins), jn...  3.86 us
    pallas_call x1, Pallas kernels, score(): pl.pallas_call(functools.partial(score_kernel, ncand, masks, len(means)),...  3.3 us
    ppermute x4, waiting for transfers between devices, per_device(): lax.ppermute(held, ('db', 'cand'), [(i, i ^ mask) for i in range(members)])  1.35 us
  transfers between devices with their start and end apart: 4, of which 4 were waited for; matrix products, arithmetic and copies ran while one was open for 0% of the time, Pallas kernels for 20%

profile of v9, /device:TPU:0, one launch (start us, length us, event | category | flops | bytes accessed | tf_op | source)
XLA Modules:
  0.0 20.4 jit_solution(15979836816976081189)
XLA Ops:
  0.0 3.9 %candidates.1 = (bf16[4,1024]{1,0:T(4,128)(2,1)S(1)}, bf16[4096,1024]{1,0:T(8,128)(2,1)S(1)}) custom-call(f32[3,4,64]{2,1,0:T(4,128)} %coords_hbm.1, s32[4,64]{1,0:T(4,128)} %species_hbm.1, s32[3,4096]{1,0:T(4,128)} %miller_hbm.1, s32[1,4096]{1,0:T(1,128)} %bitcast.3, f32[4,89]{1,0:T(4,128)} %bitcast.4, f32[4,89]{1,0:T(4,128)} %bitcast.5, ...), custom_call_target="tpu_custom_call" | custom-call | tf_op jit(solution)/shard_map/candidates/pallas_call | solution.py:218
  3.9 3.5 %collective-permute-start = (bf16[4,1024]{1,0:T(4,128)(2,1)S(1)}, bf16[4,1024]{1,0:T(4,128)(2,1)S(1)}, u32[]{:S(2)}, u32[]{:S(2)}) collective-permute-start(bf16[4,1024]{1,0:T(4,128)(2,1)S(1)} %get-tuple-element.23.after_ref), channel_id=1, source_target_pairs={{0,6},{1,7},{2,4},{3,5},{4,2},{5,3},{6,0},{7,1},{8,14},{9,15},{10,... | collective-permute-start | bytes 24584 | tf_op jit(solution)/shard_map/ppermute | solution.py:338
  7.4 1.2 %statistics.4 = (f32[1280,1]{1,0:T(8,128)S(1)}, f32[1280,1]{1,0:T(8,128)S(1)}, bf16[4096,1024]{1,0:T(8,128)(2,1)S(1)}) custom-call(bf16[4096,1024]{1,0:T(8,128)(2,1)S(1)} %get-tuple-element.24.refs_ref, bf16[4,1024]{1,0:T(4,128)(2,1)S(1)} %get-tuple-element.23.after_ref), custom_call_target="tpu_custom_call", output_to_operand_aliasing={{2}: (0, {})} | custom-call | flops 335544320 | bytes 2621440 | tf_op jit(solution)/shard_map/statistics/pallas_call | solution.py:259
  8.7 0.1 collective-permute-done
  8.8 1.9 %collective-permute-start.1 = (bf16[8,1024]{1,0:T(8,128)(2,1)S(1)}, bf16[8,1024]{1,0:T(8,128)(2,1)S(1)}, u32[]{:S(2)}, u32[]{:S(2)}) collective-permute-start(bf16[8,1024]{1,0:T(8,128)(2,1)S(1)} %pad_maximum_fusion.2.after_ref), channel_id=1, source_target_pairs={{0,5},{1,4},{2,7},{3,6},{4,1},{5,0},{6,3},{7,2},{8,13},{9,12},{10,... | collective-permute-start | bytes 49160 | tf_op jit(solution)/shard_map/ppermute | solution.py:338
  10.7 1.2 %statistics.5 = (f32[1280,1]{1,0:T(8,128)S(1)}, f32[1280,1]{1,0:T(8,128)S(1)}, bf16[4096,1024]{1,0:T(8,128)(2,1)S(1)}) custom-call(bf16[4096,1024]{1,0:T(8,128)(2,1)S(1)} %get-tuple-element.27.refs_ref, bf16[8,1024]{1,0:T(8,128)(2,1)S(1)} %pad_maximum_fusion.2.after_ref), custom_call_target="tpu_custom_call", output_to_operand_aliasing={{2}: (0, {})} | custom-call | flops 335544320 | bytes 2621440 | tf_op jit(solution)/shard_map/statistics/pallas_call | solution.py:259
  12.0 0.2 collective-permute-done.1
  12.2 1.7 %collective-permute-start.2 = (bf16[16,1024]{1,0:T(8,128)(2,1)S(1)}, bf16[16,1024]{1,0:T(8,128)(2,1)S(1)}, u32[]{:S(2)}, u32[]{:S(2)}) collective-permute-start(bf16[16,1024]{1,0:T(8,128)(2,1)S(1)} %pad_maximum_fusion.1.after_ref), channel_id=1, source_target_pairs={{0,12},{1,13},{2,14},{3,15},{4,8},{5,9},{6,10},{7,11},{8,4},{9,5},... | collective-permute-start | bytes 98312 | tf_op jit(solution)/shard_map/ppermute | solution.py:338
  13.9 1.2 %statistics.6 = (f32[1280,1]{1,0:T(8,128)S(1)}, f32[1280,1]{1,0:T(8,128)S(1)}, bf16[4096,1024]{1,0:T(8,128)(2,1)S(1)}) custom-call(bf16[4096,1024]{1,0:T(8,128)(2,1)S(1)} %get-tuple-element.30.refs_ref, bf16[16,1024]{1,0:T(8,128)(2,1)S(1)} %pad_maximum_fusion.1.after_ref), custom_call_target="tpu_custom_call", output_to_operand_aliasing={{2}: (0, {})} | custom-call | flops 335544320 | bytes 2621440 | tf_op jit(solution)/shard_map/statistics/pallas_call | solution.py:259
  15.2 0.4 %collective-permute-done.2 = bf16[16,1024]{1,0:T(8,128)(2,1)S(1)} collective-permute-done((bf16[16,1024]{1,0:T(8,128)(2,1)S(1)}, bf16[16,1024]{1,0:T(8,128)(2,1)S(1)}, u32[]{:S(2)}, u32[]{:S(2)}) %collective-permute-start.2) | collective-permute-done | bytes 32800 | tf_op jit(solution)/shard_map/ppermute | solution.py:338
  15.6 0.6 %collective-permute-start.3 = (bf16[32,1024]{1,0:T(8,128)(2,1)S(1)}, bf16[32,1024]{1,0:T(8,128)(2,1)S(1)}, u32[]{:S(2)}, u32[]{:S(2)}) collective-permute-start(bf16[32,1024]{1,0:T(8,128)(2,1)S(1)} %pad_maximum_fusion.after_ref.held_ref), channel_id=1, source_target_pairs={{0,4},{1,5},{2,6},{3,7},{4,0},{5,1},{6,2},{7,3},{8,12},{9,13},{10,... | collective-permute-start | bytes 196616 | tf_op jit(solution)/shard_map/ppermute | solution.py:338
  16.2 0.3 %statistics.7 = (f32[256,1]{1,0:T(8,128)S(1)}, f32[256,1]{1,0:T(8,128)S(1)}, bf16[4096,1024]{1,0:T(8,128)(2,1)S(1)}) custom-call(bf16[4096,1024]{1,0:T(8,128)(2,1)S(1)} %get-tuple-element.33.refs_ref, bf16[32,1024]{1,0:T(8,128)(2,1)S(1)} %pad_maximum_fusion.after_ref.held_ref), custom_call_target="tpu_custom_call", output_to_operand_aliasing={{2}: (0, {})} | custom-call | flops 67108864 | bytes 524288 | tf_op jit(solution)/shard_map/statistics/pallas_call | solution.py:259
  16.5 0.6 %collective-permute-done.3.other_ref = bf16[32,1024]{1,0:T(8,128)(2,1)S(1)} collective-permute-done((bf16[32,1024]{1,0:T(8,128)(2,1)S(1)}, bf16[32,1024]{1,0:T(8,128)(2,1)S(1)}, u32[]{:S(2)}, u32[]{:S(2)}) %collective-permute-start.3) | collective-permute-done | bytes 65568 | tf_op jit(solution)/shard_map/ppermute | solution.py:338
  17.1 3.3 %scores.1 = bf16[64,4096]{1,0:T(8,128)(2,1)} custom-call(bf16[32,1024]{1,0:T(8,128)(2,1)S(1)} %pad_maximum_fusion.after_ref.held_ref, bf16[32,1024]{1,0:T(8,128)(2,1)S(1)} %collective-permute-done.3.other_ref, bf16[4096,1024]{1,0:T(8,128)(2,1)S(1)} %get-tuple-element.36.refs_ref, f32[1280,1]{1,0:T(8,128)S(1)} %get-tuple-element.25.rest_0_, ...), custom_call_target="tpu_custom_call" | custom-call | tf_op jit(solution)/shard_map/scores/pallas_call | solution.py:310
  (3 shorter events, 0.1 us)
Async XLA Ops:
  3.9 4.9 %collective-permute-start = (bf16[4,1024]{1,0:T(4,128)(2,1)S(1)}, bf16[4,1024]{1,0:T(4,128)(2,1)S(1)}, u32[]{:S(2)}, u32[]{:S(2)}) collective-permute-start(bf16[4,1024]{1,0:T(4,128)(2,1)S(1)} %get-tuple-element.23.after_ref), channel_id=1, source_target_pairs={{0,6},{1,7},{2,4},{3,5},{4,2},{5,3},{6,0},{7,1},{8,14},{9,15},{10,... | collective-permute-start | bytes 24584 | tf_op jit(solution)/shard_map/ppermute | solution.py:338
  8.8 3.4 %collective-permute-start.1 = (bf16[8,1024]{1,0:T(8,128)(2,1)S(1)}, bf16[8,1024]{1,0:T(8,128)(2,1)S(1)}, u32[]{:S(2)}, u32[]{:S(2)}) collective-permute-start(bf16[8,1024]{1,0:T(8,128)(2,1)S(1)} %pad_maximum_fusion.2.after_ref), channel_id=1, source_target_pairs={{0,5},{1,4},{2,7},{3,6},{4,1},{5,0},{6,3},{7,2},{8,13},{9,12},{10,... | collective-permute-start | bytes 49160 | tf_op jit(solution)/shard_map/ppermute | solution.py:338
  12.2 3.4 %collective-permute-start.2 = (bf16[16,1024]{1,0:T(8,128)(2,1)S(1)}, bf16[16,1024]{1,0:T(8,128)(2,1)S(1)}, u32[]{:S(2)}, u32[]{:S(2)}) collective-permute-start(bf16[16,1024]{1,0:T(8,128)(2,1)S(1)} %pad_maximum_fusion.1.after_ref), channel_id=1, source_target_pairs={{0,12},{1,13},{2,14},{3,15},{4,8},{5,9},{6,10},{7,11},{8,4},{9,5},... | collective-permute-start | bytes 98312 | tf_op jit(solution)/shard_map/ppermute | solution.py:338
  15.6 1.5 %collective-permute-start.3 = (bf16[32,1024]{1,0:T(8,128)(2,1)S(1)}, bf16[32,1024]{1,0:T(8,128)(2,1)S(1)}, u32[]{:S(2)}, u32[]{:S(2)}) collective-permute-start(bf16[32,1024]{1,0:T(8,128)(2,1)S(1)} %pad_maximum_fusion.after_ref.held_ref), channel_id=1, source_target_pairs={{0,4},{1,5},{2,6},{3,7},{4,0},{5,1},{6,2},{7,3},{8,12},{9,13},{10,... | collective-permute-start | bytes 196616 | tf_op jit(solution)/shard_map/ppermute | solution.py:338

commit v10 on v9

--- a/solution.py
+++ b/solution.py
@@ -334,9 +334,11 @@
     share = -(-count * 5 // 16 // STAT_UNIT) * STAT_UNIT
     means, scales = [], []
     first = 0
-    for mask in masks:
+    for stage, mask in enumerate(masks):
         other = lax.ppermute(held, ("db", "cand"), [(i, i ^ mask) for i in range(members)])
         rows = min(share, count - first)
+        if stage == len(masks) - 2:
+            rows = count - first
         if rows > 0:
             mean, scale, refs = statistics(refs, first, rows, held)
             means.append(mean)

time: 20.6 us -> 20.6 us (level)
    pallas_call x4 -> x3, Pallas kernels: 4.04 us -> 3.97 us  [statistics(): pl.pallas_call(functools.partial(statistics_kernel, first), out_shape=[pl...]
  transfers between devices with their start and end apart: 4 -> 4, of which waited for: 4 -> 4; matrix products, arithmetic and copies ran while one was open for 0% -> 0% of each run, Pallas kernels for 20% -> 19%
where the time goes in v10:
time: 20.6 us; the launch traced here: 20.4 us
  Pallas kernels  11.1 us (54%)
  starting transfers between devices  7.74 us (38%)
  waiting for transfers between devices  1.43 us (7%)
    ppermute x4, starting transfers between devices, per_device(): lax.ppermute(held, ('db', 'cand'), [(i, i ^ mask) for i in range(members)])  7.74 us
    pallas_call x3, Pallas kernels, statistics(): pl.pallas_call(functools.partial(statistics_kernel, first), out_shape=[pl...  3.97 us
    pallas_call x1, Pallas kernels, candidate_patterns(): pl.pallas_call(candidate_kernel, out_shape=[pltpu.VMEM((count, nbins), jn...  3.86 us
    pallas_call x1, Pallas kernels, score(): pl.pallas_call(functools.partial(score_kernel, ncand, masks, len(means)),...  3.3 us
    ppermute x4, waiting for transfers between devices, per_device(): lax.ppermute(held, ('db', 'cand'), [(i, i ^ mask) for i in range(members)])  1.43 us
  transfers between devices with their start and end apart: 4, of which 4 were waited for; matrix products, arithmetic and copies ran while one was open for 0% of the time, Pallas kernels for 19%

profile of v10, /device:TPU:0, one launch (start us, length us, event | category | flops | bytes accessed | tf_op | source)
XLA Modules:
  0.0 20.4 jit_solution(1903672328426453689)
XLA Ops:
  0.0 3.9 %candidates.1 = (bf16[4,1024]{1,0:T(4,128)(2,1)S(1)}, bf16[4096,1024]{1,0:T(8,128)(2,1)S(1)}) custom-call(f32[3,4,64]{2,1,0:T(4,128)} %coords_hbm.1, s32[4,64]{1,0:T(4,128)} %species_hbm.1, s32[3,4096]{1,0:T(4,128)} %miller_hbm.1, s32[1,4096]{1,0:T(1,128)} %bitcast.3, f32[4,89]{1,0:T(4,128)} %bitcast.4, f32[4,89]{1,0:T(4,128)} %bitcast.5, ...), custom_call_target="tpu_custom_call" | custom-call | tf_op jit(solution)/shard_map/candidates/pallas_call | solution.py:218
  3.9 3.5 %collective-permute-start = (bf16[4,1024]{1,0:T(4,128)(2,1)S(1)}, bf16[4,1024]{1,0:T(4,128)(2,1)S(1)}, u32[]{:S(2)}, u32[]{:S(2)}) collective-permute-start(bf16[4,1024]{1,0:T(4,128)(2,1)S(1)} %get-tuple-element.19.after_ref), channel_id=1, source_target_pairs={{0,6},{1,7},{2,4},{3,5},{4,2},{5,3},{6,0},{7,1},{8,14},{9,15},{10,... | collective-permute-start | bytes 24584 | tf_op jit(solution)/shard_map/ppermute | solution.py:338
  7.4 1.2 %statistics.3 = (f32[1280,1]{1,0:T(8,128)S(1)}, f32[1280,1]{1,0:T(8,128)S(1)}, bf16[4096,1024]{1,0:T(8,128)(2,1)S(1)}) custom-call(bf16[4096,1024]{1,0:T(8,128)(2,1)S(1)} %get-tuple-element.20.refs_ref, bf16[4,1024]{1,0:T(4,128)(2,1)S(1)} %get-tuple-element.19.after_ref), custom_call_target="tpu_custom_call", output_to_operand_aliasing={{2}: (0, {})} | custom-call | flops 335544320 | bytes 2621440 | tf_op jit(solution)/shard_map/statistics/pallas_call | solution.py:259
  8.7 0.1 collective-permute-done
  8.8 1.9 %collective-permute-start.1 = (bf16[8,1024]{1,0:T(8,128)(2,1)S(1)}, bf16[8,1024]{1,0:T(8,128)(2,1)S(1)}, u32[]{:S(2)}, u32[]{:S(2)}) collective-permute-start(bf16[8,1024]{1,0:T(8,128)(2,1)S(1)} %pad_maximum_fusion.2.after_ref), channel_id=1, source_target_pairs={{0,5},{1,4},{2,7},{3,6},{4,1},{5,0},{6,3},{7,2},{8,13},{9,12},{10,... | collective-permute-start | bytes 49160 | tf_op jit(solution)/shard_map/ppermute | solution.py:338
  10.7 1.2 %statistics.4 = (f32[1280,1]{1,0:T(8,128)S(1)}, f32[1280,1]{1,0:T(8,128)S(1)}, bf16[4096,1024]{1,0:T(8,128)(2,1)S(1)}) custom-call(bf16[4096,1024]{1,0:T(8,128)(2,1)S(1)} %get-tuple-element.23.refs_ref, bf16[8,1024]{1,0:T(8,128)(2,1)S(1)} %pad_maximum_fusion.2.after_ref), custom_call_target="tpu_custom_call", output_to_operand_aliasing={{2}: (0, {})} | custom-call | flops 335544320 | bytes 2621440 | tf_op jit(solution)/shard_map/statistics/pallas_call | solution.py:259
  12.0 0.2 collective-permute-done.1
  12.2 1.7 %collective-permute-start.2 = (bf16[16,1024]{1,0:T(8,128)(2,1)S(1)}, bf16[16,1024]{1,0:T(8,128)(2,1)S(1)}, u32[]{:S(2)}, u32[]{:S(2)}) collective-permute-start(bf16[16,1024]{1,0:T(8,128)(2,1)S(1)} %pad_maximum_fusion.1.after_ref), channel_id=1, source_target_pairs={{0,12},{1,13},{2,14},{3,15},{4,8},{5,9},{6,10},{7,11},{8,4},{9,5},... | collective-permute-start | bytes 98312 | tf_op jit(solution)/shard_map/ppermute | solution.py:338
  13.9 1.5 %statistics.5 = (f32[1536,1]{1,0:T(8,128)S(1)}, f32[1536,1]{1,0:T(8,128)S(1)}, bf16[4096,1024]{1,0:T(8,128)(2,1)S(1)}) custom-call(bf16[4096,1024]{1,0:T(8,128)(2,1)S(1)} %get-tuple-element.26.refs_ref, bf16[16,1024]{1,0:T(8,128)(2,1)S(1)} %pad_maximum_fusion.1.after_ref), custom_call_target="tpu_custom_call", output_to_operand_aliasing={{2}: (0, {})} | custom-call | flops 402653184 | bytes 3145728 | tf_op jit(solution)/shard_map/statistics/pallas_call | solution.py:259
  15.4 0.2 %collective-permute-done.2 = bf16[16,1024]{1,0:T(8,128)(2,1)S(1)} collective-permute-done((bf16[16,1024]{1,0:T(8,128)(2,1)S(1)}, bf16[16,1024]{1,0:T(8,128)(2,1)S(1)}, u32[]{:S(2)}, u32[]{:S(2)}) %collective-permute-start.2) | collective-permute-done | bytes 32800 | tf_op jit(solution)/shard_map/ppermute | solution.py:338
  15.6 0.6 %collective-permute-start.3 = (bf16[32,1024]{1,0:T(8,128)(2,1)S(1)}, bf16[32,1024]{1,0:T(8,128)(2,1)S(1)}, u32[]{:S(2)}, u32[]{:S(2)}) collective-permute-start(bf16[32,1024]{1,0:T(8,128)(2,1)S(1)} %pad_maximum_fusion.held_ref), channel_id=1, source_target_pairs={{0,4},{1,5},{2,6},{3,7},{4,0},{5,1},{6,2},{7,3},{8,12},{9,13},{10,... | collective-permute-start | bytes 196616 | tf_op jit(solution)/shard_map/ppermute | solution.py:338
  16.2 0.9 %collective-permute-done.3.other_ref = bf16[32,1024]{1,0:T(8,128)(2,1)S(1)} collective-permute-done((bf16[32,1024]{1,0:T(8,128)(2,1)S(1)}, bf16[32,1024]{1,0:T(8,128)(2,1)S(1)}, u32[]{:S(2)}, u32[]{:S(2)}) %collective-permute-start.3) | collective-permute-done | bytes 65568 | tf_op jit(solution)/shard_map/ppermute | solution.py:338
  17.1 3.3 %scores.1 = bf16[64,4096]{1,0:T(8,128)(2,1)} custom-call(bf16[32,1024]{1,0:T(8,128)(2,1)S(1)} %pad_maximum_fusion.held_ref, bf16[32,1024]{1,0:T(8,128)(2,1)S(1)} %collective-permute-done.3.other_ref, bf16[4096,1024]{1,0:T(8,128)(2,1)S(1)} %get-tuple-element.29.refs_ref, f32[1280,1]{1,0:T(8,128)S(1)} %get-tuple-element.21.rest_0_, ...), custom_call_target="tpu_custom_call" | custom-call | tf_op jit(solution)/shard_map/scores/pallas_call | solution.py:310
  (3 shorter events, 0.1 us)
Async XLA Ops:
  3.9 4.9 %collective-permute-start = (bf16[4,1024]{1,0:T(4,128)(2,1)S(1)}, bf16[4,1024]{1,0:T(4,128)(2,1)S(1)}, u32[]{:S(2)}, u32[]{:S(2)}) collective-permute-start(bf16[4,1024]{1,0:T(4,128)(2,1)S(1)} %get-tuple-element.19.after_ref), channel_id=1, source_target_pairs={{0,6},{1,7},{2,4},{3,5},{4,2},{5,3},{6,0},{7,1},{8,14},{9,15},{10,... | collective-permute-start | bytes 24584 | tf_op jit(solution)/shard_map/ppermute | solution.py:338
  8.8 3.4 %collective-permute-start.1 = (bf16[8,1024]{1,0:T(8,128)(2,1)S(1)}, bf16[8,1024]{1,0:T(8,128)(2,1)S(1)}, u32[]{:S(2)}, u32[]{:S(2)}) collective-permute-start(bf16[8,1024]{1,0:T(8,128)(2,1)S(1)} %pad_maximum_fusion.2.after_ref), channel_id=1, source_target_pairs={{0,5},{1,4},{2,7},{3,6},{4,1},{5,0},{6,3},{7,2},{8,13},{9,12},{10,... | collective-permute-start | bytes 49160 | tf_op jit(solution)/shard_map/ppermute | solution.py:338
  12.2 3.4 %collective-permute-start.2 = (bf16[16,1024]{1,0:T(8,128)(2,1)S(1)}, bf16[16,1024]{1,0:T(8,128)(2,1)S(1)}, u32[]{:S(2)}, u32[]{:S(2)}) collective-permute-start(bf16[16,1024]{1,0:T(8,128)(2,1)S(1)} %pad_maximum_fusion.1.after_ref), channel_id=1, source_target_pairs={{0,12},{1,13},{2,14},{3,15},{4,8},{5,9},{6,10},{7,11},{8,4},{9,5},... | collective-permute-start | bytes 98312 | tf_op jit(solution)/shard_map/ppermute | solution.py:338
  15.6 1.5 %collective-permute-start.3 = (bf16[32,1024]{1,0:T(8,128)(2,1)S(1)}, bf16[32,1024]{1,0:T(8,128)(2,1)S(1)}, u32[]{:S(2)}, u32[]{:S(2)}) collective-permute-start(bf16[32,1024]{1,0:T(8,128)(2,1)S(1)} %pad_maximum_fusion.held_ref), channel_id=1, source_target_pairs={{0,4},{1,5},{2,6},{3,7},{4,0},{5,1},{6,2},{7,3},{8,12},{9,13},{10,... | collective-permute-start | bytes 196616 | tf_op jit(solution)/shard_map/ppermute | solution.py:338

commit v11 on v10

--- a/solution.py
+++ b/solution.py
@@ -14,7 +14,7 @@
 SIDE = 9
 POINTS = 96
 NORMS = 208
-CHUNK = 4096
+CHUNK = 2048
 SCORE_ROWS = 512
 STAT_UNIT = 256
 STAT_STEP = 256

time: 20.6 us -> 20.6 us (level)
  no operation moved by 1% of the time
where the time goes in v11:
time: 20.6 us; the launch traced here: 20.4 us
  Pallas kernels  11.2 us (54%)
  starting transfers between devices  7.74 us (38%)
  waiting for transfers between devices  1.43 us (7%)
    ppermute x4, starting transfers between devices, per_device(): lax.ppermute(held, ('db', 'cand'), [(i, i ^ mask) for i in range(members)])  7.74 us
    pallas_call x3, Pallas kernels, statistics(): pl.pallas_call(functools.partial(statistics_kernel, first), out_shape=[pl...  3.97 us
    pallas_call x1, Pallas kernels, candidate_patterns(): pl.pallas_call(candidate_kernel, out_shape=[pltpu.VMEM((count, nbins), jn...  3.9 us
    pallas_call x1, Pallas kernels, score(): pl.pallas_call(functools.partial(score_kernel, ncand, masks, len(means)),...  3.3 us
    ppermute x4, waiting for transfers between devices, per_device(): lax.ppermute(held, ('db', 'cand'), [(i, i ^ mask) for i in range(members)])  1.43 us
  transfers between devices with their start and end apart: 4, of which 4 were waited for; matrix products, arithmetic and copies ran while one was open for 0% of the time, Pallas kernels for 19%

profile of v11, /device:TPU:0, one launch (start us, length us, event | category | flops | bytes accessed | tf_op | source)
XLA Modules:
  0.0 20.4 jit_solution(4340242382483028246)
XLA Ops:
  0.0 3.9 %candidates.1 = (bf16[4,1024]{1,0:T(4,128)(2,1)S(1)}, bf16[4096,1024]{1,0:T(8,128)(2,1)S(1)}) custom-call(f32[3,4,64]{2,1,0:T(4,128)} %coords_hbm.1, s32[4,64]{1,0:T(4,128)} %species_hbm.1, s32[3,4096]{1,0:T(4,128)} %miller_hbm.1, s32[1,4096]{1,0:T(1,128)} %bitcast.3, f32[4,89]{1,0:T(4,128)} %bitcast.4, f32[4,89]{1,0:T(4,128)} %bitcast.5, ...), custom_call_target="tpu_custom_call" | custom-call | tf_op jit(solution)/shard_map/candidates/pallas_call | solution.py:218
  3.9 3.5 %collective-permute-start = (bf16[4,1024]{1,0:T(4,128)(2,1)S(1)}, bf16[4,1024]{1,0:T(4,128)(2,1)S(1)}, u32[]{:S(2)}, u32[]{:S(2)}) collective-permute-start(bf16[4,1024]{1,0:T(4,128)(2,1)S(1)} %get-tuple-element.19.after_ref), channel_id=1, source_target_pairs={{0,6},{1,7},{2,4},{3,5},{4,2},{5,3},{6,0},{7,1},{8,14},{9,15},{10,... | collective-permute-start | bytes 24584 | tf_op jit(solution)/shard_map/ppermute | solution.py:338
  7.4 1.2 %statistics.3 = (f32[1280,1]{1,0:T(8,128)S(1)}, f32[1280,1]{1,0:T(8,128)S(1)}, bf16[4096,1024]{1,0:T(8,128)(2,1)S(1)}) custom-call(bf16[4096,1024]{1,0:T(8,128)(2,1)S(1)} %get-tuple-element.20.refs_ref, bf16[4,1024]{1,0:T(4,128)(2,1)S(1)} %get-tuple-element.19.after_ref), custom_call_target="tpu_custom_call", output_to_operand_aliasing={{2}: (0, {})} | custom-call | flops 335544320 | bytes 2621440 | tf_op jit(solution)/shard_map/statistics/pallas_call | solution.py:259
  8.7 0.1 collective-permute-done
  8.8 1.9 %collective-permute-start.1 = (bf16[8,1024]{1,0:T(8,128)(2,1)S(1)}, bf16[8,1024]{1,0:T(8,128)(2,1)S(1)}, u32[]{:S(2)}, u32[]{:S(2)}) collective-permute-start(bf16[8,1024]{1,0:T(8,128)(2,1)S(1)} %pad_maximum_fusion.2.after_ref), channel_id=1, source_target_pairs={{0,5},{1,4},{2,7},{3,6},{4,1},{5,0},{6,3},{7,2},{8,13},{9,12},{10,... | collective-permute-start | bytes 49160 | tf_op jit(solution)/shard_map/ppermute | solution.py:338
  10.8 1.2 %statistics.4 = (f32[1280,1]{1,0:T(8,128)S(1)}, f32[1280,1]{1,0:T(8,128)S(1)}, bf16[4096,1024]{1,0:T(8,128)(2,1)S(1)}) custom-call(bf16[4096,1024]{1,0:T(8,128)(2,1)S(1)} %get-tuple-element.23.refs_ref, bf16[8,1024]{1,0:T(8,128)(2,1)S(1)} %pad_maximum_fusion.2.after_ref), custom_call_target="tpu_custom_call", output_to_operand_aliasing={{2}: (0, {})} | custom-call | flops 335544320 | bytes 2621440 | tf_op jit(solution)/shard_map/statistics/pallas_call | solution.py:259
  12.0 0.2 collective-permute-done.1
  12.2 1.7 %collective-permute-start.2 = (bf16[16,1024]{1,0:T(8,128)(2,1)S(1)}, bf16[16,1024]{1,0:T(8,128)(2,1)S(1)}, u32[]{:S(2)}, u32[]{:S(2)}) collective-permute-start(bf16[16,1024]{1,0:T(8,128)(2,1)S(1)} %pad_maximum_fusion.1.after_ref), channel_id=1, source_target_pairs={{0,12},{1,13},{2,14},{3,15},{4,8},{5,9},{6,10},{7,11},{8,4},{9,5},... | collective-permute-start | bytes 98312 | tf_op jit(solution)/shard_map/ppermute | solution.py:338
  13.9 1.5 %statistics.5 = (f32[1536,1]{1,0:T(8,128)S(1)}, f32[1536,1]{1,0:T(8,128)S(1)}, bf16[4096,1024]{1,0:T(8,128)(2,1)S(1)}) custom-call(bf16[4096,1024]{1,0:T(8,128)(2,1)S(1)} %get-tuple-element.26.refs_ref, bf16[16,1024]{1,0:T(8,128)(2,1)S(1)} %pad_maximum_fusion.1.after_ref), custom_call_target="tpu_custom_call", output_to_operand_aliasing={{2}: (0, {})} | custom-call | flops 402653184 | bytes 3145728 | tf_op jit(solution)/shard_map/statistics/pallas_call | solution.py:259
  15.4 0.2 %collective-permute-done.2 = bf16[16,1024]{1,0:T(8,128)(2,1)S(1)} collective-permute-done((bf16[16,1024]{1,0:T(8,128)(2,1)S(1)}, bf16[16,1024]{1,0:T(8,128)(2,1)S(1)}, u32[]{:S(2)}, u32[]{:S(2)}) %collective-permute-start.2) | collective-permute-done | bytes 32800 | tf_op jit(solution)/shard_map/ppermute | solution.py:338
  15.7 0.6 %collective-permute-start.3 = (bf16[32,1024]{1,0:T(8,128)(2,1)S(1)}, bf16[32,1024]{1,0:T(8,128)(2,1)S(1)}, u32[]{:S(2)}, u32[]{:S(2)}) collective-permute-start(bf16[32,1024]{1,0:T(8,128)(2,1)S(1)} %pad_maximum_fusion.held_ref), channel_id=1, source_target_pairs={{0,4},{1,5},{2,6},{3,7},{4,0},{5,1},{6,2},{7,3},{8,12},{9,13},{10,... | collective-permute-start | bytes 196616 | tf_op jit(solution)/shard_map/ppermute | solution.py:338
  16.2 0.9 %collective-permute-done.3.other_ref = bf16[32,1024]{1,0:T(8,128)(2,1)S(1)} collective-permute-done((bf16[32,1024]{1,0:T(8,128)(2,1)S(1)}, bf16[32,1024]{1,0:T(8,128)(2,1)S(1)}, u32[]{:S(2)}, u32[]{:S(2)}) %collective-permute-start.3) | collective-permute-done | bytes 65568 | tf_op jit(solution)/shard_map/ppermute | solution.py:338
  17.1 3.3 %scores.1 = bf16[64,4096]{1,0:T(8,128)(2,1)} custom-call(bf16[32,1024]{1,0:T(8,128)(2,1)S(1)} %pad_maximum_fusion.held_ref, bf16[32,1024]{1,0:T(8,128)(2,1)S(1)} %collective-permute-done.3.other_ref, bf16[4096,1024]{1,0:T(8,128)(2,1)S(1)} %get-tuple-element.29.refs_ref, f32[1280,1]{1,0:T(8,128)S(1)} %get-tuple-element.21.rest_0_, ...), custom_call_target="tpu_custom_call" | custom-call | tf_op jit(solution)/shard_map/scores/pallas_call | solution.py:310
  (3 shorter events, 0.1 us)
Async XLA Ops:
  3.9 4.9 %collective-permute-start = (bf16[4,1024]{1,0:T(4,128)(2,1)S(1)}, bf16[4,1024]{1,0:T(4,128)(2,1)S(1)}, u32[]{:S(2)}, u32[]{:S(2)}) collective-permute-start(bf16[4,1024]{1,0:T(4,128)(2,1)S(1)} %get-tuple-element.19.after_ref), channel_id=1, source_target_pairs={{0,6},{1,7},{2,4},{3,5},{4,2},{5,3},{6,0},{7,1},{8,14},{9,15},{10,... | collective-permute-start | bytes 24584 | tf_op jit(solution)/shard_map/ppermute | solution.py:338
  8.8 3.4 %collective-permute-start.1 = (bf16[8,1024]{1,0:T(8,128)(2,1)S(1)}, bf16[8,1024]{1,0:T(8,128)(2,1)S(1)}, u32[]{:S(2)}, u32[]{:S(2)}) collective-permute-start(bf16[8,1024]{1,0:T(8,128)(2,1)S(1)} %pad_maximum_fusion.2.after_ref), channel_id=1, source_target_pairs={{0,5},{1,4},{2,7},{3,6},{4,1},{5,0},{6,3},{7,2},{8,13},{9,12},{10,... | collective-permute-start | bytes 49160 | tf_op jit(solution)/shard_map/ppermute | solution.py:338
  12.2 3.4 %collective-permute-start.2 = (bf16[16,1024]{1,0:T(8,128)(2,1)S(1)}, bf16[16,1024]{1,0:T(8,128)(2,1)S(1)}, u32[]{:S(2)}, u32[]{:S(2)}) collective-permute-start(bf16[16,1024]{1,0:T(8,128)(2,1)S(1)} %pad_maximum_fusion.1.after_ref), channel_id=1, source_target_pairs={{0,12},{1,13},{2,14},{3,15},{4,8},{5,9},{6,10},{7,11},{8,4},{9,5},... | collective-permute-start | bytes 98312 | tf_op jit(solution)/shard_map/ppermute | solution.py:338
  15.7 1.5 %collective-permute-start.3 = (bf16[32,1024]{1,0:T(8,128)(2,1)S(1)}, bf16[32,1024]{1,0:T(8,128)(2,1)S(1)}, u32[]{:S(2)}, u32[]{:S(2)}) collective-permute-start(bf16[32,1024]{1,0:T(8,128)(2,1)S(1)} %pad_maximum_fusion.held_ref), channel_id=1, source_target_pairs={{0,4},{1,5},{2,6},{3,7},{4,0},{5,1},{6,2},{7,3},{8,12},{9,13},{10,... | collective-permute-start | bytes 196616 | tf_op jit(solution)/shard_map/ppermute | solution.py:338
